TPU v7x, 32 devices: a whole 2x2x4 slice. The times are simulated.
32 devices in a mesh: dp: 4 (over z), row: 2 (over core), col: 4 (over y, x).
Axes of the slice: x: 2, y: 2, z: 4, core: 2. Of those that a mesh axis runs over, the one named last changes fastest.
Arguments:
- tokens: float32 [1024, 1024], P(('dp', 'row'), 'col'), may hold values from -6 to 6
- segment_ids: int32 [1024], P('dp'), may hold values from 0 to 1023, as said below
- norm_gain: float32 [1024], P('col'), may hold values from 0.5 to 1.5
- in_weight: bfloat16 [1024, 3, 1024], P('col', None, 'row'), may hold values from -0.1875 to 0.1875
- conv_taps: float32 [3, 1024], P(None, ('row', 'col')), may hold values from -3 to 3
- out_weight: bfloat16 [1024, 1024], P('row', 'col'), may hold values from -0.1875 to 0.1875
- ffn_gain: float32 [1024], P('col'), may hold values from 0.5 to 1.5
- gate_weight: bfloat16 [1024, 4608], P('col', 'row'), may hold values from -0.1875 to 0.1875
- up_weight: bfloat16 [1024, 4608], P('col', 'row'), may hold values from -0.1875 to 0.1875
- down_weight: bfloat16 [4608, 1024], P('row', 'col'), may hold values from -0.09375 to 0.09375
- out_grad: float32 [1024, 1024], P(('dp', 'row'), 'col'), may hold values from -6 to 6
Outputs:
- block_out: float32 [1024, 1024], P(('dp', 'row'), 'col')
- in_grad: float32 [1024, 1024], P(('dp', 'row'), 'col')
- grad_norm_gain: float32 [1024], P('col')
- grad_in_weight: float32 [1024, 3, 1024], P('col', None, 'row')
- grad_conv_taps: float32 [3, 1024], P(None, ('row', 'col'))
- grad_out_weight: float32 [1024, 1024], P('row', 'col')
- grad_ffn_gain: float32 [1024], P('col')
- grad_gate_weight: float32 [1024, 4608], P('col', 'row')
- grad_up_weight: float32 [1024, 4608], P('col', 'row')
- grad_down_weight: float32 [4608, 1024], P('row', 'col')
Inputs may be any that keep to these rules, and one draw needn't show every extreme that they name: `segment_ids`: ids never fall along the tokens; every aligned sequence of 256 consecutive tokens starts a new id and changes id again at least once inside; runs of one id have 200 to 2000 tokens except where a sequence's start or end cuts them; the last token's id is 1023.
All inputs are finite; a program needn't handle non-finite values.
Results may differ from a plain program's by a relative error of at most 0.0094.
Values may be sent and summed in bfloat16 or wider, within the bound.
No kernel may reach another device: no remote copies, remote signals or barrier semaphores. Data moves between devices by JAX's collectives and lax.ppermute only.
A program may use at most 128 MiB of HBM per device.

v0:
```python
import jax
import jax.numpy as jnp
from jax import lax
from jax.experimental import pallas as pl
from jax.experimental.pallas import tpu as pltpu
from jax.sharding import PartitionSpec as P


epsilon = 1e-05
f32 = jnp.float32
bf16 = jnp.bfloat16


SMEM = pl.BlockSpec(memory_space=pltpu.SMEM)
VMEM = pl.BlockSpec(memory_space=pltpu.VMEM)


def dot(left, right, ldim, rdim):
    return lax.dot_general(left, right, (((ldim,), (rdim,)), ((), ())), preferred_element_type=f32)


def call(body, info, args, outs, scratch=(), flops=10**8):
    size = sum(a.size * a.dtype.itemsize for a in args)
    return pl.pallas_call(
        body,
        out_shape=[jax.ShapeDtypeStruct(s, t) for s, t in outs],
        in_specs=[SMEM] + [VMEM] * len(args),
        out_specs=[VMEM] * len(outs),
        scratch_shapes=list(scratch),
        compiler_params=pltpu.CompilerParams(vmem_limit_bytes=56 * 1024 * 1024),
        cost_estimate=pl.CostEstimate(flops=flops, bytes_accessed=size, transcendentals=0),
    )(info, *args)


def peers():
    n = lax.axis_size("col")
    assert n & (n - 1) == 0
    return range(1, n)


def col_send(piece, k):
    n = lax.axis_size("col")
    return lax.ppermute(piece, "col", [(i, i ^ k) for i in range(n)])


def row_send(piece):
    n = lax.axis_size("row")
    assert n == 2
    return lax.ppermute(piece, "row", [(i, (i + 1) % n) for i in range(n)])


def pair_send(piece):
    n = lax.axis_size("dp")
    assert n % 2 == 0
    return lax.ppermute(piece, "dp", [(i, i ^ 1) for i in range(n)])


def add_to(held, came, kind):
    return (held.astype(f32) + came.astype(f32)).astype(kind)


def line_sum(part):
    n = lax.axis_size("dp")
    me = lax.axis_index("dp")
    half = n // 2
    kind = part.dtype
    held = part
    for s in range(half - 1):
        came = lax.ppermute(held, "dp", [(s, s + 1), (n - 1 - s, n - 2 - s)])
        held = add_to(held, came, kind)
    came = lax.ppermute(held, "dp", [(half - 1, half), (half, half - 1)])
    held = add_to(held, came, kind)
    came = held
    for s in range(half - 1):
        came = lax.ppermute(held, "dp", [(half - 1 - s, half - 2 - s), (half + s, half + 1 + s)])
        if s < half - 2:
            got = (me == half - 2 - s) | (me == half + 1 + s)
            held = jnp.where(got, came, held)
    return held, came


def far_end():
    n = lax.axis_size("dp")
    me = lax.axis_index("dp")
    return (((me == 0) | (me == n - 1)) & (n > 2)).astype(jnp.int32)


def masks(seg, r, rows, group):
    wide = jnp.broadcast_to(seg, (group, 128))
    wide = jnp.where(r == 0, wide, pltpu.roll(wide, rows, 0))
    place = lax.broadcasted_iota(jnp.int32, (group, 128), 0) + r * rows
    place = jnp.where(place >= group, place - group, place)
    one = jnp.where((wide == pltpu.roll(wide, 1, 0)) & (place >= 1), 1.0, 0.0)
    two = jnp.where((wide == pltpu.roll(wide, 2, 0)) & (place >= 2), 1.0, 0.0)
    return one, two


def per_device(
    tokens,
    segment_ids,
    norm_gain,
    in_weight,
    conv_taps,
    out_weight,
    ffn_gain,
    gate_weight,
    up_weight,
    down_weight,
    out_grad,
):
    rows, width = tokens.shape
    n_col = lax.axis_size("col")
    n_row = lax.axis_size("row")
    c = lax.axis_index("col")
    r = lax.axis_index("row")
    model = width * n_col
    group = rows * n_row
    span = in_weight.shape[2]
    lanes = span // n_col
    hidden_ff = gate_weight.shape[1]
    ff = hidden_ff // n_col
    K = range(n_col)
    hw = width // 2
    ho = span // 2
    info = jnp.stack([c, r, lax.axis_index("dp") % 2, far_end()]).astype(jnp.int32)
    seg = segment_ids[:, None]
    in_t = jnp.transpose(in_weight, (1, 0, 2))

    toks = [tokens] + [col_send(tokens, k) for k in peers()]
    toks_o = [row_send(p) for p in toks]

    def prep_first(inf, ng, fg, w, *outs):
        cc = inf[0]
        parts = []
        for g in (ng[...], fg[...]):
            for _ in range(3):
                piece = g.astype(bf16).astype(f32)
                parts.append(piece)
                g = g - piece
        at = lax.broadcasted_iota(jnp.int32, (16, width), 0)
        lines = jnp.zeros((16, width), f32)
        for i, piece in enumerate(parts):
            lines = jnp.where(at == i, jnp.broadcast_to(piece, (16, width)), lines)
        lines = lines.astype(bf16)
        for k in K:
            at = pl.multiple_of((cc ^ k) * lanes, lanes)
            for t in range(3):
                outs[k][:width, t * lanes:(t + 1) * lanes] = w[t, :, pl.ds(at, lanes)]
            outs[k][width:] = jnp.zeros((16, 3 * lanes), bf16)
            outs[k][width:, :width] = lines

    w_in = call(
        prep_first, info, [norm_gain[None], ffn_gain[None], in_t],
        [((width + 16, 3 * lanes), bf16)] * n_col,
    )
    w_in = [w_in[0]] + [col_send(w_in[k], k) for k in peers()]

    last_k = n_col - 1
    fold_ff = ff // 2

    def prep_rest(inf, ow, gw, uw, dw, og, oh, x0, y0, d0, gf, *outs):
        gt, ut = outs[-2:]
        cc, p = inf[0], inf[2]
        oh[...] = ow[pl.ds(pl.multiple_of(p * ho, ho), ho), :]
        gt[...] = gw[...].T
        ut[...] = uw[...].T
        gf[...] = og[...].astype(bf16)
        for k in K:
            at = pl.ds(pl.multiple_of((cc ^ k) * ff, 32), ff)
            x = jnp.where(p == 0, gt[at, :], ut[at, :])
            if k == 0:
                x0[...] = x
                y0[...] = jnp.where(p == 0, ut[at, :], gt[at, :])
                d0[...] = dw[at, :]
            else:
                outs[k - 1][...] = x
                dn = outs[last_k + k - 1]
                if k < last_k:
                    dn[:ff] = dw[at, :]
                    dn[ff:] = gf[...]
                else:
                    part = dw[at, pl.ds(pl.multiple_of(p * hw, hw), hw)]
                    dn[:fold_ff, :hw] = part[:fold_ff]
                    dn[:fold_ff, hw:] = part[fold_ff:]
                    dn[fold_ff:] = gf[...]

    rest = call(
        prep_rest, info, [out_weight, gate_weight, up_weight, down_weight, out_grad],
        [((ho, width), bf16)] + [((ff, width), bf16)] * 3 + [((rows, width), bf16)]
        + [((ff, width), bf16)] * last_k + [((ff + rows, width), bf16)] * (last_k - 1)
        + [((fold_ff + rows, width), bf16)],
        [pltpu.VMEM((hidden_ff, width), bf16)] * 2,
    )
    out_half, x0, y0, d0, gf0 = rest[:5]
    send_x, send_d = rest[5:5 + last_k], rest[5 + last_k:]
    outs_r = [out_weight] + [col_send(out_weight if k < last_k else out_half, k) for k in peers()]
    outs_r.append(pair_send(outs_r[last_k]))
    xs = [x0] + [col_send(send_x[k - 1], k) for k in peers()]
    ys = [y0] + [pair_send(x) for k, x in enumerate(xs) if k]
    downs = [d0] + [col_send(send_d[k - 1], k) for k in peers()]
    gfs = [gf0] + downs[1:]
    gfs_o = [row_send(a) for a in gfs]
    downs.append(pair_send(downs[last_k]))
    n_out = n_col + 1

    def mixer(inf, sg, taps, *refs):
        own, oth, w = refs[:n_col], refs[n_col:2 * n_col], refs[2 * n_col:3 * n_col]
        tok, gains, mixed, mix3, n1 = refs[3 * n_col:]
        total = jnp.zeros((group, 1), f32)
        for k in K:
            cols = slice(k * width, (k + 1) * width)
            tok[:rows, cols] = own[k][...]
            tok[rows:, cols] = oth[k][...]
            for i in range(2):
                gain = w[k][width:, :width].astype(f32)[3 * i:3 * i + 3]
                gains[i:i + 1, cols] = gain[0:1] + gain[1:2] + gain[2:3]
            part = tok[:, cols]
            total = total + jnp.sum(part * part, axis=1, keepdims=True)
        scale = lax.rsqrt(total / model + epsilon)
        acc = jnp.zeros((group, 3 * lanes), f32)
        for k in K:
            cols = slice(k * width, (k + 1) * width)
            normed = (tok[:, cols] * scale * gains[0:1, cols]).astype(bf16)
            if k == 0:
                n1[...] = normed
            acc = acc + dot(normed, w[k][:width], 1, 0)
        mix3[...] = acc
        one, two = masks(sg[...], inf[1], rows, group)
        product = acc[:, :lanes] * acc[:, 2 * lanes:]
        conv = (
            taps[2:3] * product
            + taps[1:2] * (pltpu.roll(product, 1, 0) * one)
            + taps[0:1] * (pltpu.roll(product, 2, 0) * two)
        )
        mixed[...] = (acc[:, lanes:2 * lanes] * conv).astype(bf16)

    tok, gains, mixed, mix3, n1 = call(
        mixer, info, [seg, conv_taps] + toks + toks_o + w_in,
        [
            ((group, model), f32), ((8, model), f32), ((group, lanes), bf16),
            ((group, 3 * lanes), f32), ((group, width), bf16),
        ],
    )
    mixeds = [mixed] + [col_send(mixed, k) for k in peers()]

    def outproj(inf, *refs):
        mo, wr = refs[:n_col], refs[n_col:n_col + n_out]
        hp, ms = refs[n_col + n_out:]
        cc, p = inf[0], inf[2]
        for k in K:
            ms[:, pl.ds(pl.multiple_of((cc ^ k) * lanes, lanes), lanes)] = mo[k][...]
        near = pl.ds(pl.multiple_of(p * ho, ho), ho)
        away = pl.ds(pl.multiple_of((1 - p) * ho, ho), ho)
        for k in K:
            cols = slice(k * width, (k + 1) * width)
            if k < last_k:
                hp[:, cols] = dot(ms[...], wr[k][...], 1, 0)
            else:
                hp[:, cols] = dot(ms[:, near], wr[k][...], 1, 0) + dot(ms[:, away], wr[k + 1][...], 1, 0)

    hp, = call(
        outproj, info, mixeds + outs_r, [((group, model), f32)],
        [pltpu.VMEM((group, span), bf16)],
    )
    hp_o = row_send(hp)

    def ffn_in(inf, tk, gn, mine, other, *refs):
        x, y = refs[:n_col], refs[n_col:2 * n_col]
        hidden, gp_out, up_out, act_out, n2 = refs[2 * n_col:]
        p = inf[2]
        total = jnp.zeros((group, 1), f32)
        for k in K:
            cols = slice(k * width, (k + 1) * width)
            swapped = jnp.concatenate([other[rows:, cols], other[:rows, cols]], axis=0)
            h = tk[:, cols] + (mine[:, cols] + swapped)
            hidden[:, cols] = h
            total = total + jnp.sum(h * h, axis=1, keepdims=True)
        scale = lax.rsqrt(total / model + epsilon)
        ax = jnp.zeros((ff, group), f32)
        ay = jnp.zeros((ff, group), f32)
        for k in K:
            cols = slice(k * width, (k + 1) * width)
            normed = (hidden[:, cols] * scale * gn[1:2, cols]).astype(bf16)
            if k == 0:
                n2[...] = normed
            ax = ax + dot(x[k][...], normed, 1, 1)
            ay = ay + dot(y[k][...], normed, 1, 1)
        gp = jnp.where(p == 0, ax, ay)
        up = jnp.where(p == 0, ay, ax)
        gp_out[...] = gp
        up_out[...] = up
        act_out[...] = (gp * jax.nn.sigmoid(gp) * up).astype(bf16)

    hidden, gate_proj, up_proj, act, n2 = call(
        ffn_in, info, [tok, gains, hp, hp_o] + xs + ys,
        [
            ((group, model), f32), ((ff, group), f32), ((ff, group), f32), ((ff, group), bf16),
            ((group, width), bf16),
        ],
        flops=2 * 10**9,
    )

    cut = 3 * ff // 2

    cut = 3 * ff // 2

    def ffn_back(inf, gpr, upr, act_ref, n2r, *refs):
        go, gx = refs[:n_col], refs[n_col:2 * n_col]
        dn = refs[2 * n_col:3 * n_col + 1]
        piece, chunk_a, chunk_b, gf, chunk = refs[3 * n_col + 1:]
        p = inf[2]
        ga = jnp.zeros((ff, group), f32)
        for k in K:
            skip = go[k].shape[0] - rows
            gf[k, :rows] = go[k][skip:]
            gf[k, rows:] = gx[k][skip:]
            if k < last_k:
                ga = ga + dot(dn[k][:ff], gf[k], 1, 1)
            else:
                near = gf[k, :, pl.ds(pl.multiple_of(p * hw, hw), hw)]
                away = gf[k, :, pl.ds(pl.multiple_of((1 - p) * hw, hw), hw)]
                for g, d in ((near, dn[k]), (away, dn[k + 1])):
                    top = dot(d[:fold_ff, :hw], g, 1, 1)
                    ga = ga + jnp.concatenate([top, dot(d[:fold_ff, hw:], g, 1, 1)], axis=0)
        gp, up = gpr[...], upr[...]
        sig = jax.nn.sigmoid(gp)
        piece[:ff] = act_ref[...]
        piece[ff:2 * ff] = (ga * up * sig * (1.0 + gp * (1.0 - sig))).astype(bf16)
        piece[2 * ff:] = (ga * gp * sig).astype(bf16)
        chunk[:ff] = dot(act_ref[...], gf[0], 1, 0).astype(bf16)
        chunk[ff:] = dot(piece[ff:], n2r[...], 1, 0).astype(bf16)
        chunk_a[...] = chunk[:cut]
        chunk_b[...] = chunk[cut:]

    piece0, chunk_a, chunk_b = call(
        ffn_back, info, [gate_proj, up_proj, act, n2] + gfs + gfs_o + downs,
        [((3 * ff, group), bf16), ((cut, width), bf16), ((3 * ff - cut, width), bf16)],
        [pltpu.VMEM((n_col, group, width), bf16), pltpu.VMEM((3 * ff, width), bf16)],
        flops=2 * 10**9,
    )

    def ffn_part(inf, pc, *refs):
        x, y = refs[:n_col], refs[n_col:2 * n_col]
        mine, sent = refs[2 * n_col:]
        gg, gu = pc[ff:2 * ff], pc[2 * ff:]
        a = jnp.where(inf[2] == 0, gg, gu).T
        b = jnp.where(inf[2] == 0, gu, gg).T
        for k in K:
            cols = slice(k * width, (k + 1) * width)
            part = dot(a, x[k][...], 1, 0) + dot(b, y[k][...], 1, 0)
            mine[:, cols] = part[:rows]
            sent[:, cols] = part[rows:].astype(bf16)

    mine2, sent2 = call(
        ffn_part, info, [piece0] + xs + ys,
        [((rows, model), f32), ((rows, model), bf16)], flops=10**9,
    )

    def fold(which):
        def body(inf, mn, came, act_in, gn, own, rs, *outs):
            total = mn[...] + came[...].astype(f32)
            rowsum = jnp.sum(total * act_in[:rows] * gn[which:which + 1], axis=1, keepdims=True)
            line = jnp.broadcast_to(rowsum, (rows, rows)).T[:16]
            high = line.astype(bf16)
            low = (line - high.astype(f32)).astype(bf16)
            own[...] = total[:, :width]
            rs[...] = jnp.broadcast_to(rowsum, (rows, 128))
            for k in peers():
                outs[k - 1][:rows] = total[:, k * width:(k + 1) * width].astype(bf16)
                outs[k - 1][rows:] = jnp.zeros((16, width), bf16)
                outs[k - 1][rows:, :rows] = high
                outs[k - 1][rows:, width - rows:] = low

        return body

    fold_outs = [((rows, width), f32), ((rows, 128), f32)] + [((rows + 16, width), bf16)] * (n_col - 1)

    def unfold(own, rs, came):
        total, line = own[...], jnp.zeros((16, rows), f32)
        for ref in came:
            total = total + ref[:rows].astype(f32)
            line = line + ref[rows:, :rows].astype(f32) + ref[rows:, width - rows:].astype(f32)
        return total, rs[:, :1] + jnp.broadcast_to(line[:1], (rows, rows)).T[:, :1]

    came2 = row_send(sent2)
    own2, rs2, *send2 = call(fold(1), info, [mine2, came2, hidden, gains], fold_outs)
    got2 = [col_send(s, k + 1) for k, s in enumerate(send2)]

    def mid(inf, own, rs, hid_ref, gn, og, *refs):
        came, (grad_mid, mix, gain) = refs[:n_col - 1], refs[n_col - 1:]
        total, mean = unfold(own, rs, came)
        full = hid_ref[:rows]
        scale = lax.rsqrt(jnp.sum(full * full, axis=1, keepdims=True) / model + epsilon)
        hid = hid_ref[:rows, :width]
        gm = og[...] + scale * (gn[1:2, :width] * total) - hid * (scale * scale * scale) * (mean / model)
        grad_mid[...] = gm
        mix[...] = gm.astype(bf16)
        gain[...] = jnp.broadcast_to(jnp.sum(total * hid * scale, axis=0, keepdims=True), (8, width))

    grad_mid, gmix0, gain_two = call(
        mid, info, [own2, rs2, hidden, gains, out_grad] + got2,
        [((rows, width), f32), ((rows, width), bf16), ((8, width), f32)],
    )
    gmix = [gmix0] + [col_send(gmix0, k) for k in peers()]
    gmix_o = [row_send(m) for m in gmix]

    pieces = [piece0] + [col_send(piece0, k) for k in peers()]

    def ffn_grad(inf, pc, gfa, gfb, n2r, out_a, out_b, gf, out):
        gf[:rows] = gfa[...]
        gf[rows:] = gfb[...]
        out[:ff] = dot(pc[:ff], gf[...], 1, 0).astype(bf16)
        out[ff:] = dot(pc[ff:], n2r[...], 1, 0).astype(bf16)
        out_a[...] = out[:cut]
        out_b[...] = out[cut:]

    ffn_sums = [[line_sum(chunk_a), line_sum(chunk_b)]]
    for k in peers():
        chunk_a, chunk_b = call(
            ffn_grad, info, [pieces[k], gf0, gfs_o[0], n2],
            [((cut, width), bf16), ((3 * ff - cut, width), bf16)],
            [pltpu.VMEM((group, width), bf16), pltpu.VMEM((3 * ff, width), bf16)],
        )
        ffn_sums.append([line_sum(chunk_a), line_sum(chunk_b)])

    def mixer_back(inf, sg, taps, m3, *refs):
        go, gx = refs[:n_col], refs[n_col:2 * n_col]
        w = refs[2 * n_col:2 * n_col + n_out]
        wi = refs[2 * n_col + n_out:][:n_col]
        trip_t, mine, sent, tg = refs[3 * n_col + n_out:]
        cc, p = inf[0], inf[2]
        inside = lax.rem(cc * lanes, ho)
        at = pl.ds(pl.multiple_of(inside, lanes), lanes)
        here = (cc * lanes >= ho) == (p == 1)
        gm = jnp.zeros((group, lanes), f32)
        for k in K:
            if k < last_k:
                wk = w[k][pl.ds(pl.multiple_of(cc * lanes, lanes), lanes), :]
            else:
                wk = jnp.where(here, w[k][at, :], w[k + 1][at, :])
            gm = gm + dot(jnp.concatenate([go[k][...], gx[k][...]], axis=0), wk, 1, 1)
        one, two = masks(sg[...], inf[1], rows, group)
        gate_in, gate_out, carried = m3[:, :lanes], m3[:, lanes:2 * lanes], m3[:, 2 * lanes:]
        product = gate_in * carried
        back_one = pltpu.roll(product, 1, 0) * one
        back_two = pltpu.roll(product, 2, 0) * two
        conv = taps[2:3] * product + taps[1:2] * back_one + taps[0:1] * back_two
        gc = gm * gate_out
        gpr = (
            taps[2:3] * gc
            + taps[1:2] * pltpu.roll(gc * one, group - 1, 0)
            + taps[0:1] * pltpu.roll(gc * two, group - 2, 0)
        )
        tg[...] = jnp.zeros((8, lanes), f32)
        tg[0:1] = jnp.sum(gc * back_two, axis=0, keepdims=True)
        tg[1:2] = jnp.sum(gc * back_one, axis=0, keepdims=True)
        tg[2:3] = jnp.sum(gc * product, axis=0, keepdims=True)
        triple = jnp.concatenate([gpr * carried, gm * conv, gpr * gate_in], axis=1)
        trip_t[...] = triple.T.astype(bf16)
        low = triple.astype(bf16)
        for k in K:
            cols = slice(k * width, (k + 1) * width)
            part = dot(low, wi[k][:width], 1, 1)
            mine[:, cols] = part[:rows]
            sent[:, cols] = part[rows:].astype(bf16)

    trip0, mine1, sent1, taps_grad = call(
        mixer_back, info, [seg, conv_taps, mix3] + gmix + gmix_o + outs_r + w_in,
        [((3 * lanes, group), bf16), ((rows, model), f32), ((rows, model), bf16), ((8, lanes), f32)],
    )
    trips = [trip0] + [col_send(trip0, k) for k in peers()]

    def mix_grad(inf, tr, mx, n1r, ga, gb, out, gm):
        gm[:rows] = ga[...]
        gm[rows:] = gb[...]
        out[:3 * lanes] = dot(tr[...], n1r[...], 1, 0).astype(bf16)
        out[3 * lanes:] = dot(mx[...].T, gm[...], 1, 0).astype(bf16)

    mix_sums = []
    for k in K:
        chunk, = call(
            mix_grad, info, [trips[k], mixeds[k], n1, gmix[0], gmix_o[0]],
            [((4 * lanes, width), bf16)], [pltpu.VMEM((group, width), bf16)],
        )
        mix_sums.append(line_sum(chunk))

    came1 = row_send(sent1)
    own1, rs1, *send1 = call(fold(0), info, [mine1, came1, tok, gains], fold_outs)
    got1 = [col_send(s, k + 1) for k, s in enumerate(send1)]

    def last(inf, own, rs, tk, gn, gmid, *refs):
        came, (out, gain) = refs[:n_col - 1], refs[n_col - 1:]
        total, mean = unfold(own, rs, came)
        full = tk[:rows]
        scale = lax.rsqrt(jnp.sum(full * full, axis=1, keepdims=True) / model + epsilon)
        part = tk[:rows, :width]
        out[...] = gmid[...] + scale * (gn[0:1, :width] * total) - part * (scale * scale * scale) * (mean / model)
        gain[...] = jnp.broadcast_to(jnp.sum(total * part * scale, axis=0, keepdims=True), (8, width))

    in_grad, gain_one = call(
        last, info, [own1, rs1, tok, gains, grad_mid] + got1,
        [((rows, width), f32), ((8, width), f32)],
    )

    def ffn_out(inf, dw, hid, *refs):
        pcs, (mine, sent) = refs[:n_col], refs[n_col:]
        acc = jnp.zeros((group, width), f32)
        for k in K:
            at = pl.ds(pl.multiple_of((inf[0] ^ k) * ff, 32), ff)
            acc = acc + dot(pcs[k][:ff].T, dw[at, :], 1, 0)
        mine[...] = acc[:rows] + hid[:rows, :width]
        sent[...] = acc[rows:]

    out_mine, out_sent = call(
        ffn_out, info, [down_weight, hidden] + pieces,
        [((rows, width), f32)] * 2,
    )
    block_out = out_mine + row_send(out_sent)

    gain_pair = jnp.concatenate([gain_one[:1], gain_two[:1]], axis=0)
    gain_pair = gain_pair + row_send(gain_pair)
    small = jnp.concatenate(
        [gain_pair, jnp.pad(taps_grad[:3], ((0, 0), (0, width - lanes))), jnp.zeros((3, width), f32)], axis=0
    )
    held, came = line_sum(small)
    small = jnp.where(info[3] == 1, came, held)

    def ffn_place(inf, *refs):
        parts, (gate, up, down, whole, gt, ut) = refs[:4 * n_col], refs[4 * n_col:]
        far = inf[3] == 1
        for k in K:
            ha, ca, hb, cb = parts[4 * k:4 * k + 4]
            whole[:cut] = jnp.where(far, ca[...], ha[...])
            whole[cut:] = jnp.where(far, cb[...], hb[...])
            at = pl.ds(pl.multiple_of((inf[0] ^ k) * ff, 32), ff)
            for i, dest in enumerate((down, gt, ut)):
                dest[at, :] = whole[i * ff:(i + 1) * ff].astype(dest.dtype)
        gate[...] = gt[...].T.astype(f32)
        up[...] = ut[...].T.astype(f32)

    gate_sum, up_sum, down_sum = call(
        ffn_place, info, [x for pair in ffn_sums for s in pair for x in s],
        [((width, hidden_ff), f32)] * 2 + [((hidden_ff, width), f32)],
        [pltpu.VMEM((3 * ff, width), bf16)] + [pltpu.VMEM((hidden_ff, width), bf16)] * 2,
    )

    def mix_place(inf, *refs):
        held_refs, came_refs = refs[:n_col], refs[n_col:2 * n_col]
        win, wout = refs[2 * n_col:]
        far = inf[3] == 1
        for k in K:
            at = pl.ds(pl.multiple_of((inf[0] ^ k) * lanes, lanes), lanes)
            for t in range(4):
                rr = slice(t * lanes, (t + 1) * lanes)
                got = jnp.where(far, came_refs[k][rr], held_refs[k][rr])
                if t < 3:
                    win[t, :, at] = got.T.astype(f32)
                else:
                    wout[at, :] = got.astype(f32)

    in_sum, out_sum = call(
        mix_place, info, [s[0] for s in mix_sums] + [s[1] for s in mix_sums],
        [((3, width, span), f32), ((span, width), f32)],
    )
    return (
        block_out,
        in_grad,
        small[0],
        jnp.transpose(in_sum, (1, 0, 2)),
        small[2:5, :lanes],
        out_sum,
        small[1],
        gate_sum,
        up_sum,
        down_sum,
    )


def solution(mesh):
    token = P(("dp", "row"), "col")
    feature, tap = P("col"), P(None, ("row", "col"))
    split_in, split_up, split_down = P("col", None, "row"), P("col", "row"), P("row", "col")
    weights = (feature, split_in, tap, split_down, feature, split_up, split_up, split_down)
    in_specs = (token, P("dp"), *weights, token)
    out_specs = (token, token, *weights)

    return jax.shard_map(per_device, mesh=mesh, in_specs=in_specs, out_specs=out_specs, check_vma=False)
```

profile of v0, /device:TPU:0, one launch (start us, length us, event | category | flops | bytes accessed | tf_op | source)
XLA Modules:
  0.0 426.3 jit_solution(11671217772604851547)
XLA Ops:
  0.6 4.0 collective-permute-start.2
  13.0 4.3 %shard_map.188 = (bf16[256,256]{1,0:T(8,128)(2,1)}, bf16[576,256]{1,0:T(8,128)(2,1)}, bf16[576,256]{1,0:T(8,128)(2,1)}, bf16[576,256]{1,0:T(8,128)(2,1)}, bf16[1...) custom-call(s32[4]{0:T(128)} %pad_add_fusion.inf, ...), custom_call_target="tpu_custom_call" | custom-call | flops 100000000 | bytes 3932160 | tf_op jit(solution)/shard_map/pallas_call | solution.py:24
  47.6 4.6 %collective-permute-done.26.refs_3_.refs_11_ = bf16[416,256]{1,0:T(8,128)(2,1)S(1)} collective-permute-done((bf16[416,256]{1,0:T(8,128)(2,1)S(1)}, bf16[416,256]{1,0:T(8,128)(2,1)S(1)}, u32[]{:S(2)}, u32[]{:S(2)}) %collective-permute-start.26) | collective-permute-done | bytes 213024 | tf_op jit(solution)/shard_map/ppermute | solution.py:43
  53.9 4.1 collective-permute-done.18.refs_1_
  59.5 12.6 %collective-permute-done.20.refs_3_ = bf16[576,256]{1,0:T(8,128)(2,1)S(1)} collective-permute-done((bf16[576,256]{1,0:T(8,128)(2,1)S(1)}, bf16[576,256]{1,0:T(8,128)(2,1)S(1)}, u32[]{:S(2)}, u32[]{:S(2)}) %collective-permute-start.20) | collective-permute-done | bytes 294944 | tf_op jit(solution)/shard_map/ppermute | solution.py:43
  74.6 7.3 %collective-permute-done.22.refs_6_ = bf16[576,256]{1,0:T(8,128)(2,1)S(1)} collective-permute-done((bf16[576,256]{1,0:T(8,128)(2,1)S(1)}, bf16[576,256]{1,0:T(8,128)(2,1)S(1)}, u32[]{:S(2)}, u32[]{:S(2)}) %collective-permute-start.22) | collective-permute-done | bytes 294944 | tf_op jit(solution)/shard_map/ppermute | solution.py:55
  82.4 5.9 %collective-permute-done.23.refs_7_ = bf16[576,256]{1,0:T(8,128)(2,1)S(1)} collective-permute-done((bf16[576,256]{1,0:T(8,128)(2,1)S(1)}, bf16[576,256]{1,0:T(8,128)(2,1)S(1)}, u32[]{:S(2)}, u32[]{:S(2)}) %collective-permute-start.23) | collective-permute-done | bytes 294944 | tf_op jit(solution)/shard_map/ppermute | solution.py:55
  89.3 4.7 %shard_map.190 = (f32[256,1024]{1,0:T(8,128)}, f32[576,256]{1,0:T(8,128)}, f32[576,256]{1,0:T(8,128)}, bf16[576,256]{1,0:T(8,128)(2,1)}, bf16[256,256]{1,0:T(8,128)(2,1)}) custom-call(s32[4]{0:T(128)} %pad_add_fusion.inf, f32[256,1024]{1,0:T(8,128)} %get-tuple-element.76.tk.act_in, f32[8,1024]{1,0:T(8,128)} %get-tuple-element.77.gn, ...), custom_call_target="tpu_custom_call" | custom-call | flops 2000000000 | bytes 5537792 | tf_op jit(solution)/shard_map/pallas_call | solution.py:24
  95.1 4.7 %shard_map.191 = (bf16[1728,256]{1,0:T(8,128)(2,1)}, bf16[864,256]{1,0:T(8,128)(2,1)}, bf16[864,256]{1,0:T(8,128)(2,1)}) custom-call(s32[4]{0:T(128)} %pad_add_fusion.inf, f32[576,256]{1,0:T(8,128)} %get-tuple-element.86.gpr, f32[576,256]{1,0:T(8,128)} %get-tuple-element.87.upr, bf16[576,256]{1,0:T(8,128)(2,1)} %get-tuple-element.88.act_ref, ...), custom_call_target="tpu_custom_call" | custom-call | flops 2000000000 | bytes 5046272 | tf_op jit(solution)/shard_map/pallas_call | solution.py:24
  147.4 15.9 %collective-permute-done.48.refs_0_ = bf16[144,256]{1,0:T(8,128)(2,1)S(1)} collective-permute-done((bf16[144,256]{1,0:T(8,128)(2,1)}, bf16[144,256]{1,0:T(8,128)(2,1)S(1)}, u32[]{:S(2)}, u32[]{:S(2)}) %collective-permute-start.48) | collective-permute-done | bytes 73760 | tf_op jit(solution)/shard_map/ppermute | solution.py:43
  173.5 14.4 %collective-permute-done.60.tr = bf16[384,256]{1,0:T(8,128)(2,1)S(1)} collective-permute-done((bf16[384,256]{1,0:T(8,128)(2,1)S(1)}, bf16[384,256]{1,0:T(8,128)(2,1)S(1)}, u32[]{:S(2)}, u32[]{:S(2)}) %collective-permute-start.60) | collective-permute-done | bytes 196640 | tf_op jit(solution)/shard_map/ppermute | solution.py:43
  197.0 13.9 %collective-permute-start.58 = (bf16[512,256]{1,0:T(8,128)(2,1)}, bf16[512,256]{1,0:T(8,128)(2,1)S(1)}, u32[]{:S(2)}, u32[]{:S(2)}) collective-permute-start(bf16[512,256]{1,0:T(8,128)(2,1)} %shard_map.200), channel_id=1, source_target_pairs={{0,8},{24,16},{1,9},{25,17},{2,10},{26,18},{3,11},{27,19},{4,12},{... | collective-permute-start | bytes 786440 | tf_op jit(solution)/shard_map/ppermute | solution.py:69
  229.1 4.7 %collective-permute-start.88 = (bf16[864,256]{1,0:T(8,128)(2,1)S(1)}, bf16[864,256]{1,0:T(8,128)(2,1)S(1)}, u32[]{:S(2)}, u32[]{:S(2)}) collective-permute-start(bf16[864,256]{1,0:T(8,128)(2,1)S(1)} %copy-done.45), channel_id=1, source_target_pairs={{0,8},{24,16},{1,9},{25,17},{2,10},{26,18},{3,11},{27,19},{4,12},{... | collective-permute-start | bytes 1327112 | tf_op jit(solution)/shard_map/ppermute | solution.py:69
  236.5 12.8 %collective-permute-start.91 = (bf16[864,256]{1,0:T(8,128)(2,1)S(1)}, bf16[864,256]{1,0:T(8,128)(2,1)S(1)}, u32[]{:S(2)}, u32[]{:S(2)}) collective-permute-start(bf16[864,256]{1,0:T(8,128)(2,1)S(1)} %copy-done.43), channel_id=1, source_target_pairs={{0,8},{24,16},{1,9},{25,17},{2,10},{26,18},{3,11},{27,19},{4,12},{... | collective-permute-start | bytes 1327112 | tf_op jit(solution)/shard_map/ppermute | solution.py:69
  249.4 4.0 collective-permute-start.82
  255.0 4.9 %collective-permute-done.91 = bf16[864,256]{1,0:T(8,128)(2,1)S(1)} collective-permute-done((bf16[864,256]{1,0:T(8,128)(2,1)S(1)}, bf16[864,256]{1,0:T(8,128)(2,1)S(1)}, u32[]{:S(2)}, u32[]{:S(2)}) %collective-permute-start.91) | collective-permute-done | bytes 442400 | tf_op jit(solution)/shard_map/ppermute | solution.py:69
  259.8 4.4 %collective-permute-start.76 = (bf16[864,256]{1,0:T(8,128)(2,1)S(1)}, bf16[864,256]{1,0:T(8,128)(2,1)S(1)}, u32[]{:S(2)}, u32[]{:S(2)}) collective-permute-start(bf16[864,256]{1,0:T(8,128)(2,1)S(1)} %copy-done.46), channel_id=1, source_target_pairs={{0,8},{24,16},{1,9},{25,17},{2,10},{26,18},{3,11},{27,19},{4,12},{... | collective-permute-start | bytes 1327112 | tf_op jit(solution)/shard_map/ppermute | solution.py:69
  264.4 4.9 %collective-permute-done.82 = bf16[864,256]{1,0:T(8,128)(2,1)S(1)} collective-permute-done((bf16[864,256]{1,0:T(8,128)(2,1)S(1)}, bf16[864,256]{1,0:T(8,128)(2,1)S(1)}, u32[]{:S(2)}, u32[]{:S(2)}) %collective-permute-start.82) | collective-permute-done | bytes 442400 | tf_op jit(solution)/shard_map/ppermute | solution.py:69
  269.3 4.4 %collective-permute-start.79 = (bf16[864,256]{1,0:T(8,128)(2,1)S(1)}, bf16[864,256]{1,0:T(8,128)(2,1)S(1)}, u32[]{:S(2)}, u32[]{:S(2)}) collective-permute-start(bf16[864,256]{1,0:T(8,128)(2,1)S(1)} %copy-done.44), channel_id=1, source_target_pairs={{0,8},{24,16},{1,9},{25,17},{2,10},{26,18},{3,11},{27,19},{4,12},{... | collective-permute-start | bytes 1327112 | tf_op jit(solution)/shard_map/ppermute | solution.py:69
  273.9 4.9 %collective-permute-done.85 = bf16[864,256]{1,0:T(8,128)(2,1)S(1)} collective-permute-done((bf16[864,256]{1,0:T(8,128)(2,1)S(1)}, bf16[864,256]{1,0:T(8,128)(2,1)S(1)}, u32[]{:S(2)}, u32[]{:S(2)}) %collective-permute-start.85) | collective-permute-done | bytes 442400 | tf_op jit(solution)/shard_map/ppermute | solution.py:69
  280.2 6.0 %collective-permute-done.76 = bf16[864,256]{1,0:T(8,128)(2,1)S(1)} collective-permute-done((bf16[864,256]{1,0:T(8,128)(2,1)S(1)}, bf16[864,256]{1,0:T(8,128)(2,1)S(1)}, u32[]{:S(2)}, u32[]{:S(2)}) %collective-permute-start.76) | collective-permute-done | bytes 442400 | tf_op jit(solution)/shard_map/ppermute | solution.py:69
  287.0 3.9 collective-permute-done.79
  303.4 42.3 %collective-permute-done.75.refs_3_ = bf16[864,256]{1,0:T(8,128)(2,1)S(1)} collective-permute-done((bf16[864,256]{1,0:T(8,128)(2,1)S(1)}, bf16[864,256]{1,0:T(8,128)(2,1)S(1)}, u32[]{:S(2)}, u32[]{:S(2)}) %collective-permute-start.75) | collective-permute-done | bytes 442400 | tf_op jit(solution)/shard_map/ppermute | solution.py:75
  347.0 4.3 %collective-permute-done.67.refs_5_ = bf16[512,256]{1,0:T(8,128)(2,1)S(1)} collective-permute-done((bf16[512,256]{1,0:T(8,128)(2,1)S(1)}, bf16[512,256]{1,0:T(8,128)(2,1)S(1)}, u32[]{:S(2)}, u32[]{:S(2)}) %collective-permute-start.67) | collective-permute-done | bytes 262176 | tf_op jit(solution)/shard_map/ppermute | solution.py:75
  352.6 4.3 %collective-permute-done.68.refs_6_ = bf16[512,256]{1,0:T(8,128)(2,1)S(1)} collective-permute-done((bf16[512,256]{1,0:T(8,128)(2,1)S(1)}, bf16[512,256]{1,0:T(8,128)(2,1)S(1)}, u32[]{:S(2)}, u32[]{:S(2)}) %collective-permute-start.68) | collective-permute-done | bytes 262176 | tf_op jit(solution)/shard_map/ppermute | solution.py:75
  358.2 4.3 %collective-permute-done.69.refs_7_ = bf16[512,256]{1,0:T(8,128)(2,1)S(1)} collective-permute-done((bf16[512,256]{1,0:T(8,128)(2,1)S(1)}, bf16[512,256]{1,0:T(8,128)(2,1)S(1)}, u32[]{:S(2)}, u32[]{:S(2)}) %collective-permute-start.69) | collective-permute-done | bytes 262176 | tf_op jit(solution)/shard_map/ppermute | solution.py:75
  363.9 8.2 %collective-permute-done.90.refs_13_ = bf16[864,256]{1,0:T(8,128)(2,1)S(1)} collective-permute-done((bf16[864,256]{1,0:T(8,128)(2,1)S(1)}, bf16[864,256]{1,0:T(8,128)(2,1)S(1)}, u32[]{:S(2)}, u32[]{:S(2)}) %collective-permute-start.90) | collective-permute-done | bytes 442400 | tf_op jit(solution)/shard_map/ppermute | solution.py:75
  381.5 9.5 %collective-permute-done.84.refs_9_ = bf16[864,256]{1,0:T(8,128)(2,1)S(1)} collective-permute-done((bf16[864,256]{1,0:T(8,128)(2,1)S(1)}, bf16[864,256]{1,0:T(8,128)(2,1)S(1)}, u32[]{:S(2)}, u32[]{:S(2)}) %collective-permute-start.84) | collective-permute-done | bytes 442400 | tf_op jit(solution)/shard_map/ppermute | solution.py:75
  391.0 9.5 %collective-permute-done.87.refs_11_ = bf16[864,256]{1,0:T(8,128)(2,1)S(1)} collective-permute-done((bf16[864,256]{1,0:T(8,128)(2,1)S(1)}, bf16[864,256]{1,0:T(8,128)(2,1)S(1)}, u32[]{:S(2)}, u32[]{:S(2)}) %collective-permute-start.87) | collective-permute-done | bytes 442400 | tf_op jit(solution)/shard_map/ppermute | solution.py:75
  400.5 9.5 %collective-permute-done.78.refs_5_ = bf16[864,256]{1,0:T(8,128)(2,1)S(1)} collective-permute-done((bf16[864,256]{1,0:T(8,128)(2,1)S(1)}, bf16[864,256]{1,0:T(8,128)(2,1)S(1)}, u32[]{:S(2)}, u32[]{:S(2)}) %collective-permute-start.78) | collective-permute-done | bytes 442400 | tf_op jit(solution)/shard_map/ppermute | solution.py:75
  410.0 8.9 %collective-permute-done.81.refs_7_ = bf16[864,256]{1,0:T(8,128)(2,1)S(1)} collective-permute-done((bf16[864,256]{1,0:T(8,128)(2,1)S(1)}, bf16[864,256]{1,0:T(8,128)(2,1)S(1)}, u32[]{:S(2)}, u32[]{:S(2)}) %collective-permute-start.81) | collective-permute-done | bytes 442400 | tf_op jit(solution)/shard_map/ppermute | solution.py:75
  419.8 6.5 %shard_map.207 = (f32[256,2304]{1,0:T(8,128)}, f32[256,2304]{1,0:T(8,128)}, f32[2304,256]{1,0:T(8,128)}) custom-call(s32[4]{0:T(128)} %pad_add_fusion.inf, bf16[864,256]{1,0:T(8,128)(2,1)} %copy-done.4, bf16[864,256]{1,0:T(8,128)(2,1)} %copy-done.31, bf16[864,256]{1,0:T(8,128)(2,1)} %copy-done.5, bf16[864,256]{1,0:T(8,128)(2,1)} %copy-done.32, ...), custom_call_target="tpu_custom_call" | custom-call | flops 100000000 | bytes 7077888 | tf_op jit(solution)/shard_map/pallas_call | solution.py:24
  (424 shorter events, 165.3 us)
Async XLA Ops:
  43.0 45.3 %collective-permute-start.17 = (f32[256,1024]{1,0:T(8,128)}, f32[256,1024]{1,0:T(8,128)S(1)}, u32[]{:S(2)}, u32[]{:S(2)}) collective-permute-start(f32[256,1024]{1,0:T(8,128)} %shard_map.189.mine), channel_id=1, source_target_pairs={{0,4},{4,0},{1,5},{5,1},{2,6},{6,2},{3,7},{7,3},{8,12},{12,8},{9,1... | collective-permute-start | bytes 3145736 | tf_op jit(solution)/shard_map/ppermute | solution.py:49
  46.6 26.0 %collective-permute-start.24 = (bf16[704,256]{1,0:T(8,128)(2,1)S(1)}, bf16[704,256]{1,0:T(8,128)(2,1)S(1)}, u32[]{:S(2)}, u32[]{:S(2)}) collective-permute-start(bf16[704,256]{1,0:T(8,128)(2,1)S(1)} %copy-done.84), channel_id=1, source_target_pairs={{0,1},{1,0},{2,3},{3,2},{4,5},{5,4},{6,7},{7,6},{8,9},{9,8},{10,11... | collective-permute-start | bytes 1081352 | tf_op jit(solution)/shard_map/ppermute | solution.py:43
  104.0 32.7 %collective-permute-start.70 = (bf16[864,256]{1,0:T(8,128)(2,1)S(1)}, bf16[864,256]{1,0:T(8,128)(2,1)S(1)}, u32[]{:S(2)}, u32[]{:S(2)}) collective-permute-start(bf16[864,256]{1,0:T(8,128)(2,1)S(1)} %copy-done.40), channel_id=1, source_target_pairs={{0,8},{24,16},{1,9},{25,17},{2,10},{26,18},{3,11},{27,19},{4,12},{... | collective-permute-start | bytes 1327112 | tf_op jit(solution)/shard_map/ppermute | solution.py:69
  120.2 23.2 %collective-permute-start.73 = (bf16[864,256]{1,0:T(8,128)(2,1)S(1)}, bf16[864,256]{1,0:T(8,128)(2,1)S(1)}, u32[]{:S(2)}, u32[]{:S(2)}) collective-permute-start(bf16[864,256]{1,0:T(8,128)(2,1)S(1)} %copy-done.39), channel_id=1, source_target_pairs={{0,8},{24,16},{1,9},{25,17},{2,10},{26,18},{3,11},{27,19},{4,12},{... | collective-permute-start | bytes 1327112 | tf_op jit(solution)/shard_map/ppermute | solution.py:69
  134.8 62.2 %collective-permute-start.34 = (bf16[1728,256]{1,0:T(8,128)(2,1)S(1)}, bf16[1728,256]{1,0:T(8,128)(2,1)S(1)}, u32[]{:S(2)}, u32[]{:S(2)}) collective-permute-start(bf16[1728,256]{1,0:T(8,128)(2,1)S(1)} %copy-done.23), channel_id=1, source_target_pairs={{0,3},{1,2},{2,1},{3,0},{4,7},{5,6},{6,5},{7,4},{8,11},{9,10},{10,... | collective-permute-start | bytes 2654216 | tf_op jit(solution)/shard_map/ppermute | solution.py:43
  136.8 32.6 %collective-permute-start.63 = (bf16[384,256]{1,0:T(8,128)(2,1)}, bf16[384,256]{1,0:T(8,128)(2,1)S(1)}, u32[]{:S(2)}, u32[]{:S(2)}) collective-permute-start(bf16[384,256]{1,0:T(8,128)(2,1)} %get-tuple-element.119.tr), channel_id=1, source_target_pairs={{0,3},{1,2},{2,1},{3,0},{4,7},{5,6},{6,5},{7,4},{8,11},{9,10},{10,... | collective-permute-start | bytes 589832 | tf_op jit(solution)/shard_map/ppermute | solution.py:43
  142.5 22.1 %collective-permute-start.49 = (bf16[144,256]{1,0:T(8,128)(2,1)}, bf16[144,256]{1,0:T(8,128)(2,1)S(1)}, u32[]{:S(2)}, u32[]{:S(2)}) collective-permute-start(bf16[144,256]{1,0:T(8,128)(2,1)} %get-tuple-element.113), channel_id=1, source_target_pairs={{0,2},{1,3},{2,0},{3,1},{4,6},{5,7},{6,4},{7,5},{8,10},{9,11},{10,... | collective-permute-start | bytes 221192 | tf_op jit(solution)/shard_map/ppermute | solution.py:43
  143.4 21.9 %collective-permute-start.50 = (bf16[144,256]{1,0:T(8,128)(2,1)}, bf16[144,256]{1,0:T(8,128)(2,1)S(1)}, u32[]{:S(2)}, u32[]{:S(2)}) collective-permute-start(bf16[144,256]{1,0:T(8,128)(2,1)} %get-tuple-element.114), channel_id=1, source_target_pairs={{0,3},{1,2},{2,1},{3,0},{4,7},{5,6},{6,5},{7,4},{8,11},{9,10},{10,... | collective-permute-start | bytes 221192 | tf_op jit(solution)/shard_map/ppermute | solution.py:43
  163.3 50.2 %collective-permute-start.33 = (bf16[1728,256]{1,0:T(8,128)(2,1)S(1)}, bf16[1728,256]{1,0:T(8,128)(2,1)S(1)}, u32[]{:S(2)}, u32[]{:S(2)}) collective-permute-start(bf16[1728,256]{1,0:T(8,128)(2,1)S(1)} %copy-done.23), channel_id=1, source_target_pairs={{0,2},{1,3},{2,0},{3,1},{4,6},{5,7},{6,4},{7,5},{8,10},{9,11},{10,... | collective-permute-start | bytes 2654216 | tf_op jit(solution)/shard_map/ppermute | solution.py:43
  164.6 23.4 %collective-permute-start.60 = (bf16[384,256]{1,0:T(8,128)(2,1)S(1)}, bf16[384,256]{1,0:T(8,128)(2,1)S(1)}, u32[]{:S(2)}, u32[]{:S(2)}) collective-permute-start(bf16[384,256]{1,0:T(8,128)(2,1)S(1)} %copy-done.56), channel_id=1, source_target_pairs={{0,2},{1,3},{2,0},{3,1},{4,6},{5,7},{6,4},{7,5},{8,10},{9,11},{10,... | collective-permute-start | bytes 589832 | tf_op jit(solution)/shard_map/ppermute | solution.py:43
  165.4 26.1 %collective-permute-start.57 = (bf16[384,256]{1,0:T(8,128)(2,1)S(1)}, bf16[384,256]{1,0:T(8,128)(2,1)S(1)}, u32[]{:S(2)}, u32[]{:S(2)}) collective-permute-start(bf16[384,256]{1,0:T(8,128)(2,1)S(1)} %copy-done.56), channel_id=1, source_target_pairs={{0,1},{1,0},{2,3},{3,2},{4,5},{5,4},{6,7},{7,6},{8,9},{9,8},{10,11... | collective-permute-start | bytes 589832 | tf_op jit(solution)/shard_map/ppermute | solution.py:43
  191.5 28.1 %collective-permute-start.32 = (bf16[1728,256]{1,0:T(8,128)(2,1)S(1)}, bf16[1728,256]{1,0:T(8,128)(2,1)S(1)}, u32[]{:S(2)}, u32[]{:S(2)}) collective-permute-start(bf16[1728,256]{1,0:T(8,128)(2,1)S(1)} %copy-done.23), channel_id=1, source_target_pairs={{0,1},{1,0},{2,3},{3,2},{4,5},{5,4},{6,7},{7,6},{8,9},{9,8},{10,11... | collective-permute-start | bytes 2654216 | tf_op jit(solution)/shard_map/ppermute | solution.py:43
  192.6 24.8 %collective-permute-start.71 = (bf16[864,256]{1,0:T(8,128)(2,1)S(1)}, bf16[864,256]{1,0:T(8,128)(2,1)S(1)}, u32[]{:S(2)}, u32[]{:S(2)}) collective-permute-start(bf16[864,256]{1,0:T(8,128)(2,1)S(1)} %add_convert_fusion.15), channel_id=1, source_target_pairs={{8,16},{16,8},{9,17},{17,9},{10,18},{18,10},{11,19},{19,11},{12,20... | collective-permute-start | bytes 1327112 | tf_op jit(solution)/shard_map/ppermute | solution.py:71
  196.1 22.8 %collective-permute-start.74 = (bf16[864,256]{1,0:T(8,128)(2,1)S(1)}, bf16[864,256]{1,0:T(8,128)(2,1)S(1)}, u32[]{:S(2)}, u32[]{:S(2)}) collective-permute-start(bf16[864,256]{1,0:T(8,128)(2,1)S(1)} %add_convert_fusion.13), channel_id=1, source_target_pairs={{8,16},{16,8},{9,17},{17,9},{10,18},{18,10},{11,19},{19,11},{12,20... | collective-permute-start | bytes 1327112 | tf_op jit(solution)/shard_map/ppermute | solution.py:71
  197.0 30.7 %collective-permute-start.58 = (bf16[512,256]{1,0:T(8,128)(2,1)}, bf16[512,256]{1,0:T(8,128)(2,1)S(1)}, u32[]{:S(2)}, u32[]{:S(2)}) collective-permute-start(bf16[512,256]{1,0:T(8,128)(2,1)} %shard_map.200), channel_id=1, source_target_pairs={{0,8},{24,16},{1,9},{25,17},{2,10},{26,18},{3,11},{27,19},{4,12},{... | collective-permute-start | bytes 786440 | tf_op jit(solution)/shard_map/ppermute | solution.py:69
  219.7 73.9 %collective-permute-start.54 = (f32[8,256]{1,0:T(8,128)S(1)}, f32[8,256]{1,0:T(8,128)S(1)}, u32[]{:S(2)}, u32[]{:S(2)}) collective-permute-start(f32[8,256]{1,0:T(8,128)S(1)} %add.94), channel_id=1, source_target_pairs={{8,0},{16,24},{9,1},{17,25},{10,2},{18,26},{11,3},{19,27},{12,4},{... | collective-permute-start | bytes 24584 | tf_op jit(solution)/shard_map/ppermute | solution.py:75
  227.6 71.6 %collective-permute-start.72 = (bf16[864,256]{1,0:T(8,128)(2,1)S(1)}, bf16[864,256]{1,0:T(8,128)(2,1)S(1)}, u32[]{:S(2)}, u32[]{:S(2)}) collective-permute-start(bf16[864,256]{1,0:T(8,128)(2,1)S(1)} %add_convert_fusion.14.refs_0_), channel_id=1, source_target_pairs={{8,0},{16,24},{9,1},{17,25},{10,2},{18,26},{11,3},{19,27},{12,4},{... | collective-permute-start | bytes 1327112 | tf_op jit(solution)/shard_map/ppermute | solution.py:75
  229.1 24.5 %collective-permute-start.88 = (bf16[864,256]{1,0:T(8,128)(2,1)S(1)}, bf16[864,256]{1,0:T(8,128)(2,1)S(1)}, u32[]{:S(2)}, u32[]{:S(2)}) collective-permute-start(bf16[864,256]{1,0:T(8,128)(2,1)S(1)} %copy-done.45), channel_id=1, source_target_pairs={{0,8},{24,16},{1,9},{25,17},{2,10},{26,18},{3,11},{27,19},{4,12},{... | collective-permute-start | bytes 1327112 | tf_op jit(solution)/shard_map/ppermute | solution.py:69
  236.5 23.3 %collective-permute-start.91 = (bf16[864,256]{1,0:T(8,128)(2,1)S(1)}, bf16[864,256]{1,0:T(8,128)(2,1)S(1)}, u32[]{:S(2)}, u32[]{:S(2)}) collective-permute-start(bf16[864,256]{1,0:T(8,128)(2,1)S(1)} %copy-done.43), channel_id=1, source_target_pairs={{0,8},{24,16},{1,9},{25,17},{2,10},{26,18},{3,11},{27,19},{4,12},{... | collective-permute-start | bytes 1327112 | tf_op jit(solution)/shard_map/ppermute | solution.py:69
  253.5 25.3 %collective-permute-start.85 = (bf16[864,256]{1,0:T(8,128)(2,1)S(1)}, bf16[864,256]{1,0:T(8,128)(2,1)S(1)}, u32[]{:S(2)}, u32[]{:S(2)}) collective-permute-start(bf16[864,256]{1,0:T(8,128)(2,1)S(1)} %copy-done.41), channel_id=1, source_target_pairs={{0,8},{24,16},{1,9},{25,17},{2,10},{26,18},{3,11},{27,19},{4,12},{... | collective-permute-start | bytes 1327112 | tf_op jit(solution)/shard_map/ppermute | solution.py:69
  259.8 26.4 %collective-permute-start.76 = (bf16[864,256]{1,0:T(8,128)(2,1)S(1)}, bf16[864,256]{1,0:T(8,128)(2,1)S(1)}, u32[]{:S(2)}, u32[]{:S(2)}) collective-permute-start(bf16[864,256]{1,0:T(8,128)(2,1)S(1)} %copy-done.46), channel_id=1, source_target_pairs={{0,8},{24,16},{1,9},{25,17},{2,10},{26,18},{3,11},{27,19},{4,12},{... | collective-permute-start | bytes 1327112 | tf_op jit(solution)/shard_map/ppermute | solution.py:69
  269.3 21.7 %collective-permute-start.79 = (bf16[864,256]{1,0:T(8,128)(2,1)S(1)}, bf16[864,256]{1,0:T(8,128)(2,1)S(1)}, u32[]{:S(2)}, u32[]{:S(2)}) collective-permute-start(bf16[864,256]{1,0:T(8,128)(2,1)S(1)} %copy-done.44), channel_id=1, source_target_pairs={{0,8},{24,16},{1,9},{25,17},{2,10},{26,18},{3,11},{27,19},{4,12},{... | collective-permute-start | bytes 1327112 | tf_op jit(solution)/shard_map/ppermute | solution.py:69
  296.6 49.1 %collective-permute-start.75 = (bf16[864,256]{1,0:T(8,128)(2,1)S(1)}, bf16[864,256]{1,0:T(8,128)(2,1)S(1)}, u32[]{:S(2)}, u32[]{:S(2)}) collective-permute-start(bf16[864,256]{1,0:T(8,128)(2,1)S(1)} %add_convert_fusion.12.refs_2_), channel_id=1, source_target_pairs={{8,0},{16,24},{9,1},{17,25},{10,2},{18,26},{11,3},{19,27},{12,4},{... | collective-permute-start | bytes 1327112 | tf_op jit(solution)/shard_map/ppermute | solution.py:75
  297.9 53.4 %collective-permute-start.67 = (bf16[512,256]{1,0:T(8,128)(2,1)S(1)}, bf16[512,256]{1,0:T(8,128)(2,1)S(1)}, u32[]{:S(2)}, u32[]{:S(2)}) collective-permute-start(bf16[512,256]{1,0:T(8,128)(2,1)S(1)} %add_convert_fusion.20.refs_1_), channel_id=1, source_target_pairs={{8,0},{16,24},{9,1},{17,25},{10,2},{18,26},{11,3},{19,27},{12,4},{... | collective-permute-start | bytes 786440 | tf_op jit(solution)/shard_map/ppermute | solution.py:75
  299.2 57.7 %collective-permute-start.68 = (bf16[512,256]{1,0:T(8,128)(2,1)S(1)}, bf16[512,256]{1,0:T(8,128)(2,1)S(1)}, u32[]{:S(2)}, u32[]{:S(2)}) collective-permute-start(bf16[512,256]{1,0:T(8,128)(2,1)S(1)} %add_convert_fusion.18.refs_2_), channel_id=1, source_target_pairs={{8,0},{16,24},{9,1},{17,25},{10,2},{18,26},{11,3},{19,27},{12,4},{... | collective-permute-start | bytes 786440 | tf_op jit(solution)/shard_map/ppermute | solution.py:75
  300.6 62.0 %collective-permute-start.69 = (bf16[512,256]{1,0:T(8,128)(2,1)S(1)}, bf16[512,256]{1,0:T(8,128)(2,1)S(1)}, u32[]{:S(2)}, u32[]{:S(2)}) collective-permute-start(bf16[512,256]{1,0:T(8,128)(2,1)S(1)} %add_convert_fusion.16.refs_3_), channel_id=1, source_target_pairs={{8,0},{16,24},{9,1},{17,25},{10,2},{18,26},{11,3},{19,27},{12,4},{... | collective-permute-start | bytes 786440 | tf_op jit(solution)/shard_map/ppermute | solution.py:75
  301.9 70.2 %collective-permute-start.90 = (bf16[864,256]{1,0:T(8,128)(2,1)S(1)}, bf16[864,256]{1,0:T(8,128)(2,1)S(1)}, u32[]{:S(2)}, u32[]{:S(2)}) collective-permute-start(bf16[864,256]{1,0:T(8,128)(2,1)S(1)} %add_convert_fusion.2.refs_12_), channel_id=1, source_target_pairs={{8,0},{16,24},{9,1},{17,25},{10,2},{18,26},{11,3},{19,27},{12,4},{... | collective-permute-start | bytes 1327112 | tf_op jit(solution)/shard_map/ppermute | solution.py:75
  345.7 35.8 %collective-permute-start.93 = (bf16[864,256]{1,0:T(8,128)(2,1)S(1)}, bf16[864,256]{1,0:T(8,128)(2,1)S(1)}, u32[]{:S(2)}, u32[]{:S(2)}) collective-permute-start(bf16[864,256]{1,0:T(8,128)(2,1)S(1)} %add_convert_fusion.refs_14_), channel_id=1, source_target_pairs={{8,0},{16,24},{9,1},{17,25},{10,2},{18,26},{11,3},{19,27},{12,4},{... | collective-permute-start | bytes 1327112 | tf_op jit(solution)/shard_map/ppermute | solution.py:75
  351.3 39.7 %collective-permute-start.84 = (bf16[864,256]{1,0:T(8,128)(2,1)S(1)}, bf16[864,256]{1,0:T(8,128)(2,1)S(1)}, u32[]{:S(2)}, u32[]{:S(2)}) collective-permute-start(bf16[864,256]{1,0:T(8,128)(2,1)S(1)} %add_convert_fusion.6.refs_8_), channel_id=1, source_target_pairs={{8,0},{16,24},{9,1},{17,25},{10,2},{18,26},{11,3},{19,27},{12,4},{... | collective-permute-start | bytes 1327112 | tf_op jit(solution)/shard_map/ppermute | solution.py:75
  357.0 43.5 %collective-permute-start.87 = (bf16[864,256]{1,0:T(8,128)(2,1)S(1)}, bf16[864,256]{1,0:T(8,128)(2,1)S(1)}, u32[]{:S(2)}, u32[]{:S(2)}) collective-permute-start(bf16[864,256]{1,0:T(8,128)(2,1)S(1)} %add_convert_fusion.4.refs_10_), channel_id=1, source_target_pairs={{8,0},{16,24},{9,1},{17,25},{10,2},{18,26},{11,3},{19,27},{12,4},{... | collective-permute-start | bytes 1327112 | tf_op jit(solution)/shard_map/ppermute | solution.py:75
  362.6 47.4 %collective-permute-start.78 = (bf16[864,256]{1,0:T(8,128)(2,1)S(1)}, bf16[864,256]{1,0:T(8,128)(2,1)S(1)}, u32[]{:S(2)}, u32[]{:S(2)}) collective-permute-start(bf16[864,256]{1,0:T(8,128)(2,1)S(1)} %add_convert_fusion.10.refs_4_), channel_id=1, source_target_pairs={{8,0},{16,24},{9,1},{17,25},{10,2},{18,26},{11,3},{19,27},{12,4},{... | collective-permute-start | bytes 1327112 | tf_op jit(solution)/shard_map/ppermute | solution.py:75
  372.1 46.9 %collective-permute-start.81 = (bf16[864,256]{1,0:T(8,128)(2,1)S(1)}, bf16[864,256]{1,0:T(8,128)(2,1)S(1)}, u32[]{:S(2)}, u32[]{:S(2)}) collective-permute-start(bf16[864,256]{1,0:T(8,128)(2,1)S(1)} %add_convert_fusion.8.refs_6_), channel_id=1, source_target_pairs={{8,0},{16,24},{9,1},{17,25},{10,2},{18,26},{11,3},{19,27},{12,4},{... | collective-permute-start | bytes 1327112 | tf_op jit(solution)/shard_map/ppermute | solution.py:75
  (165 other events, 2476.7 us)
where the time goes:
time: 428 us; the launch traced here: 426 us
  waiting for transfers between devices  211 us (49%)
  starting transfers between devices  131 us (31%)
  Pallas kernels  67.8 us (16%)
  local copies, waits for them, and re-layouts  10.9 us (3%)
    ppermute x13, waiting for transfers between devices, line_sum(): lax.ppermute(held, 'dp', [(half - 1 - s, half - 2 - s), (half + s, half +...  104 us
    pallas_call x22, Pallas kernels, call(): pl.pallas_call(body, out_shape=[jax.ShapeDtypeStruct(s, t) for s, t in ou...  67.8 us
    ppermute x33, waiting for transfers between devices, col_send(): return lax.ppermute(piece, 'col', [(i, i ^ k) for i in range(n)])  66.1 us
    ppermute x13, starting transfers between devices, line_sum(): came = lax.ppermute(held, 'dp', [(s, s + 1), (n - 1 - s, n - 2 - s)])  54.8 us
    ppermute x33, starting transfers between devices, col_send(): return lax.ppermute(piece, 'col', [(i, i ^ k) for i in range(n)])  42.5 us
    ppermute x13, waiting for transfers between devices, line_sum(): came = lax.ppermute(held, 'dp', [(s, s + 1), (n - 1 - s, n - 2 - s)])  24.8 us
    ppermute x13, starting transfers between devices, line_sum(): lax.ppermute(held, 'dp', [(half - 1 - s, half - 2 - s), (half + s, half +...  16.8 us
    ppermute x5, waiting for transfers between devices, pair_send(): return lax.ppermute(piece, 'dp', [(i, i ^ 1) for i in range(n)])  13.2 us
  transfers between devices with their start and end apart: 94, of which 36 were waited for; matrix products, arithmetic and copies ran while one was open for 2% of the time, Pallas kernels for 12%

commit v1 on v0

--- a/solution.py
+++ b/solution.py
@@ -77,6 +77,45 @@
             got = (me == half - 2 - s) | (me == half + 1 + s)
             held = jnp.where(got, came, held)
     return held, came
+
+
+LAG = 3
+
+
+def dp_sums(chunks):
+    n = lax.axis_size("dp")
+    if n != 4:
+        return [line_sum(g) for g in chunks]
+    two = lax.axis_size("row")
+    ends = [(i, i ^ 1) for i in range(n)]
+    inner = [(a * two + r, b * two + r) for a, b in ((1, 2), (2, 1)) for r in range(two)]
+    inner += [(a * two + r, a * two + (r + 1) % two) for a in (0, 3) for r in range(two)]
+    far = far_end() == 1
+    held, came_mid, totals = [], [], []
+    for i in range(len(chunks) + LAG):
+        t = None
+        if i >= LAG:
+            t = add_to(held[i - LAG], came_mid[i - LAG], bf16)
+        if i >= len(chunks):
+            sent = t
+        else:
+            g = chunks[i]
+            sent = g
+            if t is not None:
+                size = max(g.shape[0], t.shape[0])
+                sent = jnp.where(
+                    far,
+                    jnp.pad(g, ((0, size - g.shape[0]), (0, 0))),
+                    jnp.pad(t, ((0, size - t.shape[0]), (0, 0))),
+                )
+        came = lax.ppermute(sent, "dp", ends)
+        if i < len(chunks):
+            h = add_to(g, came[:g.shape[0]], bf16)
+            held.append(h)
+            came_mid.append(lax.ppermute(h, ("dp", "row"), inner))
+        if i >= LAG:
+            totals.append((sent, came))
+    return totals
 
 
 def far_end():
@@ -414,14 +453,14 @@
         out_a[...] = out[:cut]
         out_b[...] = out[cut:]
 
-    ffn_sums = [[line_sum(chunk_a), line_sum(chunk_b)]]
+    chunks = [chunk_a, chunk_b]
     for k in peers():
         chunk_a, chunk_b = call(
             ffn_grad, info, [pieces[k], gf0, gfs_o[0], n2],
             [((cut, width), bf16), ((3 * ff - cut, width), bf16)],
             [pltpu.VMEM((group, width), bf16), pltpu.VMEM((3 * ff, width), bf16)],
         )
-        ffn_sums.append([line_sum(chunk_a), line_sum(chunk_b)])
+        chunks += [chunk_a, chunk_b]
 
     def mixer_back(inf, sg, taps, m3, *refs):
         go, gx = refs[:n_col], refs[n_col:2 * n_col]
@@ -476,13 +515,12 @@
         out[:3 * lanes] = dot(tr[...], n1r[...], 1, 0).astype(bf16)
         out[3 * lanes:] = dot(mx[...].T, gm[...], 1, 0).astype(bf16)
 
-    mix_sums = []
     for k in K:
         chunk, = call(
             mix_grad, info, [trips[k], mixeds[k], n1, gmix[0], gmix_o[0]],
             [((4 * lanes, width), bf16)], [pltpu.VMEM((group, width), bf16)],
         )
-        mix_sums.append(line_sum(chunk))
+        chunks.append(chunk)
 
     came1 = row_send(sent1)
     own1, rs1, *send1 = call(fold(0), info, [mine1, came1, tok, gains], fold_outs)
@@ -519,19 +557,18 @@
 
     gain_pair = jnp.concatenate([gain_one[:1], gain_two[:1]], axis=0)
     gain_pair = gain_pair + row_send(gain_pair)
-    small = jnp.concatenate(
-        [gain_pair, jnp.pad(taps_grad[:3], ((0, 0), (0, width - lanes))), jnp.zeros((3, width), f32)], axis=0
-    )
-    held, came = line_sum(small)
-    small = jnp.where(info[3] == 1, came, held)
+    taps = jnp.pad(taps_grad[:3], ((0, 0), (0, width - lanes)))
+    chunks.append(jnp.pad(jnp.concatenate([gain_pair, taps], axis=0), ((0, 11), (0, 0))).astype(bf16))
+    sums = dp_sums(chunks)
+    small = jnp.where(info[3] == 1, sums[-1][1], sums[-1][0]).astype(f32)
 
     def ffn_place(inf, *refs):
         parts, (gate, up, down, whole, gt, ut) = refs[:4 * n_col], refs[4 * n_col:]
         far = inf[3] == 1
         for k in K:
             ha, ca, hb, cb = parts[4 * k:4 * k + 4]
-            whole[:cut] = jnp.where(far, ca[...], ha[...])
-            whole[cut:] = jnp.where(far, cb[...], hb[...])
+            whole[:cut] = jnp.where(far, ca[:cut], ha[:cut])
+            whole[cut:] = jnp.where(far, cb[:cut], hb[:cut])
             at = pl.ds(pl.multiple_of((inf[0] ^ k) * ff, 32), ff)
             for i, dest in enumerate((down, gt, ut)):
                 dest[at, :] = whole[i * ff:(i + 1) * ff].astype(dest.dtype)
@@ -539,7 +576,7 @@
         up[...] = ut[...].T.astype(f32)
 
     gate_sum, up_sum, down_sum = call(
-        ffn_place, info, [x for pair in ffn_sums for s in pair for x in s],
+        ffn_place, info, [x for s in sums[:2 * n_col] for x in s],
         [((width, hidden_ff), f32)] * 2 + [((hidden_ff, width), f32)],
         [pltpu.VMEM((3 * ff, width), bf16)] + [pltpu.VMEM((hidden_ff, width), bf16)] * 2,
     )
@@ -559,7 +596,7 @@
                     wout[at, :] = got.astype(f32)
 
     in_sum, out_sum = call(
-        mix_place, info, [s[0] for s in mix_sums] + [s[1] for s in mix_sums],
+        mix_place, info, [s[0] for s in sums[2 * n_col:-1]] + [s[1] for s in sums[2 * n_col:-1]],
         [((3, width, span), f32), ((span, width), f32)],
     )
     return (

time: 428 us -> 333 us (0.78)
  waiting for transfers between devices: 211 us -> 145 us
  starting transfers between devices: 131 us -> 97.4 us
    ppermute x39 -> x29, waiting for transfers between devices: 129 us -> 52.5 us  [the longest x16 52.4 us: dp_sums(): came = lax.ppermute(sent, 'dp', ends)]
    ppermute x39 -> x29, starting transfers between devices: 81 us -> 46.1 us  [the longest x16 44.8 us: dp_sums(): came = lax.ppermute(sent, 'dp', ends)]
    ppermute x33, waiting for transfers between devices: 66.1 us -> 77 us  [col_send(): return lax.ppermute(piece, 'col', [(i, i ^ k) for i in range(n)])]
    unnamed x206 -> x196, local copies, waits for them, and re-layouts: 7.46 us -> 10.3 us
  transfers between devices with their start and end apart: 94 -> 84, of which waited for: 36 -> 32; matrix products, arithmetic and copies ran while one was open for 2% -> 3% of each run, Pallas kernels for 12% -> 16%
where the time goes in v1:
time: 333 us; the launch traced here: 332 us
  waiting for transfers between devices  145 us (44%)
  starting transfers between devices  97.4 us (29%)
  Pallas kernels  68.1 us (20%)
  local copies, waits for them, and re-layouts  13.7 us (4%)
  other arithmetic  6.38 us (2%)
    ppermute x33, waiting for transfers between devices, col_send(): return lax.ppermute(piece, 'col', [(i, i ^ k) for i in range(n)])  77 us
    pallas_call x22, Pallas kernels, call(): pl.pallas_call(body, out_shape=[jax.ShapeDtypeStruct(s, t) for s, t in ou...  68.1 us
    ppermute x16, waiting for transfers between devices, dp_sums(): came = lax.ppermute(sent, 'dp', ends)  52.4 us
    ppermute x16, starting transfers between devices, dp_sums(): came = lax.ppermute(sent, 'dp', ends)  44.8 us
    ppermute x33, starting transfers between devices, col_send(): return lax.ppermute(piece, 'col', [(i, i ^ k) for i in range(n)])  43.8 us
    ppermute x5, waiting for transfers between devices, pair_send(): return lax.ppermute(piece, 'dp', [(i, i ^ 1) for i in range(n)])  13.2 us
    unnamed x196, local copies, waits for them, and re-layouts  10.3 us
  transfers between devices with their start and end apart: 84, of which 32 were waited for; matrix products, arithmetic and copies ran while one was open for 3% of the time, Pallas kernels for 16%

profile of v1, /device:TPU:0, one launch (start us, length us, event | category | flops | bytes accessed | tf_op | source)
XLA Modules:
  0.0 332.1 jit_solution(2106756674603812480)
XLA Ops:
  0.6 4.0 %collective-permute-start.2 = (f32[128,256]{1,0:T(8,128)}, f32[128,256]{1,0:T(8,128)S(1)}, u32[]{:S(2)}, u32[]{:S(2)}) collective-permute-start(f32[128,256]{1,0:T(8,128)} %refs_0_.1), channel_id=1, source_target_pairs={{0,3},{1,2},{2,1},{3,0},{4,7},{5,6},{6,5},{7,4},{8,11},{9,10},{10,... | collective-permute-start | bytes 393224 | tf_op jit(solution)/shard_map/ppermute | solution.py:43
  13.0 4.3 %shard_map.188 = (bf16[256,256]{1,0:T(8,128)(2,1)}, bf16[576,256]{1,0:T(8,128)(2,1)}, bf16[576,256]{1,0:T(8,128)(2,1)}, bf16[576,256]{1,0:T(8,128)(2,1)}, bf16[1...) custom-call(s32[4]{0:T(128)} %pad_add_fusion.inf, ...), custom_call_target="tpu_custom_call" | custom-call | flops 100000000 | bytes 3932160 | tf_op jit(solution)/shard_map/pallas_call | solution.py:24
  20.2 3.2 collective-permute-done.15.refs_7_.refs_11_
  29.4 3.0 shard_map.187
  47.5 4.6 %collective-permute-done.26.refs_3_.refs_11_ = bf16[416,256]{1,0:T(8,128)(2,1)S(1)} collective-permute-done((bf16[416,256]{1,0:T(8,128)(2,1)S(1)}, bf16[416,256]{1,0:T(8,128)(2,1)S(1)}, u32[]{:S(2)}, u32[]{:S(2)}) %collective-permute-start.26) | collective-permute-done | bytes 213024 | tf_op jit(solution)/shard_map/ppermute | solution.py:43
  53.9 4.3 %collective-permute-done.18.refs_1_ = bf16[576,256]{1,0:T(8,128)(2,1)S(1)} collective-permute-done((bf16[576,256]{1,0:T(8,128)(2,1)S(1)}, bf16[576,256]{1,0:T(8,128)(2,1)S(1)}, u32[]{:S(2)}, u32[]{:S(2)}) %collective-permute-start.18) | collective-permute-done | bytes 294944 | tf_op jit(solution)/shard_map/ppermute | solution.py:43
  59.5 12.6 %collective-permute-done.20.refs_3_ = bf16[576,256]{1,0:T(8,128)(2,1)S(1)} collective-permute-done((bf16[576,256]{1,0:T(8,128)(2,1)S(1)}, bf16[576,256]{1,0:T(8,128)(2,1)S(1)}, u32[]{:S(2)}, u32[]{:S(2)}) %collective-permute-start.20) | collective-permute-done | bytes 294944 | tf_op jit(solution)/shard_map/ppermute | solution.py:43
  74.6 7.3 %collective-permute-done.22.refs_6_ = bf16[576,256]{1,0:T(8,128)(2,1)S(1)} collective-permute-done((bf16[576,256]{1,0:T(8,128)(2,1)S(1)}, bf16[576,256]{1,0:T(8,128)(2,1)S(1)}, u32[]{:S(2)}, u32[]{:S(2)}) %collective-permute-start.22) | collective-permute-done | bytes 294944 | tf_op jit(solution)/shard_map/ppermute | solution.py:55
  82.4 5.8 %collective-permute-done.23.refs_7_ = bf16[576,256]{1,0:T(8,128)(2,1)S(1)} collective-permute-done((bf16[576,256]{1,0:T(8,128)(2,1)S(1)}, bf16[576,256]{1,0:T(8,128)(2,1)S(1)}, u32[]{:S(2)}, u32[]{:S(2)}) %collective-permute-start.23) | collective-permute-done | bytes 294944 | tf_op jit(solution)/shard_map/ppermute | solution.py:55
  89.3 4.7 %shard_map.190 = (f32[256,1024]{1,0:T(8,128)}, f32[576,256]{1,0:T(8,128)}, f32[576,256]{1,0:T(8,128)}, bf16[576,256]{1,0:T(8,128)(2,1)}, bf16[256,256]{1,0:T(8,128)(2,1)}) custom-call(s32[4]{0:T(128)} %pad_add_fusion.inf, f32[256,1024]{1,0:T(8,128)} %get-tuple-element.76.tk.act_in, f32[8,1024]{1,0:T(8,128)} %get-tuple-element.77.gn, ...), custom_call_target="tpu_custom_call" | custom-call | flops 2000000000 | bytes 5537792 | tf_op jit(solution)/shard_map/pallas_call | solution.py:24
  95.1 4.7 %shard_map.191 = (bf16[1728,256]{1,0:T(8,128)(2,1)}, bf16[864,256]{1,0:T(8,128)(2,1)}, bf16[864,256]{1,0:T(8,128)(2,1)}) custom-call(s32[4]{0:T(128)} %pad_add_fusion.inf, f32[576,256]{1,0:T(8,128)} %get-tuple-element.86.gpr, f32[576,256]{1,0:T(8,128)} %get-tuple-element.87.upr, bf16[576,256]{1,0:T(8,128)(2,1)} %get-tuple-element.88.act_ref, ...), custom_call_target="tpu_custom_call" | custom-call | flops 2000000000 | bytes 5046272 | tf_op jit(solution)/shard_map/pallas_call | solution.py:24
  99.8 3.8 %shard_map.193 = (f32[128,1024]{1,0:T(8,128)}, bf16[128,1024]{1,0:T(8,128)(2,1)}) custom-call(s32[4]{0:T(128)} %pad_add_fusion.inf, bf16[1728,256]{1,0:T(8,128)(2,1)} %get-tuple-element.95.refs_0_.pc, bf16[576,256]{1,0:T(8,128)(2,1)} %get-tuple-element.80.refs_0_, bf16[576,256]{1,0:T(8,128)(2,1)} %copy-done.88, bf16[576,256]{1,0:T(8,128)(2,1)} %copy-done.89, ...), custom_call_target="tpu_custom_call" | custom-call | flops 1000000000 | bytes 3244032 | tf_op jit(solution)/shard_map/pallas_call | solution.py:24
  127.0 17.5 %collective-permute-done.40.refs_1_ = bf16[128,256]{1,0:T(8,128)(2,1)S(1)} collective-permute-done((bf16[128,256]{1,0:T(8,128)(2,1)}, bf16[128,256]{1,0:T(8,128)(2,1)S(1)}, u32[]{:S(2)}, u32[]{:S(2)}) %collective-permute-start.40) | collective-permute-done | bytes 65568 | tf_op jit(solution)/shard_map/ppermute | solution.py:43
  146.6 3.6 %shard_map.196 = (bf16[384,256]{1,0:T(8,128)(2,1)}, f32[128,1024]{1,0:T(8,128)}, bf16[128,1024]{1,0:T(8,128)(2,1)}, f32[8,128]{1,0:T(8,128)}) custom-call(s32[4]{0:T(128)} %pad_add_fusion.inf, s32[256,1]{1,0:T(8,128)} %copy.21.sg, f32[3,128]{1,0:T(4,128)} %taps.3, f32[256,384]{1,0:T(8,128)} %get-tuple-element.98.m3, ...), custom_call_target="tpu_custom_call" | custom-call | flops 100000000 | bytes 2804224 | tf_op jit(solution)/shard_map/pallas_call | solution.py:24
  157.3 4.8 %collective-permute-done.71.tr = bf16[384,256]{1,0:T(8,128)(2,1)} collective-permute-done((bf16[384,256]{1,0:T(8,128)(2,1)}, bf16[384,256]{1,0:T(8,128)(2,1)}, u32[]{:S(2)}, u32[]{:S(2)}) %collective-permute-start.71) | collective-permute-done | bytes 196640 | tf_op jit(solution)/shard_map/ppermute | solution.py:43
  166.6 19.4 %collective-permute-done.49.refs_1_ = bf16[144,256]{1,0:T(8,128)(2,1)} collective-permute-done((bf16[144,256]{1,0:T(8,128)(2,1)}, bf16[144,256]{1,0:T(8,128)(2,1)}, u32[]{:S(2)}, u32[]{:S(2)}) %collective-permute-start.49) | collective-permute-done | bytes 73760 | tf_op jit(solution)/shard_map/ppermute | solution.py:43
  211.6 3.9 %shard_map.192 = (f32[128,256]{1,0:T(8,128)}, f32[128,256]{1,0:T(8,128)}) custom-call(s32[4]{0:T(128)} %pad_add_fusion.inf, bf16[2304,256]{1,0:T(8,128)(2,1)} %dw.3, f32[256,1024]{1,0:T(8,128)} %get-tuple-element.85.hid.act_in.hid_ref, bf16[1728,256]{1,0:T(8,128)(2,1)} %get-tuple-element.95.refs_0_.pc, bf16[1728,256]{1,0:T(8,128)(2,1)} %copy-done, ...), custom_call_target="tpu_custom_call" | custom-call | flops 100000000 | bytes 5767168 | tf_op jit(solution)/shard_map/pallas_call | solution.py:24
  218.8 6.3 %collective-permute-done.65 = bf16[864,256]{1,0:T(8,128)(2,1)S(1)} collective-permute-done((bf16[864,256]{1,0:T(8,128)(2,1)S(1)}, bf16[864,256]{1,0:T(8,128)(2,1)S(1)}, u32[]{:S(2)}, u32[]{:S(2)}) %collective-permute-start.65) | collective-permute-done | bytes 442400 | tf_op jit(solution)/shard_map/ppermute | solution.py:111
  232.4 8.8 %collective-permute-start.67 = (bf16[864,256]{1,0:T(8,128)(2,1)S(1)}, bf16[864,256]{1,0:T(8,128)(2,1)S(1)}, u32[]{:S(2)}, u32[]{:S(2)}) collective-permute-start(bf16[864,256]{1,0:T(8,128)(2,1)S(1)} %fusion.3.refs_4_), channel_id=1, source_target_pairs={{0,8},{8,0},{16,24},{24,16},{1,9},{9,1},{17,25},{25,17},{2,10},{10... | collective-permute-start | bytes 1327112 | tf_op jit(solution)/shard_map/ppermute | solution.py:111
  241.4 6.7 %collective-permute-done.57.refs_7_ = bf16[864,256]{1,0:T(8,128)(2,1)S(1)} collective-permute-done((bf16[864,256]{1,0:T(8,128)(2,1)S(1)}, bf16[864,256]{1,0:T(8,128)(2,1)S(1)}, u32[]{:S(2)}, u32[]{:S(2)}) %collective-permute-start.57) | collective-permute-done | bytes 442400 | tf_op jit(solution)/shard_map/ppermute | solution.py:111
  248.4 8.8 %collective-permute-done.67.refs_5_ = bf16[864,256]{1,0:T(8,128)(2,1)S(1)} collective-permute-done((bf16[864,256]{1,0:T(8,128)(2,1)S(1)}, bf16[864,256]{1,0:T(8,128)(2,1)S(1)}, u32[]{:S(2)}, u32[]{:S(2)}) %collective-permute-start.67) | collective-permute-done | bytes 442400 | tf_op jit(solution)/shard_map/ppermute | solution.py:111
  259.9 4.3 %collective-permute-start.59 = (bf16[864,256]{1,0:T(8,128)(2,1)S(1)}, bf16[864,256]{1,0:T(8,128)(2,1)S(1)}, u32[]{:S(2)}, u32[]{:S(2)}) collective-permute-start(bf16[864,256]{1,0:T(8,128)(2,1)S(1)} %fusion.2.refs_12_), channel_id=1, source_target_pairs={{0,8},{8,0},{16,24},{24,16},{1,9},{9,1},{17,25},{25,17},{2,10},{10... | collective-permute-start | bytes 1327112 | tf_op jit(solution)/shard_map/ppermute | solution.py:111
  264.4 8.0 %collective-permute-start.69 = (bf16[864,256]{1,0:T(8,128)(2,1)S(1)}, bf16[864,256]{1,0:T(8,128)(2,1)S(1)}, u32[]{:S(2)}, u32[]{:S(2)}) collective-permute-start(bf16[864,256]{1,0:T(8,128)(2,1)S(1)} %fusion.4.refs_10_), channel_id=1, source_target_pairs={{0,8},{8,0},{16,24},{24,16},{1,9},{9,1},{17,25},{25,17},{2,10},{10... | collective-permute-start | bytes 1327112 | tf_op jit(solution)/shard_map/ppermute | solution.py:111
  272.6 7.6 %collective-permute-done.59.refs_13_ = bf16[864,256]{1,0:T(8,128)(2,1)S(1)} collective-permute-done((bf16[864,256]{1,0:T(8,128)(2,1)S(1)}, bf16[864,256]{1,0:T(8,128)(2,1)S(1)}, u32[]{:S(2)}, u32[]{:S(2)}) %collective-permute-start.59) | collective-permute-done | bytes 442400 | tf_op jit(solution)/shard_map/ppermute | solution.py:111
  280.4 8.8 %collective-permute-done.69.refs_11_ = bf16[864,256]{1,0:T(8,128)(2,1)S(1)} collective-permute-done((bf16[864,256]{1,0:T(8,128)(2,1)S(1)}, bf16[864,256]{1,0:T(8,128)(2,1)S(1)}, u32[]{:S(2)}, u32[]{:S(2)}) %collective-permute-start.69) | collective-permute-done | bytes 442400 | tf_op jit(solution)/shard_map/ppermute | solution.py:111
  292.0 5.4 %collective-permute-start.80 = (bf16[512,256]{1,0:T(8,128)(2,1)S(1)}, bf16[512,256]{1,0:T(8,128)(2,1)S(1)}, u32[]{:S(2)}, u32[]{:S(2)}) collective-permute-start(bf16[512,256]{1,0:T(8,128)(2,1)S(1)} %fusion.9.refs_0_), channel_id=1, source_target_pairs={{0,8},{8,0},{16,24},{24,16},{1,9},{9,1},{17,25},{25,17},{2,10},{10... | collective-permute-start | bytes 786440 | tf_op jit(solution)/shard_map/ppermute | solution.py:111
  297.4 5.2 %collective-permute-done.78.refs_15_ = bf16[864,256]{1,0:T(8,128)(2,1)S(1)} collective-permute-done((bf16[864,256]{1,0:T(8,128)(2,1)S(1)}, bf16[864,256]{1,0:T(8,128)(2,1)S(1)}, u32[]{:S(2)}, u32[]{:S(2)}) %collective-permute-start.78) | collective-permute-done | bytes 442400 | tf_op jit(solution)/shard_map/ppermute | solution.py:111
  303.5 6.5 %shard_map.207 = (f32[256,2304]{1,0:T(8,128)}, f32[256,2304]{1,0:T(8,128)}, f32[2304,256]{1,0:T(8,128)}) custom-call(s32[4]{0:T(128)} %pad_add_fusion.inf, bf16[864,256]{1,0:T(8,128)(2,1)} %copy-done.11, bf16[864,256]{1,0:T(8,128)(2,1)} %copy-done.12, bf16[864,256]{1,0:T(8,128)(2,1)} %copy-done.13, bf16[864,256]{1,0:T(8,128)(2,1)} %copy-done.14, ...), custom_call_target="tpu_custom_call" | custom-call | flops 100000000 | bytes 7077888 | tf_op jit(solution)/shard_map/pallas_call | solution.py:24
  310.1 3.3 collective-permute-done.80.refs_4_
  316.0 5.4 %collective-permute-start.83 = (bf16[512,256]{1,0:T(8,128)(2,1)S(1)}, bf16[512,256]{1,0:T(8,128)(2,1)S(1)}, u32[]{:S(2)}, u32[]{:S(2)}) collective-permute-start(bf16[512,256]{1,0:T(8,128)(2,1)S(1)} %add_convert_fusion.16.refs_3_), channel_id=1, source_target_pairs={{0,8},{8,0},{16,24},{24,16},{1,9},{9,1},{17,25},{25,17},{2,10},{10... | collective-permute-start | bytes 786440 | tf_op jit(solution)/shard_map/ppermute | solution.py:111
  324.3 3.9 %collective-permute-done.83.refs_7_ = bf16[512,256]{1,0:T(8,128)(2,1)S(1)} collective-permute-done((bf16[512,256]{1,0:T(8,128)(2,1)S(1)}, bf16[512,256]{1,0:T(8,128)(2,1)S(1)}, u32[]{:S(2)}, u32[]{:S(2)}) %collective-permute-start.83) | collective-permute-done | bytes 262176 | tf_op jit(solution)/shard_map/ppermute | solution.py:111
  328.9 3.1 shard_map.206
  (394 shorter events, 126.5 us)
Async XLA Ops:
  8.2 16.8 %collective-permute-start.7 = (bf16[272,384]{1,0:T(8,128)(2,1)}, bf16[272,384]{1,0:T(8,128)(2,1)S(1)}, u32[]{:S(2)}, u32[]{:S(2)}) collective-permute-start(bf16[272,384]{1,0:T(8,128)(2,1)} %get-tuple-element.73), channel_id=1, source_target_pairs={{0,1},{1,0},{2,3},{3,2},{4,5},{5,4},{6,7},{7,6},{8,9},{9,8},{10,11... | collective-permute-start | bytes 626696 | tf_op jit(solution)/shard_map/ppermute | solution.py:43
  10.1 15.6 %collective-permute-start.8 = (bf16[272,384]{1,0:T(8,128)(2,1)}, bf16[272,384]{1,0:T(8,128)(2,1)S(1)}, u32[]{:S(2)}, u32[]{:S(2)}) collective-permute-start(bf16[272,384]{1,0:T(8,128)(2,1)} %get-tuple-element.74), channel_id=1, source_target_pairs={{0,2},{1,3},{2,0},{3,1},{4,6},{5,7},{6,4},{7,5},{8,10},{9,11},{10,... | collective-permute-start | bytes 626696 | tf_op jit(solution)/shard_map/ppermute | solution.py:43
  19.0 15.7 %collective-permute-start.14 = (bf16[512,256]{1,0:T(8,128)(2,1)S(1)}, bf16[512,256]{1,0:T(8,128)(2,1)S(1)}, u32[]{:S(2)}, u32[]{:S(2)}) collective-permute-start(bf16[512,256]{1,0:T(8,128)(2,1)S(1)} %copy-done.3), channel_id=1, source_target_pairs={{0,2},{1,3},{2,0},{3,1},{4,6},{5,7},{6,4},{7,5},{8,10},{9,11},{10,... | collective-permute-start | bytes 786440 | tf_op jit(solution)/shard_map/ppermute | solution.py:43
  43.0 45.3 %collective-permute-start.17 = (f32[256,1024]{1,0:T(8,128)}, f32[256,1024]{1,0:T(8,128)S(1)}, u32[]{:S(2)}, u32[]{:S(2)}) collective-permute-start(f32[256,1024]{1,0:T(8,128)} %shard_map.189.mine), channel_id=1, source_target_pairs={{0,4},{4,0},{1,5},{5,1},{2,6},{6,2},{3,7},{7,3},{8,12},{12,8},{9,1... | collective-permute-start | bytes 3145736 | tf_op jit(solution)/shard_map/ppermute | solution.py:49
  46.5 26.0 %collective-permute-start.24 = (bf16[704,256]{1,0:T(8,128)(2,1)S(1)}, bf16[704,256]{1,0:T(8,128)(2,1)S(1)}, u32[]{:S(2)}, u32[]{:S(2)}) collective-permute-start(bf16[704,256]{1,0:T(8,128)(2,1)S(1)} %copy-done.80), channel_id=1, source_target_pairs={{0,1},{1,0},{2,3},{3,2},{4,5},{5,4},{6,7},{7,6},{8,9},{9,8},{10,11... | collective-permute-start | bytes 1081352 | tf_op jit(solution)/shard_map/ppermute | solution.py:43
  52.1 19.9 %collective-permute-start.20 = (bf16[576,256]{1,0:T(8,128)(2,1)S(1)}, bf16[576,256]{1,0:T(8,128)(2,1)S(1)}, u32[]{:S(2)}, u32[]{:S(2)}) collective-permute-start(bf16[576,256]{1,0:T(8,128)(2,1)S(1)} %copy-done.85), channel_id=1, source_target_pairs={{0,3},{1,2},{2,1},{3,0},{4,7},{5,6},{6,5},{7,4},{8,11},{9,10},{10,... | collective-permute-start | bytes 884744 | tf_op jit(solution)/shard_map/ppermute | solution.py:43
  58.2 15.8 %collective-permute-start.25 = (bf16[704,256]{1,0:T(8,128)(2,1)S(1)}, bf16[704,256]{1,0:T(8,128)(2,1)S(1)}, u32[]{:S(2)}, u32[]{:S(2)}) collective-permute-start(bf16[704,256]{1,0:T(8,128)(2,1)S(1)} %copy-done.79), channel_id=1, source_target_pairs={{0,2},{1,3},{2,0},{3,1},{4,6},{5,7},{6,4},{7,5},{8,10},{9,11},{10,... | collective-permute-start | bytes 1081352 | tf_op jit(solution)/shard_map/ppermute | solution.py:43
  59.0 15.1 %collective-permute-start.21 = (bf16[576,256]{1,0:T(8,128)(2,1)S(1)}, bf16[576,256]{1,0:T(8,128)(2,1)S(1)}, u32[]{:S(2)}, u32[]{:S(2)}) collective-permute-start(bf16[576,256]{1,0:T(8,128)(2,1)S(1)} %collective-permute-done.18.refs_1_), channel_id=1, source_target_pairs={{0,8},{8,0},{16,24},{24,16},{1,9},{9,1},{17,25},{25,17},{2,10},{10... | collective-permute-start | bytes 884744 | tf_op jit(solution)/shard_map/ppermute | solution.py:55
  72.5 15.7 %collective-permute-start.23 = (bf16[576,256]{1,0:T(8,128)(2,1)S(1)}, bf16[576,256]{1,0:T(8,128)(2,1)S(1)}, u32[]{:S(2)}, u32[]{:S(2)}) collective-permute-start(bf16[576,256]{1,0:T(8,128)(2,1)S(1)} %collective-permute-done.20.refs_3_), channel_id=1, source_target_pairs={{0,8},{8,0},{16,24},{24,16},{1,9},{9,1},{17,25},{25,17},{2,10},{10... | collective-permute-start | bytes 884744 | tf_op jit(solution)/shard_map/ppermute | solution.py:55
  74.1 20.0 %collective-permute-start.28 = (bf16[704,256]{1,0:T(8,128)(2,1)S(1)}, bf16[704,256]{1,0:T(8,128)(2,1)S(1)}, u32[]{:S(2)}, u32[]{:S(2)}) collective-permute-start(bf16[704,256]{1,0:T(8,128)(2,1)S(1)} %collective-permute-done.24.refs_1_.refs_9_), channel_id=1, source_target_pairs={{0,4},{4,0},{1,5},{5,1},{2,6},{6,2},{3,7},{7,3},{8,12},{12,8},{9,1... | collective-permute-start | bytes 1081352 | tf_op jit(solution)/shard_map/ppermute | solution.py:49
  74.1 20.0 %collective-permute-start.29 = (bf16[704,256]{1,0:T(8,128)(2,1)S(1)}, bf16[704,256]{1,0:T(8,128)(2,1)S(1)}, u32[]{:S(2)}, u32[]{:S(2)}) collective-permute-start(bf16[704,256]{1,0:T(8,128)(2,1)S(1)} %collective-permute-done.25.refs_2_.refs_10_), channel_id=1, source_target_pairs={{0,4},{4,0},{1,5},{5,1},{2,6},{6,2},{3,7},{7,3},{8,12},{12,8},{9,1... | collective-permute-start | bytes 1081352 | tf_op jit(solution)/shard_map/ppermute | solution.py:49
  104.0 48.0 %collective-permute-start.53 = (bf16[864,256]{1,0:T(8,128)(2,1)S(1)}, bf16[864,256]{1,0:T(8,128)(2,1)S(1)}, u32[]{:S(2)}, u32[]{:S(2)}) collective-permute-start(bf16[864,256]{1,0:T(8,128)(2,1)S(1)} %copy-done.46), channel_id=1, source_target_pairs={{0,8},{8,0},{16,24},{24,16},{1,9},{9,1},{17,25},{25,17},{2,10},{10... | collective-permute-start | bytes 1327112 | tf_op jit(solution)/shard_map/ppermute | solution.py:111
  120.5 78.2 %collective-permute-start.32 = (bf16[1728,256]{1,0:T(8,128)(2,1)S(1)}, bf16[1728,256]{1,0:T(8,128)(2,1)S(1)}, u32[]{:S(2)}, u32[]{:S(2)}) collective-permute-start(bf16[1728,256]{1,0:T(8,128)(2,1)S(1)} %copy-done.37), channel_id=1, source_target_pairs={{0,1},{1,0},{2,3},{3,2},{4,5},{5,4},{6,7},{7,6},{8,9},{9,8},{10,11... | collective-permute-start | bytes 2654216 | tf_op jit(solution)/shard_map/ppermute | solution.py:43
  122.9 21.7 %collective-permute-start.40 = (bf16[128,256]{1,0:T(8,128)(2,1)}, bf16[128,256]{1,0:T(8,128)(2,1)S(1)}, u32[]{:S(2)}, u32[]{:S(2)}) collective-permute-start(bf16[128,256]{1,0:T(8,128)(2,1)} %get-tuple-element.106.refs_0_.ga), channel_id=1, source_target_pairs={{0,1},{1,0},{2,3},{3,2},{4,5},{5,4},{6,7},{7,6},{8,9},{9,8},{10,11... | collective-permute-start | bytes 196616 | tf_op jit(solution)/shard_map/ppermute | solution.py:43
  125.4 19.1 %collective-permute-start.46 = (bf16[128,256]{1,0:T(8,128)(2,1)S(1)}, bf16[128,256]{1,0:T(8,128)(2,1)S(1)}, u32[]{:S(2)}, u32[]{:S(2)}) collective-permute-start(bf16[128,256]{1,0:T(8,128)(2,1)S(1)} %collective-permute-done.42.refs_3_), channel_id=1, source_target_pairs={{0,4},{4,0},{1,5},{5,1},{2,6},{6,2},{3,7},{7,3},{8,12},{12,8},{9,1... | collective-permute-start | bytes 196616 | tf_op jit(solution)/shard_map/ppermute | solution.py:49
  126.3 30.0 %collective-permute-start.72 = (bf16[864,256]{1,0:T(8,128)(2,1)S(1)}, bf16[864,256]{1,0:T(8,128)(2,1)S(1)}, u32[]{:S(2)}, u32[]{:S(2)}) collective-permute-start(bf16[864,256]{1,0:T(8,128)(2,1)S(1)} %copy-done.45), channel_id=1, source_target_pairs={{0,8},{8,0},{16,24},{24,16},{1,9},{9,1},{17,25},{25,17},{2,10},{10... | collective-permute-start | bytes 1327112 | tf_op jit(solution)/shard_map/ppermute | solution.py:111
  153.2 49.4 %collective-permute-start.54 = (bf16[864,256]{1,0:T(8,128)(2,1)S(1)}, bf16[864,256]{1,0:T(8,128)(2,1)S(1)}, u32[]{:S(2)}, u32[]{:S(2)}) collective-permute-start(bf16[864,256]{1,0:T(8,128)(2,1)S(1)} %add_convert_fusion.15), channel_id=1, source_target_pairs={{8,16},{12,20},{16,8},{20,12},{0,4},{4,0},{24,28},{28,24},{9,17},{... | collective-permute-start | bytes 1327112 | tf_op jit(solution)/shard_map/ppermute | solution.py:115
  162.1 23.8 %collective-permute-start.49 = (bf16[144,256]{1,0:T(8,128)(2,1)}, bf16[144,256]{1,0:T(8,128)(2,1)}, u32[]{:S(2)}, u32[]{:S(2)}) collective-permute-start(bf16[144,256]{1,0:T(8,128)(2,1)} %get-tuple-element.113), channel_id=1, source_target_pairs={{0,2},{1,3},{2,0},{3,1},{4,6},{5,7},{6,4},{7,5},{8,10},{9,11},{10,... | collective-permute-start | bytes 221192 | tf_op jit(solution)/shard_map/ppermute | solution.py:43
  164.2 45.6 %collective-permute-start.34 = (bf16[1728,256]{1,0:T(8,128)(2,1)S(1)}, bf16[1728,256]{1,0:T(8,128)(2,1)S(1)}, u32[]{:S(2)}, u32[]{:S(2)}) collective-permute-start(bf16[1728,256]{1,0:T(8,128)(2,1)S(1)} %copy-done.37), channel_id=1, source_target_pairs={{0,3},{1,2},{2,1},{3,0},{4,7},{5,6},{6,5},{7,4},{8,11},{9,10},{10,... | collective-permute-start | bytes 2654216 | tf_op jit(solution)/shard_map/ppermute | solution.py:43
  165.3 44.5 %collective-permute-start.33 = (bf16[1728,256]{1,0:T(8,128)(2,1)S(1)}, bf16[1728,256]{1,0:T(8,128)(2,1)S(1)}, u32[]{:S(2)}, u32[]{:S(2)}) collective-permute-start(bf16[1728,256]{1,0:T(8,128)(2,1)S(1)} %copy-done.37), channel_id=1, source_target_pairs={{0,2},{1,3},{2,0},{3,1},{4,6},{5,7},{6,4},{7,5},{8,10},{9,11},{10,... | collective-permute-start | bytes 2654216 | tf_op jit(solution)/shard_map/ppermute | solution.py:43
  195.1 30.2 %collective-permute-start.73 = (bf16[864,256]{1,0:T(8,128)(2,1)S(1)}, bf16[864,256]{1,0:T(8,128)(2,1)S(1)}, u32[]{:S(2)}, u32[]{:S(2)}) collective-permute-start(bf16[864,256]{1,0:T(8,128)(2,1)S(1)} %add_convert_fusion.5), channel_id=1, source_target_pairs={{8,16},{12,20},{16,8},{20,12},{0,4},{4,0},{24,28},{28,24},{9,17},{... | collective-permute-start | bytes 1327112 | tf_op jit(solution)/shard_map/ppermute | solution.py:115
  208.2 16.9 %collective-permute-start.65 = (bf16[864,256]{1,0:T(8,128)(2,1)S(1)}, bf16[864,256]{1,0:T(8,128)(2,1)S(1)}, u32[]{:S(2)}, u32[]{:S(2)}) collective-permute-start(bf16[864,256]{1,0:T(8,128)(2,1)S(1)} %copy-done.47), channel_id=1, source_target_pairs={{0,8},{8,0},{16,24},{24,16},{1,9},{9,1},{17,25},{25,17},{2,10},{10... | collective-permute-start | bytes 1327112 | tf_op jit(solution)/shard_map/ppermute | solution.py:111
  225.6 15.6 %collective-permute-start.74 = (bf16[864,256]{1,0:T(8,128)(2,1)S(1)}, bf16[864,256]{1,0:T(8,128)(2,1)S(1)}, u32[]{:S(2)}, u32[]{:S(2)}) collective-permute-start(bf16[864,256]{1,0:T(8,128)(2,1)S(1)} %fusion.5.refs_2_), channel_id=1, source_target_pairs={{0,8},{8,0},{16,24},{24,16},{1,9},{9,1},{17,25},{25,17},{2,10},{10... | collective-permute-start | bytes 1327112 | tf_op jit(solution)/shard_map/ppermute | solution.py:111
  232.1 16.0 %collective-permute-start.57 = (bf16[864,256]{1,0:T(8,128)(2,1)S(1)}, bf16[864,256]{1,0:T(8,128)(2,1)S(1)}, u32[]{:S(2)}, u32[]{:S(2)}) collective-permute-start(bf16[864,256]{1,0:T(8,128)(2,1)S(1)} %fusion.1.refs_6_), channel_id=1, source_target_pairs={{0,8},{8,0},{16,24},{24,16},{1,9},{9,1},{17,25},{25,17},{2,10},{10... | collective-permute-start | bytes 1327112 | tf_op jit(solution)/shard_map/ppermute | solution.py:111
  232.4 24.7 %collective-permute-start.67 = (bf16[864,256]{1,0:T(8,128)(2,1)S(1)}, bf16[864,256]{1,0:T(8,128)(2,1)S(1)}, u32[]{:S(2)}, u32[]{:S(2)}) collective-permute-start(bf16[864,256]{1,0:T(8,128)(2,1)S(1)} %fusion.3.refs_4_), channel_id=1, source_target_pairs={{0,8},{8,0},{16,24},{24,16},{1,9},{9,1},{17,25},{25,17},{2,10},{10... | collective-permute-start | bytes 1327112 | tf_op jit(solution)/shard_map/ppermute | solution.py:111
  241.3 16.0 %collective-permute-start.75 = (bf16[864,256]{1,0:T(8,128)(2,1)S(1)}, bf16[864,256]{1,0:T(8,128)(2,1)S(1)}, u32[]{:S(2)}, u32[]{:S(2)}) collective-permute-start(bf16[864,256]{1,0:T(8,128)(2,1)S(1)} %add_convert_fusion.3), channel_id=1, source_target_pairs={{8,16},{12,20},{16,8},{20,12},{0,4},{4,0},{24,28},{28,24},{9,17},{... | collective-permute-start | bytes 1327112 | tf_op jit(solution)/shard_map/ppermute | solution.py:115
  257.6 14.8 %collective-permute-start.76 = (bf16[864,256]{1,0:T(8,128)(2,1)S(1)}, bf16[864,256]{1,0:T(8,128)(2,1)S(1)}, u32[]{:S(2)}, u32[]{:S(2)}) collective-permute-start(bf16[864,256]{1,0:T(8,128)(2,1)S(1)} %fusion.6.refs_8_), channel_id=1, source_target_pairs={{0,8},{8,0},{16,24},{24,16},{1,9},{9,1},{17,25},{25,17},{2,10},{10... | collective-permute-start | bytes 1327112 | tf_op jit(solution)/shard_map/ppermute | solution.py:111
  259.9 20.3 %collective-permute-start.59 = (bf16[864,256]{1,0:T(8,128)(2,1)S(1)}, bf16[864,256]{1,0:T(8,128)(2,1)S(1)}, u32[]{:S(2)}, u32[]{:S(2)}) collective-permute-start(bf16[864,256]{1,0:T(8,128)(2,1)S(1)} %fusion.2.refs_12_), channel_id=1, source_target_pairs={{0,8},{8,0},{16,24},{24,16},{1,9},{9,1},{17,25},{25,17},{2,10},{10... | collective-permute-start | bytes 1327112 | tf_op jit(solution)/shard_map/ppermute | solution.py:111
  264.4 24.8 %collective-permute-start.69 = (bf16[864,256]{1,0:T(8,128)(2,1)S(1)}, bf16[864,256]{1,0:T(8,128)(2,1)S(1)}, u32[]{:S(2)}, u32[]{:S(2)}) collective-permute-start(bf16[864,256]{1,0:T(8,128)(2,1)S(1)} %fusion.4.refs_10_), channel_id=1, source_target_pairs={{0,8},{8,0},{16,24},{24,16},{1,9},{9,1},{17,25},{25,17},{2,10},{10... | collective-permute-start | bytes 1327112 | tf_op jit(solution)/shard_map/ppermute | solution.py:111
  272.5 16.8 %collective-permute-start.77 = (bf16[864,256]{1,0:T(8,128)(2,1)S(1)}, bf16[864,256]{1,0:T(8,128)(2,1)S(1)}, u32[]{:S(2)}, u32[]{:S(2)}) collective-permute-start(bf16[864,256]{1,0:T(8,128)(2,1)S(1)} %add_convert_fusion.1), channel_id=1, source_target_pairs={{8,16},{12,20},{16,8},{20,12},{0,4},{4,0},{24,28},{28,24},{9,17},{... | collective-permute-start | bytes 1327112 | tf_op jit(solution)/shard_map/ppermute | solution.py:115
  291.8 18.3 %collective-permute-start.61 = (bf16[512,256]{1,0:T(8,128)(2,1)S(1)}, bf16[512,256]{1,0:T(8,128)(2,1)S(1)}, u32[]{:S(2)}, u32[]{:S(2)}) collective-permute-start(bf16[512,256]{1,0:T(8,128)(2,1)S(1)} %fusion.8.refs_1_), channel_id=1, source_target_pairs={{0,8},{8,0},{16,24},{24,16},{1,9},{9,1},{17,25},{25,17},{2,10},{10... | collective-permute-start | bytes 786440 | tf_op jit(solution)/shard_map/ppermute | solution.py:111
  292.0 21.4 %collective-permute-start.80 = (bf16[512,256]{1,0:T(8,128)(2,1)S(1)}, bf16[512,256]{1,0:T(8,128)(2,1)S(1)}, u32[]{:S(2)}, u32[]{:S(2)}) collective-permute-start(bf16[512,256]{1,0:T(8,128)(2,1)S(1)} %fusion.9.refs_0_), channel_id=1, source_target_pairs={{0,8},{8,0},{16,24},{24,16},{1,9},{9,1},{17,25},{25,17},{2,10},{10... | collective-permute-start | bytes 786440 | tf_op jit(solution)/shard_map/ppermute | solution.py:111
  (150 other events, 1429.9 us)

commit v2 on v1

--- a/solution.py
+++ b/solution.py
@@ -509,82 +509,100 @@
     )
     trips = [trip0] + [col_send(trip0, k) for k in peers()]
 
-    def mix_grad(inf, tr, mx, n1r, ga, gb, out, gm):
+    def mix_grad(inf, n1r, ga, gb, *refs):
+        count = len(refs[:-1]) // 3
+        gm = refs[-1]
         gm[:rows] = ga[...]
         gm[rows:] = gb[...]
-        out[:3 * lanes] = dot(tr[...], n1r[...], 1, 0).astype(bf16)
-        out[3 * lanes:] = dot(mx[...].T, gm[...], 1, 0).astype(bf16)
-
-    for k in K:
-        chunk, = call(
-            mix_grad, info, [trips[k], mixeds[k], n1, gmix[0], gmix_o[0]],
-            [((4 * lanes, width), bf16)], [pltpu.VMEM((group, width), bf16)],
+        for tr, mx, out in zip(refs[:count], refs[count:2 * count], refs[2 * count:-1]):
+            out[:3 * lanes] = dot(tr[...], n1r[...], 1, 0).astype(bf16)
+            out[3 * lanes:] = dot(mx[...].T, gm[...], 1, 0).astype(bf16)
+
+    for part in (slice(0, 1), slice(1, n_col)):
+        chunks += call(
+            mix_grad, info, [n1, gmix[0], gmix_o[0]] + trips[part] + mixeds[part],
+            [((4 * lanes, width), bf16)] * len(trips[part]), [pltpu.VMEM((group, width), bf16)],
         )
-        chunks.append(chunk)
 
     came1 = row_send(sent1)
     own1, rs1, *send1 = call(fold(0), info, [mine1, came1, tok, gains], fold_outs)
     got1 = [col_send(s, k + 1) for k, s in enumerate(send1)]
 
-    def last(inf, own, rs, tk, gn, gmid, *refs):
+    def last(inf, own, rs, tk, gn, gmid, gtwo, *refs):
         came, (out, gain) = refs[:n_col - 1], refs[n_col - 1:]
         total, mean = unfold(own, rs, came)
         full = tk[:rows]
         scale = lax.rsqrt(jnp.sum(full * full, axis=1, keepdims=True) / model + epsilon)
         part = tk[:rows, :width]
         out[...] = gmid[...] + scale * (gn[0:1, :width] * total) - part * (scale * scale * scale) * (mean / model)
-        gain[...] = jnp.broadcast_to(jnp.sum(total * part * scale, axis=0, keepdims=True), (8, width))
-
-    in_grad, gain_one = call(
-        last, info, [own1, rs1, tok, gains, grad_mid] + got1,
+        gain[...] = gtwo[...]
+        gain[0:1] = jnp.sum(total * part * scale, axis=0, keepdims=True)
+
+    in_grad, gain_pair = call(
+        last, info, [own1, rs1, tok, gains, grad_mid, gain_two] + got1,
         [((rows, width), f32), ((8, width), f32)],
     )
 
-    def ffn_out(inf, dw, hid, *refs):
-        pcs, (mine, sent) = refs[:n_col], refs[n_col:]
+    gain_came = row_send(gain_pair)
+
+    def ffn_out(inf, dw, hid, ga, gb, tg, *refs):
+        pcs, (mine, sent, small) = refs[:n_col], refs[n_col:]
         acc = jnp.zeros((group, width), f32)
         for k in K:
             at = pl.ds(pl.multiple_of((inf[0] ^ k) * ff, 32), ff)
             acc = acc + dot(pcs[k][:ff].T, dw[at, :], 1, 0)
         mine[...] = acc[:rows] + hid[:rows, :width]
         sent[...] = acc[rows:]
-
-    out_mine, out_sent = call(
-        ffn_out, info, [down_weight, hidden] + pieces,
-        [((rows, width), f32)] * 2,
-    )
-    block_out = out_mine + row_send(out_sent)
-
-    gain_pair = jnp.concatenate([gain_one[:1], gain_two[:1]], axis=0)
-    gain_pair = gain_pair + row_send(gain_pair)
-    taps = jnp.pad(taps_grad[:3], ((0, 0), (0, width - lanes)))
-    chunks.append(jnp.pad(jnp.concatenate([gain_pair, taps], axis=0), ((0, 11), (0, 0))).astype(bf16))
+        wide = jnp.concatenate([tg[...], jnp.zeros((8, width - lanes), f32)], axis=1) if width > lanes else tg[...]
+        small[...] = jnp.concatenate([ga[...] + gb[...], wide], axis=0).astype(bf16)
+
+    out_mine, out_sent, small = call(
+        ffn_out, info, [down_weight, hidden, gain_pair, gain_came, taps_grad] + pieces,
+        [((rows, width), f32)] * 2 + [((16, width), bf16)],
+    )
+    out_came = row_send(out_sent)
+
+    chunks.append(small)
     sums = dp_sums(chunks)
-    small = jnp.where(info[3] == 1, sums[-1][1], sums[-1][0]).astype(f32)
+
+    def place_down(inf, *refs):
+        parts, (oa, ob, down, out) = refs[:2 * n_col], refs[2 * n_col:]
+        out[...] = oa[...] + ob[...]
+        for k in K:
+            at = pl.ds(pl.multiple_of((inf[0] ^ k) * ff, 32), ff)
+            down[at, :] = jnp.where(inf[3] == 1, parts[2 * k + 1][:ff], parts[2 * k][:ff]).astype(f32)
+
+    down_sum, block_out = call(
+        place_down, info, [x for s in sums[:2 * n_col:2] for x in s] + [out_mine, out_came],
+        [((hidden_ff, width), f32), ((rows, width), f32)],
+    )
 
     def ffn_place(inf, *refs):
-        parts, (gate, up, down, whole, gt, ut) = refs[:4 * n_col], refs[4 * n_col:]
+        parts, (gate, up, gt, ut) = refs[:4 * n_col], refs[4 * n_col:]
         far = inf[3] == 1
         for k in K:
             ha, ca, hb, cb = parts[4 * k:4 * k + 4]
-            whole[:cut] = jnp.where(far, ca[:cut], ha[:cut])
-            whole[cut:] = jnp.where(far, cb[:cut], hb[:cut])
-            at = pl.ds(pl.multiple_of((inf[0] ^ k) * ff, 32), ff)
-            for i, dest in enumerate((down, gt, ut)):
-                dest[at, :] = whole[i * ff:(i + 1) * ff].astype(dest.dtype)
+            at = (inf[0] ^ k) * ff
+            near = cut - ff
+            gt[pl.ds(pl.multiple_of(at, 32), near), :] = jnp.where(far, ca[ff:cut], ha[ff:cut])
+            gt[pl.ds(pl.multiple_of(at + near, 32), ff - near), :] = jnp.where(far, cb[:ff - near], hb[:ff - near])
+            ut[pl.ds(pl.multiple_of(at, 32), ff), :] = jnp.where(far, cb[ff - near:cut], hb[ff - near:cut])
         gate[...] = gt[...].T.astype(f32)
         up[...] = ut[...].T.astype(f32)
 
-    gate_sum, up_sum, down_sum = call(
+    gate_sum, up_sum = call(
         ffn_place, info, [x for s in sums[:2 * n_col] for x in s],
-        [((width, hidden_ff), f32)] * 2 + [((hidden_ff, width), f32)],
-        [pltpu.VMEM((3 * ff, width), bf16)] + [pltpu.VMEM((hidden_ff, width), bf16)] * 2,
+        [((width, hidden_ff), f32)] * 2, [pltpu.VMEM((hidden_ff, width), bf16)] * 2,
     )
 
     def mix_place(inf, *refs):
-        held_refs, came_refs = refs[:n_col], refs[n_col:2 * n_col]
-        win, wout = refs[2 * n_col:]
+        held_refs, came_refs = refs[:n_col], refs[n_col + 1:2 * n_col + 1]
+        win, wout, g1, g2, tg = refs[2 * n_col + 2:]
         far = inf[3] == 1
+        small = jnp.where(far, refs[2 * n_col + 1][...], refs[n_col][...]).astype(f32)
+        g1[...] = small[0:1]
+        g2[...] = small[1:2]
+        tg[...] = small[8:11, :lanes]
         for k in K:
             at = pl.ds(pl.multiple_of((inf[0] ^ k) * lanes, lanes), lanes)
             for t in range(4):
@@ -595,18 +613,18 @@
                 else:
                     wout[at, :] = got.astype(f32)
 
-    in_sum, out_sum = call(
-        mix_place, info, [s[0] for s in sums[2 * n_col:-1]] + [s[1] for s in sums[2 * n_col:-1]],
-        [((3, width, span), f32), ((span, width), f32)],
+    in_sum, out_sum, small_one, small_two, small_taps = call(
+        mix_place, info, [s[0] for s in sums[2 * n_col:]] + [s[1] for s in sums[2 * n_col:]],
+        [((3, width, span), f32), ((span, width), f32)] + [((1, width), f32)] * 2 + [((3, lanes), f32)],
     )
     return (
         block_out,
         in_grad,
-        small[0],
+        small_one.reshape(width),
         jnp.transpose(in_sum, (1, 0, 2)),
-        small[2:5, :lanes],
+        small_taps,
         out_sum,
-        small[1],
+        small_two.reshape(width),
         gate_sum,
         up_sum,
         down_sum,

time: 333 us -> 328 us (0.985)
  starting transfers between devices: 97.4 us -> 106 us
  waiting for transfers between devices: 145 us -> 138 us
  local copies, waits for them, and re-layouts: 13.7 us -> 9.38 us
    ppermute x16, starting transfers between devices: 44.8 us -> 55.8 us  [dp_sums(): came = lax.ppermute(sent, 'dp', ends)]
    ppermute x16, waiting for transfers between devices: 52.4 us -> 47.4 us  [dp_sums(): came = lax.ppermute(sent, 'dp', ends)]
    unnamed x196 -> x208, local copies, waits for them, and re-layouts: 10.3 us -> 8.58 us
    pallas_call x22 -> x21, Pallas kernels: 68.1 us -> 67.2 us  [call(): pl.pallas_call(body, out_shape=[jax.ShapeDtypeStruct(s, t) for s, t in ou...]
  transfers between devices with their start and end apart: 84 -> 84, of which waited for: 32 -> 29; matrix products, arithmetic and copies ran while one was open for 3% -> 2% of each run, Pallas kernels for 16% -> 16%
where the time goes in v2:
time: 328 us
  waiting for transfers between devices  138 us (42%)
  starting transfers between devices  106 us (32%)
  Pallas kernels  67.2 us (20%)
  local copies, waits for them, and re-layouts  9.38 us (3%)
  other arithmetic  5.4 us (2%)
    ppermute x33, waiting for transfers between devices, col_send(): return lax.ppermute(piece, 'col', [(i, i ^ k) for i in range(n)])  75.7 us
    pallas_call x21, Pallas kernels, call(): pl.pallas_call(body, out_shape=[jax.ShapeDtypeStruct(s, t) for s, t in ou...  67.2 us
    ppermute x16, starting transfers between devices, dp_sums(): came = lax.ppermute(sent, 'dp', ends)  55.8 us
    ppermute x16, waiting for transfers between devices, dp_sums(): came = lax.ppermute(sent, 'dp', ends)  47.4 us
    ppermute x33, starting transfers between devices, col_send(): return lax.ppermute(piece, 'col', [(i, i ^ k) for i in range(n)])  41.6 us
    ppermute x5, waiting for transfers between devices, pair_send(): return lax.ppermute(piece, 'dp', [(i, i ^ 1) for i in range(n)])  13.2 us
    unnamed x208, local copies, waits for them, and re-layouts  8.58 us
  transfers between devices with their start and end apart: 84, of which 29 were waited for; matrix products, arithmetic and copies ran while one was open for 2% of the time, Pallas kernels for 16%

profile of v2, /device:TPU:0, one launch (start us, length us, event | category | flops | bytes accessed | tf_op | source)
XLA Modules:
  0.0 327.8 jit_solution(18423623548219914603)
XLA Ops:
  0.6 4.0 %collective-permute-start.2 = (f32[128,256]{1,0:T(8,128)}, f32[128,256]{1,0:T(8,128)S(1)}, u32[]{:S(2)}, u32[]{:S(2)}) collective-permute-start(f32[128,256]{1,0:T(8,128)} %refs_0_.1), channel_id=1, source_target_pairs={{0,3},{1,2},{2,1},{3,0},{4,7},{5,6},{6,5},{7,4},{8,11},{9,10},{10,... | collective-permute-start | bytes 393224 | tf_op jit(solution)/shard_map/ppermute | solution.py:43
  13.0 4.3 %shard_map.188 = (bf16[256,256]{1,0:T(8,128)(2,1)}, bf16[576,256]{1,0:T(8,128)(2,1)}, bf16[576,256]{1,0:T(8,128)(2,1)}, bf16[576,256]{1,0:T(8,128)(2,1)}, bf16[1...) custom-call(s32[4]{0:T(128)} %pad_add_fusion.inf, ...), custom_call_target="tpu_custom_call" | custom-call | flops 100000000 | bytes 3932160 | tf_op jit(solution)/shard_map/pallas_call | solution.py:24
  20.2 3.2 collective-permute-done.15.refs_7_.refs_11_
  47.6 4.6 %collective-permute-done.26.refs_3_.refs_11_ = bf16[416,256]{1,0:T(8,128)(2,1)S(1)} collective-permute-done((bf16[416,256]{1,0:T(8,128)(2,1)S(1)}, bf16[416,256]{1,0:T(8,128)(2,1)S(1)}, u32[]{:S(2)}, u32[]{:S(2)}) %collective-permute-start.26) | collective-permute-done | bytes 213024 | tf_op jit(solution)/shard_map/ppermute | solution.py:43
  53.9 4.3 %collective-permute-done.18.refs_1_ = bf16[576,256]{1,0:T(8,128)(2,1)S(1)} collective-permute-done((bf16[576,256]{1,0:T(8,128)(2,1)S(1)}, bf16[576,256]{1,0:T(8,128)(2,1)S(1)}, u32[]{:S(2)}, u32[]{:S(2)}) %collective-permute-start.18) | collective-permute-done | bytes 294944 | tf_op jit(solution)/shard_map/ppermute | solution.py:43
  59.5 12.6 %collective-permute-done.20.refs_3_ = bf16[576,256]{1,0:T(8,128)(2,1)S(1)} collective-permute-done((bf16[576,256]{1,0:T(8,128)(2,1)S(1)}, bf16[576,256]{1,0:T(8,128)(2,1)S(1)}, u32[]{:S(2)}, u32[]{:S(2)}) %collective-permute-start.20) | collective-permute-done | bytes 294944 | tf_op jit(solution)/shard_map/ppermute | solution.py:43
  74.6 7.3 %collective-permute-done.22.refs_6_ = bf16[576,256]{1,0:T(8,128)(2,1)S(1)} collective-permute-done((bf16[576,256]{1,0:T(8,128)(2,1)S(1)}, bf16[576,256]{1,0:T(8,128)(2,1)S(1)}, u32[]{:S(2)}, u32[]{:S(2)}) %collective-permute-start.22) | collective-permute-done | bytes 294944 | tf_op jit(solution)/shard_map/ppermute | solution.py:55
  82.4 5.9 %collective-permute-done.23.refs_7_ = bf16[576,256]{1,0:T(8,128)(2,1)S(1)} collective-permute-done((bf16[576,256]{1,0:T(8,128)(2,1)S(1)}, bf16[576,256]{1,0:T(8,128)(2,1)S(1)}, u32[]{:S(2)}, u32[]{:S(2)}) %collective-permute-start.23) | collective-permute-done | bytes 294944 | tf_op jit(solution)/shard_map/ppermute | solution.py:55
  89.4 4.7 %shard_map.190 = (f32[256,1024]{1,0:T(8,128)}, f32[576,256]{1,0:T(8,128)}, f32[576,256]{1,0:T(8,128)}, bf16[576,256]{1,0:T(8,128)(2,1)}, bf16[256,256]{1,0:T(8,128)(2,1)}) custom-call(s32[4]{0:T(128)} %pad_add_fusion.inf, f32[256,1024]{1,0:T(8,128)} %get-tuple-element.84.tk.act_in, f32[8,1024]{1,0:T(8,128)} %get-tuple-element.85.gn, ...), custom_call_target="tpu_custom_call" | custom-call | flops 2000000000 | bytes 5537792 | tf_op jit(solution)/shard_map/pallas_call | solution.py:24
  95.1 4.7 %shard_map.191 = (bf16[1728,256]{1,0:T(8,128)(2,1)}, bf16[864,256]{1,0:T(8,128)(2,1)}, bf16[864,256]{1,0:T(8,128)(2,1)}) custom-call(s32[4]{0:T(128)} %pad_add_fusion.inf, f32[576,256]{1,0:T(8,128)} %get-tuple-element.93.gpr, f32[576,256]{1,0:T(8,128)} %get-tuple-element.94.upr, bf16[576,256]{1,0:T(8,128)(2,1)} %get-tuple-element.95.act_ref, ...), custom_call_target="tpu_custom_call" | custom-call | flops 2000000000 | bytes 5046272 | tf_op jit(solution)/shard_map/pallas_call | solution.py:24
  99.7 3.8 %shard_map.195 = (f32[128,1024]{1,0:T(8,128)}, bf16[128,1024]{1,0:T(8,128)(2,1)}) custom-call(s32[4]{0:T(128)} %pad_add_fusion.inf, bf16[1728,256]{1,0:T(8,128)(2,1)} %get-tuple-element.102.pc.refs_0_, bf16[576,256]{1,0:T(8,128)(2,1)} %get-tuple-element.88.refs_0_, bf16[576,256]{1,0:T(8,128)(2,1)} %copy-done.93, bf16[576,256]{1,0:T(8,128)(2,1)} %copy-done.94, ...), custom_call_target="tpu_custom_call" | custom-call | flops 1000000000 | bytes 3244032 | tf_op jit(solution)/shard_map/pallas_call | solution.py:24
  111.9 16.1 %collective-permute-done.47.refs_0_ = bf16[144,256]{1,0:T(8,128)(2,1)S(1)} collective-permute-done((bf16[144,256]{1,0:T(8,128)(2,1)}, bf16[144,256]{1,0:T(8,128)(2,1)S(1)}, u32[]{:S(2)}, u32[]{:S(2)}) %collective-permute-start.47) | collective-permute-done | bytes 73760 | tf_op jit(solution)/shard_map/ppermute | solution.py:43
  141.3 3.6 %shard_map.198 = (bf16[384,256]{1,0:T(8,128)(2,1)}, f32[128,1024]{1,0:T(8,128)}, bf16[128,1024]{1,0:T(8,128)(2,1)}, f32[8,128]{1,0:T(8,128)}) custom-call(s32[4]{0:T(128)} %pad_add_fusion.inf, s32[256,1]{1,0:T(8,128)} %copy.21.sg, f32[3,128]{1,0:T(4,128)} %taps.3, f32[256,384]{1,0:T(8,128)} %get-tuple-element.120.m3, ...), custom_call_target="tpu_custom_call" | custom-call | flops 100000000 | bytes 2804224 | tf_op jit(solution)/shard_map/pallas_call | solution.py:24
  159.2 7.9 %collective-permute-done.41 = bf16[864,256]{1,0:T(8,128)(2,1)S(1)} collective-permute-done((bf16[864,256]{1,0:T(8,128)(2,1)S(1)}, bf16[864,256]{1,0:T(8,128)(2,1)S(1)}, u32[]{:S(2)}, u32[]{:S(2)}) %collective-permute-start.41) | collective-permute-done | bytes 442400 | tf_op jit(solution)/shard_map/ppermute | solution.py:111
  172.3 26.4 %collective-permute-done.66.refs_1_ = bf16[144,256]{1,0:T(8,128)(2,1)S(1)} collective-permute-done((bf16[144,256]{1,0:T(8,128)(2,1)}, bf16[144,256]{1,0:T(8,128)(2,1)S(1)}, u32[]{:S(2)}, u32[]{:S(2)}) %collective-permute-start.66) | collective-permute-done | bytes 73760 | tf_op jit(solution)/shard_map/ppermute | solution.py:43
  214.9 4.3 %collective-permute-start.43 = (bf16[864,256]{1,0:T(8,128)(2,1)S(1)}, bf16[864,256]{1,0:T(8,128)(2,1)S(1)}, u32[]{:S(2)}, u32[]{:S(2)}) collective-permute-start(bf16[864,256]{1,0:T(8,128)(2,1)S(1)} %fusion.2.refs_2_), channel_id=1, source_target_pairs={{0,8},{8,0},{16,24},{24,16},{1,9},{9,1},{17,25},{25,17},{2,10},{10... | collective-permute-start | bytes 1327112 | tf_op jit(solution)/shard_map/ppermute | solution.py:111
  220.1 4.0 %shard_map.202 = (f32[128,256]{1,0:T(8,128)}, f32[128,256]{1,0:T(8,128)}, bf16[16,256]{1,0:T(8,128)(2,1)}) custom-call(s32[4]{0:T(128)} %pad_add_fusion.inf, bf16[2304,256]{1,0:T(8,128)(2,1)} %dw.3, f32[256,1024]{1,0:T(8,128)} %get-tuple-element.113.act_in.hid_ref.hid, f32[8,256]{1,0:T(8,128)} %get-tuple-element.133.ga, f32[8,256]{1,0:T(8,128)} %copy-done.80, ...), custom_call_target="tpu_custom_call" | custom-call | flops 100000000 | bytes 5787648 | tf_op jit(solution)/shard_map/pallas_call | solution.py:24
  227.9 3.7 %collective-permute-done.43.refs_3_ = bf16[864,256]{1,0:T(8,128)(2,1)S(1)} collective-permute-done((bf16[864,256]{1,0:T(8,128)(2,1)S(1)}, bf16[864,256]{1,0:T(8,128)(2,1)S(1)}, u32[]{:S(2)}, u32[]{:S(2)}) %collective-permute-start.43) | collective-permute-done | bytes 442400 | tf_op jit(solution)/shard_map/ppermute | solution.py:111
  231.8 8.8 %collective-permute-done.39.refs_3_.refs_5_ = bf16[864,256]{1,0:T(8,128)(2,1)S(1)} collective-permute-done((bf16[864,256]{1,0:T(8,128)(2,1)S(1)}, bf16[864,256]{1,0:T(8,128)(2,1)S(1)}, u32[]{:S(2)}, u32[]{:S(2)}) %collective-permute-start.39) | collective-permute-done | bytes 442400 | tf_op jit(solution)/shard_map/ppermute | solution.py:111
  241.0 3.4 %collective-permute-start.61 = (bf16[864,256]{1,0:T(8,128)(2,1)S(1)}, bf16[864,256]{1,0:T(8,128)(2,1)S(1)}, u32[]{:S(2)}, u32[]{:S(2)}) collective-permute-start(bf16[864,256]{1,0:T(8,128)(2,1)S(1)} %fusion.4.refs_6_), channel_id=1, source_target_pairs={{0,8},{8,0},{16,24},{24,16},{1,9},{9,1},{17,25},{25,17},{2,10},{10... | collective-permute-start | bytes 1327112 | tf_op jit(solution)/shard_map/ppermute | solution.py:111
  244.7 7.3 %collective-permute-start.45 = (bf16[864,256]{1,0:T(8,128)(2,1)S(1)}, bf16[864,256]{1,0:T(8,128)(2,1)S(1)}, u32[]{:S(2)}, u32[]{:S(2)}) collective-permute-start(bf16[864,256]{1,0:T(8,128)(2,1)S(1)} %fusion.3.refs_4_.refs_8_), channel_id=1, source_target_pairs={{0,8},{8,0},{16,24},{24,16},{1,9},{9,1},{17,25},{25,17},{2,10},{10... | collective-permute-start | bytes 1327112 | tf_op jit(solution)/shard_map/ppermute | solution.py:111
  252.1 8.8 %collective-permute-start.71 = (bf16[864,256]{1,0:T(8,128)(2,1)S(1)}, bf16[864,256]{1,0:T(8,128)(2,1)S(1)}, u32[]{:S(2)}, u32[]{:S(2)}) collective-permute-start(bf16[864,256]{1,0:T(8,128)(2,1)S(1)} %fusion.6.refs_10_), channel_id=1, source_target_pairs={{0,8},{8,0},{16,24},{24,16},{1,9},{9,1},{17,25},{25,17},{2,10},{10... | collective-permute-start | bytes 1327112 | tf_op jit(solution)/shard_map/ppermute | solution.py:111
  261.2 3.8 %collective-permute-done.45.refs_5_.refs_9_ = bf16[864,256]{1,0:T(8,128)(2,1)S(1)} collective-permute-done((bf16[864,256]{1,0:T(8,128)(2,1)S(1)}, bf16[864,256]{1,0:T(8,128)(2,1)S(1)}, u32[]{:S(2)}, u32[]{:S(2)}) %collective-permute-start.45) | collective-permute-done | bytes 442400 | tf_op jit(solution)/shard_map/ppermute | solution.py:111
  265.2 7.7 %collective-permute-done.71.refs_11_ = bf16[864,256]{1,0:T(8,128)(2,1)S(1)} collective-permute-done((bf16[864,256]{1,0:T(8,128)(2,1)S(1)}, bf16[864,256]{1,0:T(8,128)(2,1)S(1)}, u32[]{:S(2)}, u32[]{:S(2)}) %collective-permute-start.71) | collective-permute-done | bytes 442400 | tf_op jit(solution)/shard_map/ppermute | solution.py:111
  275.5 8.4 %collective-permute-start.75 = (bf16[864,256]{1,0:T(8,128)(2,1)S(1)}, bf16[864,256]{1,0:T(8,128)(2,1)S(1)}, u32[]{:S(2)}, u32[]{:S(2)}) collective-permute-start(bf16[864,256]{1,0:T(8,128)(2,1)S(1)} %fusion.7.refs_14_), channel_id=1, source_target_pairs={{0,8},{8,0},{16,24},{24,16},{1,9},{9,1},{17,25},{25,17},{2,10},{10... | collective-permute-start | bytes 1327112 | tf_op jit(solution)/shard_map/ppermute | solution.py:111
  284.1 4.1 %collective-permute-start.77 = (bf16[512,256]{1,0:T(8,128)(2,1)S(1)}, bf16[512,256]{1,0:T(8,128)(2,1)S(1)}, u32[]{:S(2)}, u32[]{:S(2)}) collective-permute-start(bf16[512,256]{1,0:T(8,128)(2,1)S(1)} %fusion.8.refs_0_), channel_id=1, source_target_pairs={{0,8},{8,0},{16,24},{24,16},{1,9},{9,1},{17,25},{25,17},{2,10},{10... | collective-permute-start | bytes 786440 | tf_op jit(solution)/shard_map/ppermute | solution.py:111
  288.3 7.5 %collective-permute-done.75.refs_15_ = bf16[864,256]{1,0:T(8,128)(2,1)S(1)} collective-permute-done((bf16[864,256]{1,0:T(8,128)(2,1)S(1)}, bf16[864,256]{1,0:T(8,128)(2,1)S(1)}, u32[]{:S(2)}, u32[]{:S(2)}) %collective-permute-start.75) | collective-permute-done | bytes 442400 | tf_op jit(solution)/shard_map/ppermute | solution.py:111
  296.0 4.9 %collective-permute-done.77.refs_5_ = bf16[512,256]{1,0:T(8,128)(2,1)S(1)} collective-permute-done((bf16[512,256]{1,0:T(8,128)(2,1)S(1)}, bf16[512,256]{1,0:T(8,128)(2,1)S(1)}, u32[]{:S(2)}, u32[]{:S(2)}) %collective-permute-start.77) | collective-permute-done | bytes 262176 | tf_op jit(solution)/shard_map/ppermute | solution.py:111
  306.2 3.9 %collective-permute-start.82 = (bf16[512,256]{1,0:T(8,128)(2,1)S(1)}, bf16[512,256]{1,0:T(8,128)(2,1)S(1)}, u32[]{:S(2)}, u32[]{:S(2)}) collective-permute-start(bf16[512,256]{1,0:T(8,128)(2,1)S(1)} %add_convert_fusion.16.refs_3_), channel_id=1, source_target_pairs={{0,8},{8,0},{16,24},{24,16},{1,9},{9,1},{17,25},{25,17},{2,10},{10... | collective-permute-start | bytes 786440 | tf_op jit(solution)/shard_map/ppermute | solution.py:111
  310.5 5.8 %shard_map.206 = (f32[256,2304]{1,0:T(8,128)}, f32[256,2304]{1,0:T(8,128)}) custom-call(s32[4]{0:T(128)} %pad_add_fusion.inf, bf16[864,256]{1,0:T(8,128)(2,1)} %copy-done.1, bf16[864,256]{1,0:T(8,128)(2,1)} %copy-done.2, bf16[864,256]{1,0:T(8,128)(2,1)} %copy-done.15, bf16[864,256]{1,0:T(8,128)(2,1)} %copy-done.16, bf16[864,256]{1,0:T(8,128)(2,1)} %copy-done.3, ...), custom_call_target="tpu_custom_call" | custom-call | flops 100000000 | bytes 7077888 | tf_op jit(solution)/shard_map/pallas_call | solution.py:24
  319.6 3.7 %shard_map.203 = (f32[2304,256]{1,0:T(8,128)}, f32[128,256]{1,0:T(8,128)}) custom-call(s32[4]{0:T(128)} %pad_add_fusion.inf, bf16[864,256]{1,0:T(8,128)(2,1)} %copy-done.1, bf16[864,256]{1,0:T(8,128)(2,1)} %copy-done.2, bf16[864,256]{1,0:T(8,128)(2,1)} %copy-done.3, bf16[864,256]{1,0:T(8,128)(2,1)} %copy-done.4, bf16[864,256]{1,0:T(8,128)(2,1)} %copy-done.5, ...), custom_call_target="tpu_custom_call" | custom-call | flops 100000000 | bytes 3801088 | tf_op jit(solution)/shard_map/pallas_call | solution.py:24
  324.7 3.1 shard_map.205
  (393 shorter events, 119.5 us)
Async XLA Ops:
  8.1 16.8 %collective-permute-start.7 = (bf16[272,384]{1,0:T(8,128)(2,1)}, bf16[272,384]{1,0:T(8,128)(2,1)S(1)}, u32[]{:S(2)}, u32[]{:S(2)}) collective-permute-start(bf16[272,384]{1,0:T(8,128)(2,1)} %get-tuple-element.81), channel_id=1, source_target_pairs={{0,1},{1,0},{2,3},{3,2},{4,5},{5,4},{6,7},{7,6},{8,9},{9,8},{10,11... | collective-permute-start | bytes 626696 | tf_op jit(solution)/shard_map/ppermute | solution.py:43
  19.0 15.7 %collective-permute-start.14 = (bf16[512,256]{1,0:T(8,128)(2,1)S(1)}, bf16[512,256]{1,0:T(8,128)(2,1)S(1)}, u32[]{:S(2)}, u32[]{:S(2)}) collective-permute-start(bf16[512,256]{1,0:T(8,128)(2,1)S(1)} %copy-done.11), channel_id=1, source_target_pairs={{0,2},{1,3},{2,0},{3,1},{4,6},{5,7},{6,4},{7,5},{8,10},{9,11},{10,... | collective-permute-start | bytes 786440 | tf_op jit(solution)/shard_map/ppermute | solution.py:43
  43.0 45.3 %collective-permute-start.17 = (f32[256,1024]{1,0:T(8,128)}, f32[256,1024]{1,0:T(8,128)S(1)}, u32[]{:S(2)}, u32[]{:S(2)}) collective-permute-start(f32[256,1024]{1,0:T(8,128)} %shard_map.189.mine), channel_id=1, source_target_pairs={{0,4},{4,0},{1,5},{5,1},{2,6},{6,2},{3,7},{7,3},{8,12},{12,8},{9,1... | collective-permute-start | bytes 3145736 | tf_op jit(solution)/shard_map/ppermute | solution.py:49
  46.6 26.0 %collective-permute-start.24 = (bf16[704,256]{1,0:T(8,128)(2,1)S(1)}, bf16[704,256]{1,0:T(8,128)(2,1)S(1)}, u32[]{:S(2)}, u32[]{:S(2)}) collective-permute-start(bf16[704,256]{1,0:T(8,128)(2,1)S(1)} %copy-done.85), channel_id=1, source_target_pairs={{0,1},{1,0},{2,3},{3,2},{4,5},{5,4},{6,7},{7,6},{8,9},{9,8},{10,11... | collective-permute-start | bytes 1081352 | tf_op jit(solution)/shard_map/ppermute | solution.py:43
  52.1 19.9 %collective-permute-start.20 = (bf16[576,256]{1,0:T(8,128)(2,1)S(1)}, bf16[576,256]{1,0:T(8,128)(2,1)S(1)}, u32[]{:S(2)}, u32[]{:S(2)}) collective-permute-start(bf16[576,256]{1,0:T(8,128)(2,1)S(1)} %copy-done.90), channel_id=1, source_target_pairs={{0,3},{1,2},{2,1},{3,0},{4,7},{5,6},{6,5},{7,4},{8,11},{9,10},{10,... | collective-permute-start | bytes 884744 | tf_op jit(solution)/shard_map/ppermute | solution.py:43
  58.2 15.9 %collective-permute-start.25 = (bf16[704,256]{1,0:T(8,128)(2,1)S(1)}, bf16[704,256]{1,0:T(8,128)(2,1)S(1)}, u32[]{:S(2)}, u32[]{:S(2)}) collective-permute-start(bf16[704,256]{1,0:T(8,128)(2,1)S(1)} %copy-done.84), channel_id=1, source_target_pairs={{0,2},{1,3},{2,0},{3,1},{4,6},{5,7},{6,4},{7,5},{8,10},{9,11},{10,... | collective-permute-start | bytes 1081352 | tf_op jit(solution)/shard_map/ppermute | solution.py:43
  72.5 15.7 %collective-permute-start.23 = (bf16[576,256]{1,0:T(8,128)(2,1)S(1)}, bf16[576,256]{1,0:T(8,128)(2,1)S(1)}, u32[]{:S(2)}, u32[]{:S(2)}) collective-permute-start(bf16[576,256]{1,0:T(8,128)(2,1)S(1)} %collective-permute-done.20.refs_3_), channel_id=1, source_target_pairs={{0,8},{8,0},{16,24},{24,16},{1,9},{9,1},{17,25},{25,17},{2,10},{10... | collective-permute-start | bytes 884744 | tf_op jit(solution)/shard_map/ppermute | solution.py:55
  74.1 20.0 %collective-permute-start.28 = (bf16[704,256]{1,0:T(8,128)(2,1)S(1)}, bf16[704,256]{1,0:T(8,128)(2,1)S(1)}, u32[]{:S(2)}, u32[]{:S(2)}) collective-permute-start(bf16[704,256]{1,0:T(8,128)(2,1)S(1)} %collective-permute-done.24.refs_1_.refs_9_), channel_id=1, source_target_pairs={{0,4},{4,0},{1,5},{5,1},{2,6},{6,2},{3,7},{7,3},{8,12},{12,8},{9,1... | collective-permute-start | bytes 1081352 | tf_op jit(solution)/shard_map/ppermute | solution.py:49
  74.2 20.0 %collective-permute-start.29 = (bf16[704,256]{1,0:T(8,128)(2,1)S(1)}, bf16[704,256]{1,0:T(8,128)(2,1)S(1)}, u32[]{:S(2)}, u32[]{:S(2)}) collective-permute-start(bf16[704,256]{1,0:T(8,128)(2,1)S(1)} %collective-permute-done.25.refs_2_.refs_10_), channel_id=1, source_target_pairs={{0,4},{4,0},{1,5},{5,1},{2,6},{6,2},{3,7},{7,3},{8,12},{12,8},{9,1... | collective-permute-start | bytes 1081352 | tf_op jit(solution)/shard_map/ppermute | solution.py:49
  103.9 48.1 %collective-permute-start.32 = (bf16[1728,256]{1,0:T(8,128)(2,1)S(1)}, bf16[1728,256]{1,0:T(8,128)(2,1)S(1)}, u32[]{:S(2)}, u32[]{:S(2)}) collective-permute-start(bf16[1728,256]{1,0:T(8,128)(2,1)S(1)} %copy-done.36), channel_id=1, source_target_pairs={{0,1},{1,0},{2,3},{3,2},{4,5},{5,4},{6,7},{7,6},{8,9},{9,8},{10,11... | collective-permute-start | bytes 2654216 | tf_op jit(solution)/shard_map/ppermute | solution.py:43
  108.4 19.6 %collective-permute-start.47 = (bf16[144,256]{1,0:T(8,128)(2,1)}, bf16[144,256]{1,0:T(8,128)(2,1)S(1)}, u32[]{:S(2)}, u32[]{:S(2)}) collective-permute-start(bf16[144,256]{1,0:T(8,128)(2,1)} %get-tuple-element.116), channel_id=1, source_target_pairs={{0,1},{1,0},{2,3},{3,2},{4,5},{5,4},{6,7},{7,6},{8,9},{9,8},{10,11... | collective-permute-start | bytes 221192 | tf_op jit(solution)/shard_map/ppermute | solution.py:43
  109.4 18.6 %collective-permute-start.48 = (bf16[144,256]{1,0:T(8,128)(2,1)}, bf16[144,256]{1,0:T(8,128)(2,1)S(1)}, u32[]{:S(2)}, u32[]{:S(2)}) collective-permute-start(bf16[144,256]{1,0:T(8,128)(2,1)} %get-tuple-element.117), channel_id=1, source_target_pairs={{0,2},{1,3},{2,0},{3,1},{4,6},{5,7},{6,4},{7,5},{8,10},{9,11},{10,... | collective-permute-start | bytes 221192 | tf_op jit(solution)/shard_map/ppermute | solution.py:43
  110.7 18.6 %collective-permute-start.49 = (bf16[144,256]{1,0:T(8,128)(2,1)}, bf16[144,256]{1,0:T(8,128)(2,1)S(1)}, u32[]{:S(2)}, u32[]{:S(2)}) collective-permute-start(bf16[144,256]{1,0:T(8,128)(2,1)} %get-tuple-element.118), channel_id=1, source_target_pairs={{0,3},{1,2},{2,1},{3,0},{4,7},{5,6},{6,5},{7,4},{8,11},{9,10},{10,... | collective-permute-start | bytes 221192 | tf_op jit(solution)/shard_map/ppermute | solution.py:43
  145.7 21.4 %collective-permute-start.41 = (bf16[864,256]{1,0:T(8,128)(2,1)S(1)}, bf16[864,256]{1,0:T(8,128)(2,1)S(1)}, u32[]{:S(2)}, u32[]{:S(2)}) collective-permute-start(bf16[864,256]{1,0:T(8,128)(2,1)S(1)} %copy-done.45), channel_id=1, source_target_pairs={{0,8},{8,0},{16,24},{24,16},{1,9},{9,1},{17,25},{25,17},{2,10},{10... | collective-permute-start | bytes 1327112 | tf_op jit(solution)/shard_map/ppermute | solution.py:111
  147.2 20.8 %collective-permute-start.59 = (bf16[384,256]{1,0:T(8,128)(2,1)}, bf16[384,256]{1,0:T(8,128)(2,1)}, u32[]{:S(2)}, u32[]{:S(2)}) collective-permute-start(bf16[384,256]{1,0:T(8,128)(2,1)} %get-tuple-element.121.refs_0_), channel_id=1, source_target_pairs={{0,3},{1,2},{2,1},{3,0},{4,7},{5,6},{6,5},{7,4},{8,11},{9,10},{10,... | collective-permute-start | bytes 589832 | tf_op jit(solution)/shard_map/ppermute | solution.py:43
  148.4 20.4 %collective-permute-start.58 = (bf16[384,256]{1,0:T(8,128)(2,1)}, bf16[384,256]{1,0:T(8,128)(2,1)}, u32[]{:S(2)}, u32[]{:S(2)}) collective-permute-start(bf16[384,256]{1,0:T(8,128)(2,1)} %get-tuple-element.121.refs_0_), channel_id=1, source_target_pairs={{0,2},{1,3},{2,0},{3,1},{4,6},{5,7},{6,4},{7,5},{8,10},{9,11},{10,... | collective-permute-start | bytes 589832 | tf_op jit(solution)/shard_map/ppermute | solution.py:43
  152.0 56.3 %collective-permute-start.36 = (bf16[1728,256]{1,0:T(8,128)(2,1)S(1)}, bf16[1728,256]{1,0:T(8,128)(2,1)S(1)}, u32[]{:S(2)}, u32[]{:S(2)}) collective-permute-start(bf16[1728,256]{1,0:T(8,128)(2,1)S(1)} %copy-done.36), channel_id=1, source_target_pairs={{0,2},{1,3},{2,0},{3,1},{4,6},{5,7},{6,4},{7,5},{8,10},{9,11},{10,... | collective-permute-start | bytes 2654216 | tf_op jit(solution)/shard_map/ppermute | solution.py:43
  168.0 30.6 %collective-permute-start.66 = (bf16[144,256]{1,0:T(8,128)(2,1)}, bf16[144,256]{1,0:T(8,128)(2,1)S(1)}, u32[]{:S(2)}, u32[]{:S(2)}) collective-permute-start(bf16[144,256]{1,0:T(8,128)(2,1)} %get-tuple-element.131), channel_id=1, source_target_pairs={{0,2},{1,3},{2,0},{3,1},{4,6},{5,7},{6,4},{7,5},{8,10},{9,11},{10,... | collective-permute-start | bytes 221192 | tf_op jit(solution)/shard_map/ppermute | solution.py:43
  168.9 38.6 %collective-permute-start.37 = (bf16[864,256]{1,0:T(8,128)(2,1)}, bf16[864,256]{1,0:T(8,128)(2,1)S(1)}, u32[]{:S(2)}, u32[]{:S(2)}) collective-permute-start(bf16[864,256]{1,0:T(8,128)(2,1)} %get-tuple-element.106), channel_id=1, source_target_pairs={{0,8},{8,0},{16,24},{24,16},{1,9},{9,1},{17,25},{25,17},{2,10},{10... | collective-permute-start | bytes 1327112 | tf_op jit(solution)/shard_map/ppermute | solution.py:111
  170.5 48.7 %collective-permute-start.40 = (bf16[1728,256]{1,0:T(8,128)(2,1)S(1)}, bf16[1728,256]{1,0:T(8,128)(2,1)S(1)}, u32[]{:S(2)}, u32[]{:S(2)}) collective-permute-start(bf16[1728,256]{1,0:T(8,128)(2,1)S(1)} %copy-done.36), channel_id=1, source_target_pairs={{0,3},{1,2},{2,1},{3,0},{4,7},{5,6},{6,5},{7,4},{8,11},{9,10},{10,... | collective-permute-start | bytes 2654216 | tf_op jit(solution)/shard_map/ppermute | solution.py:43
  172.3 35.5 %collective-permute-start.34 = (bf16[864,256]{1,0:T(8,128)(2,1)S(1)}, bf16[864,256]{1,0:T(8,128)(2,1)S(1)}, u32[]{:S(2)}, u32[]{:S(2)}) collective-permute-start(bf16[864,256]{1,0:T(8,128)(2,1)S(1)} %add_convert_fusion.15), channel_id=1, source_target_pairs={{8,16},{12,20},{16,8},{20,12},{0,4},{4,0},{24,28},{28,24},{9,17},{... | collective-permute-start | bytes 1327112 | tf_op jit(solution)/shard_map/ppermute | solution.py:115
  207.8 18.9 %collective-permute-start.38 = (bf16[864,256]{1,0:T(8,128)(2,1)S(1)}, bf16[864,256]{1,0:T(8,128)(2,1)S(1)}, u32[]{:S(2)}, u32[]{:S(2)}) collective-permute-start(bf16[864,256]{1,0:T(8,128)(2,1)S(1)} %add_convert_fusion.13), channel_id=1, source_target_pairs={{8,16},{12,20},{16,8},{20,12},{0,4},{4,0},{24,28},{28,24},{9,17},{... | collective-permute-start | bytes 1327112 | tf_op jit(solution)/shard_map/ppermute | solution.py:115
  208.4 19.3 %collective-permute-start.35 = (bf16[864,256]{1,0:T(8,128)(2,1)S(1)}, bf16[864,256]{1,0:T(8,128)(2,1)S(1)}, u32[]{:S(2)}, u32[]{:S(2)}) collective-permute-start(bf16[864,256]{1,0:T(8,128)(2,1)S(1)} %fusion.refs_0_), channel_id=1, source_target_pairs={{0,8},{8,0},{16,24},{24,16},{1,9},{9,1},{17,25},{25,17},{2,10},{10... | collective-permute-start | bytes 1327112 | tf_op jit(solution)/shard_map/ppermute | solution.py:111
  214.9 16.7 %collective-permute-start.43 = (bf16[864,256]{1,0:T(8,128)(2,1)S(1)}, bf16[864,256]{1,0:T(8,128)(2,1)S(1)}, u32[]{:S(2)}, u32[]{:S(2)}) collective-permute-start(bf16[864,256]{1,0:T(8,128)(2,1)S(1)} %fusion.2.refs_2_), channel_id=1, source_target_pairs={{0,8},{8,0},{16,24},{24,16},{1,9},{9,1},{17,25},{25,17},{2,10},{10... | collective-permute-start | bytes 1327112 | tf_op jit(solution)/shard_map/ppermute | solution.py:111
  224.1 94.8 %collective-permute-start.69 = (f32[128,256]{1,0:T(8,128)}, f32[128,256]{1,0:T(8,128)S(1)}, u32[]{:S(2)}, u32[]{:S(2)}) collective-permute-start(f32[128,256]{1,0:T(8,128)} %get-tuple-element.136), channel_id=1, source_target_pairs={{0,4},{4,0},{1,5},{5,1},{2,6},{6,2},{3,7},{7,3},{8,12},{12,8},{9,1... | collective-permute-start | bytes 393224 | tf_op jit(solution)/shard_map/ppermute | solution.py:49
  241.0 19.9 %collective-permute-start.61 = (bf16[864,256]{1,0:T(8,128)(2,1)S(1)}, bf16[864,256]{1,0:T(8,128)(2,1)S(1)}, u32[]{:S(2)}, u32[]{:S(2)}) collective-permute-start(bf16[864,256]{1,0:T(8,128)(2,1)S(1)} %fusion.4.refs_6_), channel_id=1, source_target_pairs={{0,8},{8,0},{16,24},{24,16},{1,9},{9,1},{17,25},{25,17},{2,10},{10... | collective-permute-start | bytes 1327112 | tf_op jit(solution)/shard_map/ppermute | solution.py:111
  244.7 20.3 %collective-permute-start.45 = (bf16[864,256]{1,0:T(8,128)(2,1)S(1)}, bf16[864,256]{1,0:T(8,128)(2,1)S(1)}, u32[]{:S(2)}, u32[]{:S(2)}) collective-permute-start(bf16[864,256]{1,0:T(8,128)(2,1)S(1)} %fusion.3.refs_4_.refs_8_), channel_id=1, source_target_pairs={{0,8},{8,0},{16,24},{24,16},{1,9},{9,1},{17,25},{25,17},{2,10},{10... | collective-permute-start | bytes 1327112 | tf_op jit(solution)/shard_map/ppermute | solution.py:111
  252.1 20.7 %collective-permute-start.71 = (bf16[864,256]{1,0:T(8,128)(2,1)S(1)}, bf16[864,256]{1,0:T(8,128)(2,1)S(1)}, u32[]{:S(2)}, u32[]{:S(2)}) collective-permute-start(bf16[864,256]{1,0:T(8,128)(2,1)S(1)} %fusion.6.refs_10_), channel_id=1, source_target_pairs={{0,8},{8,0},{16,24},{24,16},{1,9},{9,1},{17,25},{25,17},{2,10},{10... | collective-permute-start | bytes 1327112 | tf_op jit(solution)/shard_map/ppermute | solution.py:111
  275.5 20.3 %collective-permute-start.75 = (bf16[864,256]{1,0:T(8,128)(2,1)S(1)}, bf16[864,256]{1,0:T(8,128)(2,1)S(1)}, u32[]{:S(2)}, u32[]{:S(2)}) collective-permute-start(bf16[864,256]{1,0:T(8,128)(2,1)S(1)} %fusion.7.refs_14_), channel_id=1, source_target_pairs={{0,8},{8,0},{16,24},{24,16},{1,9},{9,1},{17,25},{25,17},{2,10},{10... | collective-permute-start | bytes 1327112 | tf_op jit(solution)/shard_map/ppermute | solution.py:111
  284.1 16.8 %collective-permute-start.77 = (bf16[512,256]{1,0:T(8,128)(2,1)S(1)}, bf16[512,256]{1,0:T(8,128)(2,1)S(1)}, u32[]{:S(2)}, u32[]{:S(2)}) collective-permute-start(bf16[512,256]{1,0:T(8,128)(2,1)S(1)} %fusion.8.refs_0_), channel_id=1, source_target_pairs={{0,8},{8,0},{16,24},{24,16},{1,9},{9,1},{17,25},{25,17},{2,10},{10... | collective-permute-start | bytes 786440 | tf_op jit(solution)/shard_map/ppermute | solution.py:111
  303.1 20.2 %collective-permute-start.81 = (bf16[512,256]{1,0:T(8,128)(2,1)S(1)}, bf16[512,256]{1,0:T(8,128)(2,1)S(1)}, u32[]{:S(2)}, u32[]{:S(2)}) collective-permute-start(bf16[512,256]{1,0:T(8,128)(2,1)S(1)} %add_convert_fusion.18.refs_2_), channel_id=1, source_target_pairs={{0,8},{8,0},{16,24},{24,16},{1,9},{9,1},{17,25},{25,17},{2,10},{10... | collective-permute-start | bytes 786440 | tf_op jit(solution)/shard_map/ppermute | solution.py:111
  306.2 17.1 %collective-permute-start.82 = (bf16[512,256]{1,0:T(8,128)(2,1)S(1)}, bf16[512,256]{1,0:T(8,128)(2,1)S(1)}, u32[]{:S(2)}, u32[]{:S(2)}) collective-permute-start(bf16[512,256]{1,0:T(8,128)(2,1)S(1)} %add_convert_fusion.16.refs_3_), channel_id=1, source_target_pairs={{0,8},{8,0},{16,24},{24,16},{1,9},{9,1},{17,25},{25,17},{2,10},{10... | collective-permute-start | bytes 786440 | tf_op jit(solution)/shard_map/ppermute | solution.py:111
  (156 other events, 1471.1 us)

commit v3 on v2

--- a/solution.py
+++ b/solution.py
@@ -305,7 +305,7 @@
 
     def ffn_in(inf, tk, gn, mine, other, *refs):
         x, y = refs[:n_col], refs[n_col:2 * n_col]
-        hidden, gp_out, up_out, act_out, n2 = refs[2 * n_col:]
+        hidden_out, gp_out, up_out, act_out, n2, hidden = refs[2 * n_col:]
         p = inf[2]
         total = jnp.zeros((group, 1), f32)
         for k in K:
@@ -314,6 +314,7 @@
             h = tk[:, cols] + (mine[:, cols] + swapped)
             hidden[:, cols] = h
             total = total + jnp.sum(h * h, axis=1, keepdims=True)
+        hidden_out[...] = hidden[:rows]
         scale = lax.rsqrt(total / model + epsilon)
         ax = jnp.zeros((ff, group), f32)
         ay = jnp.zeros((ff, group), f32)
@@ -333,9 +334,10 @@
     hidden, gate_proj, up_proj, act, n2 = call(
         ffn_in, info, [tok, gains, hp, hp_o] + xs + ys,
         [
-            ((group, model), f32), ((ff, group), f32), ((ff, group), f32), ((ff, group), bf16),
+            ((rows, model), f32), ((ff, group), f32), ((ff, group), f32), ((ff, group), bf16),
             ((group, width), bf16),
         ],
+        [pltpu.VMEM((group, model), f32)],
         flops=2 * 10**9,
     )
 
@@ -363,17 +365,16 @@
                     ga = ga + jnp.concatenate([top, dot(d[:fold_ff, hw:], g, 1, 1)], axis=0)
         gp, up = gpr[...], upr[...]
         sig = jax.nn.sigmoid(gp)
-        piece[:ff] = act_ref[...]
-        piece[ff:2 * ff] = (ga * up * sig * (1.0 + gp * (1.0 - sig))).astype(bf16)
-        piece[2 * ff:] = (ga * gp * sig).astype(bf16)
+        piece[:ff] = (ga * up * sig * (1.0 + gp * (1.0 - sig))).astype(bf16)
+        piece[ff:] = (ga * gp * sig).astype(bf16)
         chunk[:ff] = dot(act_ref[...], gf[0], 1, 0).astype(bf16)
-        chunk[ff:] = dot(piece[ff:], n2r[...], 1, 0).astype(bf16)
+        chunk[ff:] = dot(piece[...], n2r[...], 1, 0).astype(bf16)
         chunk_a[...] = chunk[:cut]
         chunk_b[...] = chunk[cut:]
 
     piece0, chunk_a, chunk_b = call(
         ffn_back, info, [gate_proj, up_proj, act, n2] + gfs + gfs_o + downs,
-        [((3 * ff, group), bf16), ((cut, width), bf16), ((3 * ff - cut, width), bf16)],
+        [((2 * ff, group), bf16), ((cut, width), bf16), ((3 * ff - cut, width), bf16)],
         [pltpu.VMEM((n_col, group, width), bf16), pltpu.VMEM((3 * ff, width), bf16)],
         flops=2 * 10**9,
     )
@@ -381,7 +382,7 @@
     def ffn_part(inf, pc, *refs):
         x, y = refs[:n_col], refs[n_col:2 * n_col]
         mine, sent = refs[2 * n_col:]
-        gg, gu = pc[ff:2 * ff], pc[2 * ff:]
+        gg, gu = pc[:ff], pc[ff:]
         a = jnp.where(inf[2] == 0, gg, gu).T
         b = jnp.where(inf[2] == 0, gu, gg).T
         for k in K:
@@ -443,20 +444,21 @@
     gmix = [gmix0] + [col_send(gmix0, k) for k in peers()]
     gmix_o = [row_send(m) for m in gmix]
 
+    acts = [act] + [col_send(act, k) for k in peers()]
     pieces = [piece0] + [col_send(piece0, k) for k in peers()]
 
-    def ffn_grad(inf, pc, gfa, gfb, n2r, out_a, out_b, gf, out):
+    def ffn_grad(inf, ac, pc, gfa, gfb, n2r, out_a, out_b, gf, out):
         gf[:rows] = gfa[...]
         gf[rows:] = gfb[...]
-        out[:ff] = dot(pc[:ff], gf[...], 1, 0).astype(bf16)
-        out[ff:] = dot(pc[ff:], n2r[...], 1, 0).astype(bf16)
+        out[:ff] = dot(ac[...], gf[...], 1, 0).astype(bf16)
+        out[ff:] = dot(pc[...], n2r[...], 1, 0).astype(bf16)
         out_a[...] = out[:cut]
         out_b[...] = out[cut:]
 
     chunks = [chunk_a, chunk_b]
     for k in peers():
         chunk_a, chunk_b = call(
-            ffn_grad, info, [pieces[k], gf0, gfs_o[0], n2],
+            ffn_grad, info, [acts[k], pieces[k], gf0, gfs_o[0], n2],
             [((cut, width), bf16), ((3 * ff - cut, width), bf16)],
             [pltpu.VMEM((group, width), bf16), pltpu.VMEM((3 * ff, width), bf16)],
         )
@@ -550,14 +552,14 @@
         acc = jnp.zeros((group, width), f32)
         for k in K:
             at = pl.ds(pl.multiple_of((inf[0] ^ k) * ff, 32), ff)
-            acc = acc + dot(pcs[k][:ff].T, dw[at, :], 1, 0)
+            acc = acc + dot(pcs[k][...].T, dw[at, :], 1, 0)
         mine[...] = acc[:rows] + hid[:rows, :width]
         sent[...] = acc[rows:]
         wide = jnp.concatenate([tg[...], jnp.zeros((8, width - lanes), f32)], axis=1) if width > lanes else tg[...]
         small[...] = jnp.concatenate([ga[...] + gb[...], wide], axis=0).astype(bf16)
 
     out_mine, out_sent, small = call(
-        ffn_out, info, [down_weight, hidden, gain_pair, gain_came, taps_grad] + pieces,
+        ffn_out, info, [down_weight, hidden, gain_pair, gain_came, taps_grad] + acts,
         [((rows, width), f32)] * 2 + [((16, width), bf16)],
     )
     out_came = row_send(out_sent)

time: 328 us -> 326 us (level)
    ppermute x16, waiting for transfers between devices: 47.4 us -> 56 us  [dp_sums(): came = lax.ppermute(sent, 'dp', ends)]
    ppermute x33 -> x36, waiting for transfers between devices: 75.7 us -> 67.3 us  [col_send(): return lax.ppermute(piece, 'col', [(i, i ^ k) for i in range(n)])]
    ppermute x16, starting transfers between devices: 55.8 us -> 47.6 us  [dp_sums(): came = lax.ppermute(sent, 'dp', ends)]
    ppermute x33 -> x36, starting transfers between devices: 41.6 us -> 46.2 us  [col_send(): return lax.ppermute(piece, 'col', [(i, i ^ k) for i in range(n)])]
    unnamed x208 -> x212, local copies, waits for them, and re-layouts: 8.58 us -> 8.77 us
  transfers between devices with their start and end apart: 84 -> 87, of which waited for: 29 -> 30; matrix products, arithmetic and copies ran while one was open for 2% -> 2% of each run, Pallas kernels for 16% -> 16%
where the time goes in v3:
time: 326 us; the launch traced here: 325 us
  waiting for transfers between devices  139 us (43%)
  starting transfers between devices  103 us (32%)
  Pallas kernels  65.8 us (20%)
  local copies, waits for them, and re-layouts  9.57 us (3%)
  other arithmetic  5.48 us (2%)
    ppermute x36, waiting for transfers between devices, col_send(): return lax.ppermute(piece, 'col', [(i, i ^ k) for i in range(n)])  67.3 us
    pallas_call x21, Pallas kernels, call(): pl.pallas_call(body, out_shape=[jax.ShapeDtypeStruct(s, t) for s, t in ou...  65.8 us
    ppermute x16, waiting for transfers between devices, dp_sums(): came = lax.ppermute(sent, 'dp', ends)  56 us
    ppermute x16, starting transfers between devices, dp_sums(): came = lax.ppermute(sent, 'dp', ends)  47.6 us
    ppermute x36, starting transfers between devices, col_send(): return lax.ppermute(piece, 'col', [(i, i ^ k) for i in range(n)])  46.2 us
    ppermute x5, waiting for transfers between devices, pair_send(): return lax.ppermute(piece, 'dp', [(i, i ^ 1) for i in range(n)])  13.2 us
    unnamed x212, local copies, waits for them, and re-layouts  8.77 us
  transfers between devices with their start and end apart: 87, of which 30 were waited for; matrix products, arithmetic and copies ran while one was open for 2% of the time, Pallas kernels for 16%

profile of v3, /device:TPU:0, one launch (start us, length us, event | category | flops | bytes accessed | tf_op | source)
XLA Modules:
  0.0 325.0 jit_solution(368786088043063697)
XLA Ops:
  0.6 4.0 %collective-permute-start.2 = (f32[128,256]{1,0:T(8,128)}, f32[128,256]{1,0:T(8,128)S(1)}, u32[]{:S(2)}, u32[]{:S(2)}) collective-permute-start(f32[128,256]{1,0:T(8,128)} %refs_0_.1), channel_id=1, source_target_pairs={{0,3},{1,2},{2,1},{3,0},{4,7},{5,6},{6,5},{7,4},{8,11},{9,10},{10,... | collective-permute-start | bytes 393224 | tf_op jit(solution)/shard_map/ppermute | solution.py:43
  13.0 4.3 %shard_map.188 = (bf16[256,256]{1,0:T(8,128)(2,1)}, bf16[576,256]{1,0:T(8,128)(2,1)}, bf16[576,256]{1,0:T(8,128)(2,1)}, bf16[576,256]{1,0:T(8,128)(2,1)}, bf16[1...) custom-call(s32[4]{0:T(128)} %pad_add_fusion.inf, ...), custom_call_target="tpu_custom_call" | custom-call | flops 100000000 | bytes 3932160 | tf_op jit(solution)/shard_map/pallas_call | solution.py:24
  20.2 3.2 collective-permute-done.15.refs_7_.refs_11_
  47.6 4.6 %collective-permute-done.27.refs_3_.refs_11_ = bf16[416,256]{1,0:T(8,128)(2,1)S(1)} collective-permute-done((bf16[416,256]{1,0:T(8,128)(2,1)S(1)}, bf16[416,256]{1,0:T(8,128)(2,1)S(1)}, u32[]{:S(2)}, u32[]{:S(2)}) %collective-permute-start.27) | collective-permute-done | bytes 213024 | tf_op jit(solution)/shard_map/ppermute | solution.py:43
  53.9 4.2 %collective-permute-done.18.refs_1_ = bf16[576,256]{1,0:T(8,128)(2,1)S(1)} collective-permute-done((bf16[576,256]{1,0:T(8,128)(2,1)S(1)}, bf16[576,256]{1,0:T(8,128)(2,1)S(1)}, u32[]{:S(2)}, u32[]{:S(2)}) %collective-permute-start.18) | collective-permute-done | bytes 294944 | tf_op jit(solution)/shard_map/ppermute | solution.py:43
  59.5 12.6 %collective-permute-done.20.refs_3_ = bf16[576,256]{1,0:T(8,128)(2,1)S(1)} collective-permute-done((bf16[576,256]{1,0:T(8,128)(2,1)S(1)}, bf16[576,256]{1,0:T(8,128)(2,1)S(1)}, u32[]{:S(2)}, u32[]{:S(2)}) %collective-permute-start.20) | collective-permute-done | bytes 294944 | tf_op jit(solution)/shard_map/ppermute | solution.py:43
  74.6 7.3 %collective-permute-done.22.refs_6_ = bf16[576,256]{1,0:T(8,128)(2,1)S(1)} collective-permute-done((bf16[576,256]{1,0:T(8,128)(2,1)S(1)}, bf16[576,256]{1,0:T(8,128)(2,1)S(1)}, u32[]{:S(2)}, u32[]{:S(2)}) %collective-permute-start.22) | collective-permute-done | bytes 294944 | tf_op jit(solution)/shard_map/ppermute | solution.py:55
  82.4 5.9 %collective-permute-done.23.refs_7_ = bf16[576,256]{1,0:T(8,128)(2,1)S(1)} collective-permute-done((bf16[576,256]{1,0:T(8,128)(2,1)S(1)}, bf16[576,256]{1,0:T(8,128)(2,1)S(1)}, u32[]{:S(2)}, u32[]{:S(2)}) %collective-permute-start.23) | collective-permute-done | bytes 294944 | tf_op jit(solution)/shard_map/ppermute | solution.py:55
  89.4 4.7 %shard_map.190 = (f32[128,1024]{1,0:T(8,128)}, f32[576,256]{1,0:T(8,128)}, f32[576,256]{1,0:T(8,128)}, bf16[576,256]{1,0:T(8,128)(2,1)}, bf16[256,256]{1,0:T(8,128)(2,1)}) custom-call(s32[4]{0:T(128)} %pad_add_fusion.inf, f32[256,1024]{1,0:T(8,128)} %get-tuple-element.84.tk.act_in, f32[8,1024]{1,0:T(8,128)} %get-tuple-element.85.gn, ...), custom_call_target="tpu_custom_call" | custom-call | flops 2000000000 | bytes 5537792 | tf_op jit(solution)/shard_map/pallas_call | solution.py:24
  95.1 4.6 %shard_map.191 = (bf16[1152,256]{1,0:T(8,128)(2,1)}, bf16[864,256]{1,0:T(8,128)(2,1)}, bf16[864,256]{1,0:T(8,128)(2,1)}) custom-call(s32[4]{0:T(128)} %pad_add_fusion.inf, f32[576,256]{1,0:T(8,128)} %get-tuple-element.94.gpr, f32[576,256]{1,0:T(8,128)} %get-tuple-element.95.upr, bf16[576,256]{1,0:T(8,128)(2,1)} %get-tuple-element.93.act_ref.refs_0_, ...), custom_call_target="tpu_custom_call" | custom-call | flops 2000000000 | bytes 5046272 | tf_op jit(solution)/shard_map/pallas_call | solution.py:24
  99.6 3.6 %shard_map.195 = (f32[128,1024]{1,0:T(8,128)}, bf16[128,1024]{1,0:T(8,128)(2,1)}) custom-call(s32[4]{0:T(128)} %pad_add_fusion.inf, bf16[1152,256]{1,0:T(8,128)(2,1)} %get-tuple-element.102.pc, bf16[576,256]{1,0:T(8,128)(2,1)} %get-tuple-element.88.refs_0_, bf16[576,256]{1,0:T(8,128)(2,1)} %copy-done.96, bf16[576,256]{1,0:T(8,128)(2,1)} %copy-done.97, ...), custom_call_target="tpu_custom_call" | custom-call | flops 1000000000 | bytes 2949120 | tf_op jit(solution)/shard_map/pallas_call | solution.py:24
  111.5 10.1 %collective-permute-done.50.refs_0_ = bf16[144,256]{1,0:T(8,128)(2,1)S(1)} collective-permute-done((bf16[144,256]{1,0:T(8,128)(2,1)}, bf16[144,256]{1,0:T(8,128)(2,1)S(1)}, u32[]{:S(2)}, u32[]{:S(2)}) %collective-permute-start.50) | collective-permute-done | bytes 73760 | tf_op jit(solution)/shard_map/ppermute | solution.py:43
  138.6 3.7 %shard_map.198 = (bf16[384,256]{1,0:T(8,128)(2,1)}, f32[128,1024]{1,0:T(8,128)}, bf16[128,1024]{1,0:T(8,128)(2,1)}, f32[8,128]{1,0:T(8,128)}) custom-call(s32[4]{0:T(128)} %pad_add_fusion.inf, s32[256,1]{1,0:T(8,128)} %copy.21.sg, f32[3,128]{1,0:T(4,128)} %taps.3, f32[256,384]{1,0:T(8,128)} %get-tuple-element.120.m3, ...), custom_call_target="tpu_custom_call" | custom-call | flops 100000000 | bytes 2804224 | tf_op jit(solution)/shard_map/pallas_call | solution.py:24
  142.9 3.3 %collective-permute-done.24.ac.refs_1_ = bf16[576,256]{1,0:T(8,128)(2,1)S(1)} collective-permute-done((bf16[576,256]{1,0:T(8,128)(2,1)S(1)}, bf16[576,256]{1,0:T(8,128)(2,1)S(1)}, u32[]{:S(2)}, u32[]{:S(2)}) %collective-permute-start.24) | collective-permute-done | bytes 294944 | tf_op jit(solution)/shard_map/ppermute | solution.py:43
  153.7 22.3 %collective-permute-done.37.ac.refs_2_ = bf16[576,256]{1,0:T(8,128)(2,1)S(1)} collective-permute-done((bf16[576,256]{1,0:T(8,128)(2,1)S(1)}, bf16[576,256]{1,0:T(8,128)(2,1)S(1)}, u32[]{:S(2)}, u32[]{:S(2)}) %collective-permute-start.37) | collective-permute-done | bytes 294944 | tf_op jit(solution)/shard_map/ppermute | solution.py:43
  200.5 3.1 shard_map.202
  204.6 4.3 %collective-permute-start.36 = (bf16[864,256]{1,0:T(8,128)(2,1)S(1)}, bf16[864,256]{1,0:T(8,128)(2,1)S(1)}, u32[]{:S(2)}, u32[]{:S(2)}) collective-permute-start(bf16[864,256]{1,0:T(8,128)(2,1)S(1)} %fusion.refs_0_), channel_id=1, source_target_pairs={{0,8},{8,0},{16,24},{24,16},{1,9},{9,1},{17,25},{25,17},{2,10},{10... | collective-permute-start | bytes 1327112 | tf_op jit(solution)/shard_map/ppermute | solution.py:111
  209.4 10.7 %collective-permute-start.41 = (bf16[864,256]{1,0:T(8,128)(2,1)S(1)}, bf16[864,256]{1,0:T(8,128)(2,1)S(1)}, u32[]{:S(2)}, u32[]{:S(2)}) collective-permute-start(bf16[864,256]{1,0:T(8,128)(2,1)S(1)} %fusion.1.refs_2_.refs_4_), channel_id=1, source_target_pairs={{0,8},{8,0},{16,24},{24,16},{1,9},{9,1},{17,25},{25,17},{2,10},{10... | collective-permute-start | bytes 1327112 | tf_op jit(solution)/shard_map/ppermute | solution.py:111
  220.3 9.1 %collective-permute-done.46.refs_3_ = bf16[864,256]{1,0:T(8,128)(2,1)S(1)} collective-permute-done((bf16[864,256]{1,0:T(8,128)(2,1)S(1)}, bf16[864,256]{1,0:T(8,128)(2,1)S(1)}, u32[]{:S(2)}, u32[]{:S(2)}) %collective-permute-start.46) | collective-permute-done | bytes 442400 | tf_op jit(solution)/shard_map/ppermute | solution.py:111
  229.6 8.8 %collective-permute-done.41.refs_3_.refs_5_ = bf16[864,256]{1,0:T(8,128)(2,1)S(1)} collective-permute-done((bf16[864,256]{1,0:T(8,128)(2,1)S(1)}, bf16[864,256]{1,0:T(8,128)(2,1)S(1)}, u32[]{:S(2)}, u32[]{:S(2)}) %collective-permute-start.41) | collective-permute-done | bytes 442400 | tf_op jit(solution)/shard_map/ppermute | solution.py:111
  242.7 9.3 %collective-permute-start.74 = (bf16[864,256]{1,0:T(8,128)(2,1)S(1)}, bf16[864,256]{1,0:T(8,128)(2,1)S(1)}, u32[]{:S(2)}, u32[]{:S(2)}) collective-permute-start(bf16[864,256]{1,0:T(8,128)(2,1)S(1)} %fusion.6.refs_10_), channel_id=1, source_target_pairs={{0,8},{8,0},{16,24},{24,16},{1,9},{9,1},{17,25},{25,17},{2,10},{10... | collective-permute-start | bytes 1327112 | tf_op jit(solution)/shard_map/ppermute | solution.py:111
  252.5 9.3 %collective-permute-done.48.refs_5_.refs_9_ = bf16[864,256]{1,0:T(8,128)(2,1)S(1)} collective-permute-done((bf16[864,256]{1,0:T(8,128)(2,1)S(1)}, bf16[864,256]{1,0:T(8,128)(2,1)S(1)}, u32[]{:S(2)}, u32[]{:S(2)}) %collective-permute-start.48) | collective-permute-done | bytes 442400 | tf_op jit(solution)/shard_map/ppermute | solution.py:111
  261.9 8.4 %collective-permute-done.74.refs_11_ = bf16[864,256]{1,0:T(8,128)(2,1)S(1)} collective-permute-done((bf16[864,256]{1,0:T(8,128)(2,1)S(1)}, bf16[864,256]{1,0:T(8,128)(2,1)S(1)}, u32[]{:S(2)}, u32[]{:S(2)}) %collective-permute-start.74) | collective-permute-done | bytes 442400 | tf_op jit(solution)/shard_map/ppermute | solution.py:111
  273.5 4.6 %collective-permute-start.80 = (bf16[512,256]{1,0:T(8,128)(2,1)S(1)}, bf16[512,256]{1,0:T(8,128)(2,1)S(1)}, u32[]{:S(2)}, u32[]{:S(2)}) collective-permute-start(bf16[512,256]{1,0:T(8,128)(2,1)S(1)} %fusion.8.refs_0_), channel_id=1, source_target_pairs={{0,8},{8,0},{16,24},{24,16},{1,9},{9,1},{17,25},{25,17},{2,10},{10... | collective-permute-start | bytes 786440 | tf_op jit(solution)/shard_map/ppermute | solution.py:111
  278.1 6.0 %collective-permute-done.66.refs_7_.refs_13_ = bf16[864,256]{1,0:T(8,128)(2,1)S(1)} collective-permute-done((bf16[864,256]{1,0:T(8,128)(2,1)S(1)}, bf16[864,256]{1,0:T(8,128)(2,1)S(1)}, u32[]{:S(2)}, u32[]{:S(2)}) %collective-permute-start.66) | collective-permute-done | bytes 442400 | tf_op jit(solution)/shard_map/ppermute | solution.py:111
  284.3 9.3 %collective-permute-done.78.refs_15_ = bf16[864,256]{1,0:T(8,128)(2,1)S(1)} collective-permute-done((bf16[864,256]{1,0:T(8,128)(2,1)S(1)}, bf16[864,256]{1,0:T(8,128)(2,1)S(1)}, u32[]{:S(2)}, u32[]{:S(2)}) %collective-permute-start.78) | collective-permute-done | bytes 442400 | tf_op jit(solution)/shard_map/ppermute | solution.py:111
  293.8 4.7 %collective-permute-done.80.refs_5_ = bf16[512,256]{1,0:T(8,128)(2,1)S(1)} collective-permute-done((bf16[512,256]{1,0:T(8,128)(2,1)S(1)}, bf16[512,256]{1,0:T(8,128)(2,1)S(1)}, u32[]{:S(2)}, u32[]{:S(2)}) %collective-permute-start.80) | collective-permute-done | bytes 262176 | tf_op jit(solution)/shard_map/ppermute | solution.py:111
  299.9 4.5 %collective-permute-start.84 = (bf16[512,256]{1,0:T(8,128)(2,1)S(1)}, bf16[512,256]{1,0:T(8,128)(2,1)S(1)}, u32[]{:S(2)}, u32[]{:S(2)}) collective-permute-start(bf16[512,256]{1,0:T(8,128)(2,1)S(1)} %add_convert_fusion.18.refs_2_), channel_id=1, source_target_pairs={{0,8},{8,0},{16,24},{24,16},{1,9},{9,1},{17,25},{25,17},{2,10},{10... | collective-permute-start | bytes 786440 | tf_op jit(solution)/shard_map/ppermute | solution.py:111
  304.5 3.5 %collective-permute-start.85 = (bf16[512,256]{1,0:T(8,128)(2,1)S(1)}, bf16[512,256]{1,0:T(8,128)(2,1)S(1)}, u32[]{:S(2)}, u32[]{:S(2)}) collective-permute-start(bf16[512,256]{1,0:T(8,128)(2,1)S(1)} %add_convert_fusion.16.refs_3_), channel_id=1, source_target_pairs={{0,8},{8,0},{16,24},{24,16},{1,9},{9,1},{17,25},{25,17},{2,10},{10... | collective-permute-start | bytes 786440 | tf_op jit(solution)/shard_map/ppermute | solution.py:111
  308.1 5.8 %shard_map.206 = (f32[256,2304]{1,0:T(8,128)}, f32[256,2304]{1,0:T(8,128)}) custom-call(s32[4]{0:T(128)} %pad_add_fusion.inf, bf16[864,256]{1,0:T(8,128)(2,1)} %copy-done.1, bf16[864,256]{1,0:T(8,128)(2,1)} %copy-done.2, bf16[864,256]{1,0:T(8,128)(2,1)} %copy-done.12, bf16[864,256]{1,0:T(8,128)(2,1)} %copy-done.13, bf16[864,256]{1,0:T(8,128)(2,1)} %copy-done.3, ...), custom_call_target="tpu_custom_call" | custom-call | flops 100000000 | bytes 7077888 | tf_op jit(solution)/shard_map/pallas_call | solution.py:24
  316.9 3.6 %shard_map.203 = (f32[2304,256]{1,0:T(8,128)}, f32[128,256]{1,0:T(8,128)}) custom-call(s32[4]{0:T(128)} %pad_add_fusion.inf, bf16[864,256]{1,0:T(8,128)(2,1)} %copy-done.1, bf16[864,256]{1,0:T(8,128)(2,1)} %copy-done.2, bf16[864,256]{1,0:T(8,128)(2,1)} %copy-done.3, bf16[864,256]{1,0:T(8,128)(2,1)} %copy-done.4, bf16[864,256]{1,0:T(8,128)(2,1)} %copy-done.5, ...), custom_call_target="tpu_custom_call" | custom-call | flops 100000000 | bytes 3801088 | tf_op jit(solution)/shard_map/pallas_call | solution.py:24
  321.9 3.1 shard_map.205
  (403 shorter events, 116.6 us)
Async XLA Ops:
  8.1 16.9 %collective-permute-start.7 = (bf16[272,384]{1,0:T(8,128)(2,1)}, bf16[272,384]{1,0:T(8,128)(2,1)S(1)}, u32[]{:S(2)}, u32[]{:S(2)}) collective-permute-start(bf16[272,384]{1,0:T(8,128)(2,1)} %get-tuple-element.81), channel_id=1, source_target_pairs={{0,1},{1,0},{2,3},{3,2},{4,5},{5,4},{6,7},{7,6},{8,9},{9,8},{10,11... | collective-permute-start | bytes 626696 | tf_op jit(solution)/shard_map/ppermute | solution.py:43
  10.0 15.6 %collective-permute-start.8 = (bf16[272,384]{1,0:T(8,128)(2,1)}, bf16[272,384]{1,0:T(8,128)(2,1)S(1)}, u32[]{:S(2)}, u32[]{:S(2)}) collective-permute-start(bf16[272,384]{1,0:T(8,128)(2,1)} %get-tuple-element.82), channel_id=1, source_target_pairs={{0,2},{1,3},{2,0},{3,1},{4,6},{5,7},{6,4},{7,5},{8,10},{9,11},{10,... | collective-permute-start | bytes 626696 | tf_op jit(solution)/shard_map/ppermute | solution.py:43
  18.9 15.8 %collective-permute-start.14 = (bf16[512,256]{1,0:T(8,128)(2,1)S(1)}, bf16[512,256]{1,0:T(8,128)(2,1)S(1)}, u32[]{:S(2)}, u32[]{:S(2)}) collective-permute-start(bf16[512,256]{1,0:T(8,128)(2,1)S(1)} %copy-done.8), channel_id=1, source_target_pairs={{0,2},{1,3},{2,0},{3,1},{4,6},{5,7},{6,4},{7,5},{8,10},{9,11},{10,... | collective-permute-start | bytes 786440 | tf_op jit(solution)/shard_map/ppermute | solution.py:43
  43.0 45.3 %collective-permute-start.17 = (f32[256,1024]{1,0:T(8,128)}, f32[256,1024]{1,0:T(8,128)S(1)}, u32[]{:S(2)}, u32[]{:S(2)}) collective-permute-start(f32[256,1024]{1,0:T(8,128)} %shard_map.189.mine), channel_id=1, source_target_pairs={{0,4},{4,0},{1,5},{5,1},{2,6},{6,2},{3,7},{7,3},{8,12},{12,8},{9,1... | collective-permute-start | bytes 3145736 | tf_op jit(solution)/shard_map/ppermute | solution.py:49
  46.6 26.0 %collective-permute-start.25 = (bf16[704,256]{1,0:T(8,128)(2,1)S(1)}, bf16[704,256]{1,0:T(8,128)(2,1)S(1)}, u32[]{:S(2)}, u32[]{:S(2)}) collective-permute-start(bf16[704,256]{1,0:T(8,128)(2,1)S(1)} %copy-done.88), channel_id=1, source_target_pairs={{0,1},{1,0},{2,3},{3,2},{4,5},{5,4},{6,7},{7,6},{8,9},{9,8},{10,11... | collective-permute-start | bytes 1081352 | tf_op jit(solution)/shard_map/ppermute | solution.py:43
  52.2 19.9 %collective-permute-start.20 = (bf16[576,256]{1,0:T(8,128)(2,1)S(1)}, bf16[576,256]{1,0:T(8,128)(2,1)S(1)}, u32[]{:S(2)}, u32[]{:S(2)}) collective-permute-start(bf16[576,256]{1,0:T(8,128)(2,1)S(1)} %copy-done.93), channel_id=1, source_target_pairs={{0,3},{1,2},{2,1},{3,0},{4,7},{5,6},{6,5},{7,4},{8,11},{9,10},{10,... | collective-permute-start | bytes 884744 | tf_op jit(solution)/shard_map/ppermute | solution.py:43
  58.1 16.0 %collective-permute-start.26 = (bf16[704,256]{1,0:T(8,128)(2,1)S(1)}, bf16[704,256]{1,0:T(8,128)(2,1)S(1)}, u32[]{:S(2)}, u32[]{:S(2)}) collective-permute-start(bf16[704,256]{1,0:T(8,128)(2,1)S(1)} %copy-done.87), channel_id=1, source_target_pairs={{0,2},{1,3},{2,0},{3,1},{4,6},{5,7},{6,4},{7,5},{8,10},{9,11},{10,... | collective-permute-start | bytes 1081352 | tf_op jit(solution)/shard_map/ppermute | solution.py:43
  59.0 15.1 %collective-permute-start.21 = (bf16[576,256]{1,0:T(8,128)(2,1)S(1)}, bf16[576,256]{1,0:T(8,128)(2,1)S(1)}, u32[]{:S(2)}, u32[]{:S(2)}) collective-permute-start(bf16[576,256]{1,0:T(8,128)(2,1)S(1)} %collective-permute-done.18.refs_1_), channel_id=1, source_target_pairs={{0,8},{8,0},{16,24},{24,16},{1,9},{9,1},{17,25},{25,17},{2,10},{10... | collective-permute-start | bytes 884744 | tf_op jit(solution)/shard_map/ppermute | solution.py:55
  72.5 15.7 %collective-permute-start.23 = (bf16[576,256]{1,0:T(8,128)(2,1)S(1)}, bf16[576,256]{1,0:T(8,128)(2,1)S(1)}, u32[]{:S(2)}, u32[]{:S(2)}) collective-permute-start(bf16[576,256]{1,0:T(8,128)(2,1)S(1)} %collective-permute-done.20.refs_3_), channel_id=1, source_target_pairs={{0,8},{8,0},{16,24},{24,16},{1,9},{9,1},{17,25},{25,17},{2,10},{10... | collective-permute-start | bytes 884744 | tf_op jit(solution)/shard_map/ppermute | solution.py:55
  74.1 20.0 %collective-permute-start.29 = (bf16[704,256]{1,0:T(8,128)(2,1)S(1)}, bf16[704,256]{1,0:T(8,128)(2,1)S(1)}, u32[]{:S(2)}, u32[]{:S(2)}) collective-permute-start(bf16[704,256]{1,0:T(8,128)(2,1)S(1)} %collective-permute-done.25.refs_1_.refs_9_), channel_id=1, source_target_pairs={{0,4},{4,0},{1,5},{5,1},{2,6},{6,2},{3,7},{7,3},{8,12},{12,8},{9,1... | collective-permute-start | bytes 1081352 | tf_op jit(solution)/shard_map/ppermute | solution.py:49
  74.2 20.0 %collective-permute-start.30 = (bf16[704,256]{1,0:T(8,128)(2,1)S(1)}, bf16[704,256]{1,0:T(8,128)(2,1)S(1)}, u32[]{:S(2)}, u32[]{:S(2)}) collective-permute-start(bf16[704,256]{1,0:T(8,128)(2,1)S(1)} %collective-permute-done.26.refs_2_.refs_10_), channel_id=1, source_target_pairs={{0,4},{4,0},{1,5},{5,1},{2,6},{6,2},{3,7},{7,3},{8,12},{12,8},{9,1... | collective-permute-start | bytes 1081352 | tf_op jit(solution)/shard_map/ppermute | solution.py:49
  103.7 43.0 %collective-permute-start.33 = (bf16[1152,256]{1,0:T(8,128)(2,1)}, bf16[1152,256]{1,0:T(8,128)(2,1)S(1)}, u32[]{:S(2)}, u32[]{:S(2)}) collective-permute-start(bf16[1152,256]{1,0:T(8,128)(2,1)} %get-tuple-element.102.pc), channel_id=1, source_target_pairs={{0,1},{1,0},{2,3},{3,2},{4,5},{5,4},{6,7},{7,6},{8,9},{9,8},{10,11... | collective-permute-start | bytes 1769480 | tf_op jit(solution)/shard_map/ppermute | solution.py:43
  136.4 42.2 %collective-permute-start.43 = (bf16[1152,256]{1,0:T(8,128)(2,1)}, bf16[1152,256]{1,0:T(8,128)(2,1)S(1)}, u32[]{:S(2)}, u32[]{:S(2)}) collective-permute-start(bf16[1152,256]{1,0:T(8,128)(2,1)} %get-tuple-element.102.pc), channel_id=1, source_target_pairs={{0,3},{1,2},{2,1},{3,0},{4,7},{5,6},{6,5},{7,4},{8,11},{9,10},{10,... | collective-permute-start | bytes 1769480 | tf_op jit(solution)/shard_map/ppermute | solution.py:43
  142.3 34.2 %collective-permute-start.34 = (bf16[864,256]{1,0:T(8,128)(2,1)}, bf16[864,256]{1,0:T(8,128)(2,1)}, u32[]{:S(2)}, u32[]{:S(2)}) collective-permute-start(bf16[864,256]{1,0:T(8,128)(2,1)} %get-tuple-element.104), channel_id=1, source_target_pairs={{0,8},{8,0},{16,24},{24,16},{1,9},{9,1},{17,25},{25,17},{2,10},{10... | collective-permute-start | bytes 1327112 | tf_op jit(solution)/shard_map/ppermute | solution.py:111
  146.2 31.5 %collective-permute-start.44 = (bf16[864,256]{1,0:T(8,128)(2,1)S(1)}, bf16[864,256]{1,0:T(8,128)(2,1)}, u32[]{:S(2)}, u32[]{:S(2)}) collective-permute-start(bf16[864,256]{1,0:T(8,128)(2,1)S(1)} %copy-done.47), channel_id=1, source_target_pairs={{0,8},{8,0},{16,24},{24,16},{1,9},{9,1},{17,25},{25,17},{2,10},{10... | collective-permute-start | bytes 1327112 | tf_op jit(solution)/shard_map/ppermute | solution.py:111
  146.7 34.6 %collective-permute-start.38 = (bf16[1152,256]{1,0:T(8,128)(2,1)}, bf16[1152,256]{1,0:T(8,128)(2,1)S(1)}, u32[]{:S(2)}, u32[]{:S(2)}) collective-permute-start(bf16[1152,256]{1,0:T(8,128)(2,1)} %get-tuple-element.102.pc), channel_id=1, source_target_pairs={{0,2},{1,3},{2,0},{3,1},{4,6},{5,7},{6,4},{7,5},{8,10},{9,11},{10,... | collective-permute-start | bytes 1769480 | tf_op jit(solution)/shard_map/ppermute | solution.py:43
  147.4 28.7 %collective-permute-start.37 = (bf16[576,256]{1,0:T(8,128)(2,1)S(1)}, bf16[576,256]{1,0:T(8,128)(2,1)S(1)}, u32[]{:S(2)}, u32[]{:S(2)}) collective-permute-start(bf16[576,256]{1,0:T(8,128)(2,1)S(1)} %copy-done.49), channel_id=1, source_target_pairs={{0,2},{1,3},{2,0},{3,1},{4,6},{5,7},{6,4},{7,5},{8,10},{9,11},{10,... | collective-permute-start | bytes 884744 | tf_op jit(solution)/shard_map/ppermute | solution.py:43
  176.1 28.1 %collective-permute-start.39 = (bf16[864,256]{1,0:T(8,128)(2,1)S(1)}, bf16[864,256]{1,0:T(8,128)(2,1)S(1)}, u32[]{:S(2)}, u32[]{:S(2)}) collective-permute-start(bf16[864,256]{1,0:T(8,128)(2,1)S(1)} %copy-done.48), channel_id=1, source_target_pairs={{0,8},{8,0},{16,24},{24,16},{1,9},{9,1},{17,25},{25,17},{2,10},{10... | collective-permute-start | bytes 1327112 | tf_op jit(solution)/shard_map/ppermute | solution.py:111
  181.3 23.1 %collective-permute-start.35 = (bf16[864,256]{1,0:T(8,128)(2,1)S(1)}, bf16[864,256]{1,0:T(8,128)(2,1)S(1)}, u32[]{:S(2)}, u32[]{:S(2)}) collective-permute-start(bf16[864,256]{1,0:T(8,128)(2,1)S(1)} %add_convert_fusion.15), channel_id=1, source_target_pairs={{8,16},{12,20},{16,8},{20,12},{0,4},{4,0},{24,28},{28,24},{9,17},{... | collective-permute-start | bytes 1327112 | tf_op jit(solution)/shard_map/ppermute | solution.py:115
  181.4 14.7 %collective-permute-start.62 = (bf16[384,256]{1,0:T(8,128)(2,1)S(1)}, bf16[384,256]{1,0:T(8,128)(2,1)S(1)}, u32[]{:S(2)}, u32[]{:S(2)}) collective-permute-start(bf16[384,256]{1,0:T(8,128)(2,1)S(1)} %copy-done.57), channel_id=1, source_target_pairs={{0,3},{1,2},{2,1},{3,0},{4,7},{5,6},{6,5},{7,4},{8,11},{9,10},{10,... | collective-permute-start | bytes 589832 | tf_op jit(solution)/shard_map/ppermute | solution.py:43
  203.7 112.5 %collective-permute-start.72 = (f32[128,256]{1,0:T(8,128)}, f32[128,256]{1,0:T(8,128)S(1)}, u32[]{:S(2)}, u32[]{:S(2)}) collective-permute-start(f32[128,256]{1,0:T(8,128)} %get-tuple-element.136), channel_id=1, source_target_pairs={{0,4},{4,0},{1,5},{5,1},{2,6},{6,2},{3,7},{7,3},{8,12},{12,8},{9,1... | collective-permute-start | bytes 393224 | tf_op jit(solution)/shard_map/ppermute | solution.py:49
  204.6 15.5 %collective-permute-start.36 = (bf16[864,256]{1,0:T(8,128)(2,1)S(1)}, bf16[864,256]{1,0:T(8,128)(2,1)S(1)}, u32[]{:S(2)}, u32[]{:S(2)}) collective-permute-start(bf16[864,256]{1,0:T(8,128)(2,1)S(1)} %fusion.refs_0_), channel_id=1, source_target_pairs={{0,8},{8,0},{16,24},{24,16},{1,9},{9,1},{17,25},{25,17},{2,10},{10... | collective-permute-start | bytes 1327112 | tf_op jit(solution)/shard_map/ppermute | solution.py:111
  209.1 20.3 %collective-permute-start.46 = (bf16[864,256]{1,0:T(8,128)(2,1)S(1)}, bf16[864,256]{1,0:T(8,128)(2,1)S(1)}, u32[]{:S(2)}, u32[]{:S(2)}) collective-permute-start(bf16[864,256]{1,0:T(8,128)(2,1)S(1)} %fusion.2.refs_2_), channel_id=1, source_target_pairs={{0,8},{8,0},{16,24},{24,16},{1,9},{9,1},{17,25},{25,17},{2,10},{10... | collective-permute-start | bytes 1327112 | tf_op jit(solution)/shard_map/ppermute | solution.py:111
  209.4 29.0 %collective-permute-start.41 = (bf16[864,256]{1,0:T(8,128)(2,1)S(1)}, bf16[864,256]{1,0:T(8,128)(2,1)S(1)}, u32[]{:S(2)}, u32[]{:S(2)}) collective-permute-start(bf16[864,256]{1,0:T(8,128)(2,1)S(1)} %fusion.1.refs_2_.refs_4_), channel_id=1, source_target_pairs={{0,8},{8,0},{16,24},{24,16},{1,9},{9,1},{17,25},{25,17},{2,10},{10... | collective-permute-start | bytes 1327112 | tf_op jit(solution)/shard_map/ppermute | solution.py:111
  220.2 18.4 %collective-permute-start.63 = (bf16[864,256]{1,0:T(8,128)(2,1)S(1)}, bf16[864,256]{1,0:T(8,128)(2,1)S(1)}, u32[]{:S(2)}, u32[]{:S(2)}) collective-permute-start(bf16[864,256]{1,0:T(8,128)(2,1)S(1)} %add_convert_fusion.7), channel_id=1, source_target_pairs={{8,16},{12,20},{16,8},{20,12},{0,4},{4,0},{24,28},{28,24},{9,17},{... | collective-permute-start | bytes 1327112 | tf_op jit(solution)/shard_map/ppermute | solution.py:115
  241.4 20.3 %collective-permute-start.48 = (bf16[864,256]{1,0:T(8,128)(2,1)S(1)}, bf16[864,256]{1,0:T(8,128)(2,1)S(1)}, u32[]{:S(2)}, u32[]{:S(2)}) collective-permute-start(bf16[864,256]{1,0:T(8,128)(2,1)S(1)} %fusion.3.refs_4_.refs_8_), channel_id=1, source_target_pairs={{0,8},{8,0},{16,24},{24,16},{1,9},{9,1},{17,25},{25,17},{2,10},{10... | collective-permute-start | bytes 1327112 | tf_op jit(solution)/shard_map/ppermute | solution.py:111
  242.7 27.7 %collective-permute-start.74 = (bf16[864,256]{1,0:T(8,128)(2,1)S(1)}, bf16[864,256]{1,0:T(8,128)(2,1)S(1)}, u32[]{:S(2)}, u32[]{:S(2)}) collective-permute-start(bf16[864,256]{1,0:T(8,128)(2,1)S(1)} %fusion.6.refs_10_), channel_id=1, source_target_pairs={{0,8},{8,0},{16,24},{24,16},{1,9},{9,1},{17,25},{25,17},{2,10},{10... | collective-permute-start | bytes 1327112 | tf_op jit(solution)/shard_map/ppermute | solution.py:111
  252.4 18.2 %collective-permute-start.65 = (bf16[864,256]{1,0:T(8,128)(2,1)S(1)}, bf16[864,256]{1,0:T(8,128)(2,1)S(1)}, u32[]{:S(2)}, u32[]{:S(2)}) collective-permute-start(bf16[864,256]{1,0:T(8,128)(2,1)S(1)} %add_convert_fusion.5), channel_id=1, source_target_pairs={{8,16},{12,20},{16,8},{20,12},{0,4},{4,0},{24,28},{28,24},{9,17},{... | collective-permute-start | bytes 1327112 | tf_op jit(solution)/shard_map/ppermute | solution.py:115
  273.3 20.3 %collective-permute-start.78 = (bf16[864,256]{1,0:T(8,128)(2,1)S(1)}, bf16[864,256]{1,0:T(8,128)(2,1)S(1)}, u32[]{:S(2)}, u32[]{:S(2)}) collective-permute-start(bf16[864,256]{1,0:T(8,128)(2,1)S(1)} %fusion.7.refs_14_), channel_id=1, source_target_pairs={{0,8},{8,0},{16,24},{24,16},{1,9},{9,1},{17,25},{25,17},{2,10},{10... | collective-permute-start | bytes 1327112 | tf_op jit(solution)/shard_map/ppermute | solution.py:111
  273.5 24.9 %collective-permute-start.80 = (bf16[512,256]{1,0:T(8,128)(2,1)S(1)}, bf16[512,256]{1,0:T(8,128)(2,1)S(1)}, u32[]{:S(2)}, u32[]{:S(2)}) collective-permute-start(bf16[512,256]{1,0:T(8,128)(2,1)S(1)} %fusion.8.refs_0_), channel_id=1, source_target_pairs={{0,8},{8,0},{16,24},{24,16},{1,9},{9,1},{17,25},{25,17},{2,10},{10... | collective-permute-start | bytes 786440 | tf_op jit(solution)/shard_map/ppermute | solution.py:111
  299.9 20.6 %collective-permute-start.84 = (bf16[512,256]{1,0:T(8,128)(2,1)S(1)}, bf16[512,256]{1,0:T(8,128)(2,1)S(1)}, u32[]{:S(2)}, u32[]{:S(2)}) collective-permute-start(bf16[512,256]{1,0:T(8,128)(2,1)S(1)} %add_convert_fusion.18.refs_2_), channel_id=1, source_target_pairs={{0,8},{8,0},{16,24},{24,16},{1,9},{9,1},{17,25},{25,17},{2,10},{10... | collective-permute-start | bytes 786440 | tf_op jit(solution)/shard_map/ppermute | solution.py:111
  304.5 16.1 %collective-permute-start.85 = (bf16[512,256]{1,0:T(8,128)(2,1)S(1)}, bf16[512,256]{1,0:T(8,128)(2,1)S(1)}, u32[]{:S(2)}, u32[]{:S(2)}) collective-permute-start(bf16[512,256]{1,0:T(8,128)(2,1)S(1)} %add_convert_fusion.16.refs_3_), channel_id=1, source_target_pairs={{0,8},{8,0},{16,24},{24,16},{1,9},{9,1},{17,25},{25,17},{2,10},{10... | collective-permute-start | bytes 786440 | tf_op jit(solution)/shard_map/ppermute | solution.py:111
  (161 other events, 1561.9 us)
